TPU v7x, 32 devices: a whole 2x2x4 slice. The times are simulated.
32 devices in a mesh: date: 2 (over x), strip: 16 (over z, y, core).
Axes of the slice: x: 2, y: 2, z: 4, core: 2. Of those that a mesh axis runs over, the one named last changes fastest.
Arguments:
- slc: bfloat16 [20, 2, 192, 1408], P('date', None, 'strip'), may hold values from -60 to 60
Outputs:
- coherence: float32 [20, 20, 2, 64, 128], P('date', None, None, 'strip')
All inputs are finite; a program needn't handle non-finite values.
Results may differ from a plain program's by a relative error of at most 0.0003.
Values may be sent and summed in bfloat16 or wider, within the bound.
No kernel may reach another device: no remote copies, remote signals or barrier semaphores. Data moves between devices by JAX's collectives and lax.ppermute only.
A program may use at most 128 MiB of HBM per device.

v0:
```python
import jax
import jax.numpy as jnp
from jax import lax
from jax.sharding import PartitionSpec as P

EPS = 1e-06


def with_halo(cells, sides, width):
    for axis, dim in sides:
        count = lax.axis_size(axis)
        ends = count - 1
        head = lax.slice_in_dim(cells, 0, width, axis=dim)
        tail = lax.slice_in_dim(cells, cells.shape[dim] - width, cells.shape[dim], axis=dim)
        cells = jnp.concatenate(
            [
                lax.ppermute(tail, axis, [(i, (i + 1) % count) for i in range(ends)]),
                cells,
                lax.ppermute(head, axis, [((i + 1) % count, i) for i in range(ends)]),
            ],
            axis=dim,
        )
    return cells


def cell_layout(block):
    shape = block.shape
    return block.reshape((shape[0], 2, shape[2] // 3, 3, shape[3] // 11, 11))


def boxcar(cells):
    padded = jnp.pad(cells, [(0, 0)] * (cells.ndim - 1) + [(1, 1)])
    tri = padded[..., :-2] + padded[..., 1:-1] + padded[..., 2:]
    return tri[..., :-2, :] + tri[..., 1:-1, :] + tri[..., 2:, :]


def amplitude(cells_bf):
    values = cells_bf.astype(jnp.float32)
    power = jnp.sum(values * values, axis=(1, 3, 5))
    return lax.rsqrt(boxcar(power) + EPS)


def pair_terms(own_cells, own_scale, other_cells, other_scale):
    sums = lax.dot_general(
        own_cells,
        other_cells,
        (((3, 5), (3, 5)), ((2, 4), (2, 4))),
        preferred_element_type=jnp.float32,
    )
    first = sums[:, :, :, 0, :, 0] + sums[:, :, :, 1, :, 1]
    second = sums[:, :, :, 1, :, 0] - sums[:, :, :, 0, :, 1]
    both = jnp.stack([first, second], axis=4)
    both = jnp.transpose(both, (2, 3, 4, 0, 1))
    return boxcar(both) * (own_scale[:, None] * other_scale[None])[:, :, None]


def per_device(slc):
    local_dates = slc.shape[0]
    whole = lax.all_gather(slc, "date", axis=0, tiled=True)
    padded = with_halo(whole, (("strip", 2),), 3)
    all_cells = cell_layout(padded)
    all_scale = amplitude(all_cells)
    first_date = lax.axis_index("date") * local_dates
    own_cells = lax.dynamic_slice_in_dim(all_cells, first_date, local_dates, 0)
    own_scale = lax.dynamic_slice_in_dim(all_scale, first_date, local_dates, 0)
    return pair_terms(own_cells, own_scale, all_cells, all_scale)


def solution(mesh):
    return jax.shard_map(
        per_device,
        mesh=mesh,
        in_specs=(P("date", None, "strip", None),),
        out_specs=P("date", None, None, "strip", None),
        check_vma=False,
    )
```

profile of v0, /device:TPU:5, one launch (start us, length us, event | category | flops | bytes accessed | tf_op | source)
XLA Modules:
  0.0 243.3 jit_solution(3144084779581970662)
XLA Ops:
  6.5 0.7 all-gather.2.cloned.1.call-update
  7.3 27.6 %all-gather.2.cloned.1.call-done = bf16[20,2,12,1408]{3,1,2,0:T(2,128)(2,1)} async-done(((bf16[10,2,12,1408]{3,1,2,0:T(2,128)(2,1)}), bf16[20,2,12,1408]{3,1,2,0:T(2,128)(2,1)}) %all-gather.2.cloned.1.call-update) | async-done | bytes 1351696 | tf_op jit(solution)/shard_map/all_gather | solution.py:59
  34.9 1.7 fusion.14
  36.5 3.7 %collective-permute-start = (bf16[20,2,3,1408]{3,1,2,0:T(2,128)(2,1)S(1)}, bf16[20,2,3,1408]{3,1,2,0:T(2,128)(2,1)S(1)}, u32[]{:S(2)}, u32[]{:S(2)}) collective-permute-start(bf16[20,2,3,1408]{3,1,2,0:T(2,128)(2,1)S(1)} %get-tuple-element.8), channel_id=1, source_target_pairs={{0,1},{1,2},{2,3},{3,4},{4,5},{5,6},{6,7},{7,8},{8,9},{9,10},{10,1... | collective-permute-start | bytes 1013768 | tf_op jit(solution)/shard_map/ppermute | solution.py:17
  40.2 1.9 collective-permute-start.1
  42.1 2.2 collective-permute-done
  44.5 1.1 constant_dynamic-update-slice_fusion.1
  45.6 4.0 %collective-permute-done.1 = bf16[20,2,3,1408]{3,1,2,0:T(2,128)(2,1)S(1)} collective-permute-done((bf16[20,2,3,1408]{3,1,2,0:T(2,128)(2,1)S(1)}, bf16[20,2,3,1408]{3,1,2,0:T(2,128)(2,1)S(1)}, u32[]{:S(2)}, u32[]{:S(2)}) %collective-permute-start.1) | collective-permute-done | bytes 337952 | tf_op jit(solution)/shard_map/ppermute | solution.py:19
  49.6 0.3 constant_dynamic-update-slice_fusion
  49.9 1.3 copy-done
  51.2 5.4 %multiply_reduce_fusion = f32[20,18,1408]{2,1,0:T(8,128)S(1)} fusion(bf16[20,2,18,1408]{3,1,2,0:T(2,128)(2,1)S(1)} %constant_dynamic-update-slice_fusion), kind=kLoop, calls=%fused_computation.8 | loop fusion | flops 2534400 | bytes 4055040 | tf_op jit(solution)/shard_map/reduce_sum | solution.py:39
  56.6 55.1 %reshape.43 = bf16[20,2,6,3,128,11]{5,4,1,3,2,0:T(8,128)(2,1)} reshape(bf16[20,2,18,1408]{3,1,2,0:T(2,128)(2,1)} %copy-done) | data formatting | bytes 4055040 | tf_op jit(solution)/shard_map/reshape | solution.py:28
  111.7 1.8 copy.15
  113.5 26.9 %reduce_sum.14 = f32[20,6,3,128,11]{4,3,0,2,1:T(8,128)} reshape(f32[20,18,1408]{2,0,1:T(8,128)} %copy.15) | data formatting | bytes 4055040 | tf_op jit(solution)/shard_map/reduce_sum | solution.py:39
  140.4 9.3 %reduce_sum.18 = f32[20,6,128]{2,0,1:T(8,128)S(1)} reduce(f32[20,6,3,128,11]{4,3,0,2,1:T(8,128)} %reduce_sum.14, f32[]{:T(128)} %constant.15.clone.1), dimensions={2,4}, to_apply=%region_1.2 | reduce | flops 491520 | bytes 2088964 | tf_op jit(solution)/shard_map/reduce_sum | solution.py:39
  149.9 11.3 %constant_dynamic-slice_fusion.1 = bf16[10,2,6,3,128,11]{5,4,1,3,2,0:T(8,128)(2,1)} fusion(bf16[20,2,6,3,128,11]{5,4,1,3,2,0:T(8,128)(2,1)} %reshape.43, s32[]{:T(128)S(6)} %select_n.4), kind=kLoop, calls=%fused_computation.30 | loop fusion | bytes 2027524 | tf_op jit(solution)/shard_map/dynamic_slice | solution.py:64
  161.2 45.5 %fusion.2 = f32[6,128,10,2,20,2]{4,2,5,3,1,0:T(8,128)} fusion(bf16[20,2,6,3,128,11,1]{5,4,1,3,2,0,6:T(8,128)(2,1)} %bitcast.21, bf16[10,2,6,3,128,11]{5,4,1,3,2,0:T(8,128)(2,1)} %constant_dynamic-slice_fusion.1), kind=kOutput, calls=%fused_computation.3 | convolution fusion | flops 40550400 | bytes 5498880 | tf_op jit(solution)/shard_map/dot_general | solution.py:44
  206.7 14.2 %fusion.6 = (f32[6,128,10,20,1]{3,2,1,0,4:T(8,128)}, f32[6,128,10,20,1]{3,2,1,0,4:T(8,128)}) fusion(f32[6,128,10,2,20,2]{4,2,5,3,1,0:T(8,128)} %fusion.2), kind=kLoop, calls=%fused_computation.7 | loop fusion | flops 307200 | bytes 3686400 | tf_op jit(solution)/shard_map/add | solution.py:50
  220.8 5.0 %copy.13 = f32[6,128,10,20,1]{1,4,3,2,0:T(1,128)S(1)} copy(f32[6,128,10,20,1]{3,2,1,0,4:T(8,128)} %get-tuple-element.5) | data formatting | bytes 1228800 | tf_op jit(solution)/shard_map/add | solution.py:50
  225.8 5.2 %copy.14 = f32[6,128,10,20,1]{1,4,3,2,0:T(1,128)S(1)} copy(f32[6,128,10,20,1]{3,2,1,0,4:T(8,128)} %get-tuple-element.6) | data formatting | bytes 1228800 | tf_op jit(solution)/shard_map/sub | solution.py:51
  231.0 1.1 maximum_bitcast_fusion
  232.1 2.6 %fusion.8 = f32[10,20,2,6,128]{4,2,1,0,3:T(2,128)S(1)} fusion(f32[10,20,2,6,128]{4,2,1,0,3:T(2,128)S(1)} %maximum_bitcast_fusion), kind=kLoop, calls=%fused_computation.12 | loop fusion | flops 614400 | bytes 2457600 | tf_op jit(solution)/shard_map/add | solution.py:33
  234.7 0.5 fusion.9
  235.3 1.2 copy.16
  (9 shorter events, 0.4 us)
Async XLA Ops:
  6.5 28.3 %all-gather.2.cloned.1.call-start = ((), (), s32[]{:S(2)}) async-start(), calls=%async_computation | async-start | bytes 2027520 | tf_op jit(solution)/shard_map/all_gather | solution.py:59
  34.9 9.7 %copy-start.1 = (bf16[20,2,12,1408]{3,1,2,0:T(2,128)(2,1)S(1)}, bf16[20,2,12,1408]{3,1,2,0:T(2,128)(2,1)}, u32[]{:S(2)}) copy-start(bf16[20,2,12,1408]{3,1,2,0:T(2,128)(2,1)} %all-gather.2.cloned.1.call-done) | copy-start | bytes 4055044
  36.5 7.8 %collective-permute-start = (bf16[20,2,3,1408]{3,1,2,0:T(2,128)(2,1)S(1)}, bf16[20,2,3,1408]{3,1,2,0:T(2,128)(2,1)S(1)}, u32[]{:S(2)}, u32[]{:S(2)}) collective-permute-start(bf16[20,2,3,1408]{3,1,2,0:T(2,128)(2,1)S(1)} %get-tuple-element.8), channel_id=1, source_target_pairs={{0,1},{1,2},{2,3},{3,4},{4,5},{5,6},{6,7},{7,8},{8,9},{9,10},{10,1... | collective-permute-start | bytes 1013768 | tf_op jit(solution)/shard_map/ppermute | solution.py:17
  40.2 9.4 %collective-permute-start.1 = (bf16[20,2,3,1408]{3,1,2,0:T(2,128)(2,1)S(1)}, bf16[20,2,3,1408]{3,1,2,0:T(2,128)(2,1)S(1)}, u32[]{:S(2)}, u32[]{:S(2)}) collective-permute-start(bf16[20,2,3,1408]{3,1,2,0:T(2,128)(2,1)S(1)} %get-tuple-element.7), channel_id=1, source_target_pairs={{1,0},{2,1},{3,2},{4,3},{5,4},{6,5},{7,6},{8,7},{9,8},{10,9},{11,1... | collective-permute-start | bytes 1013768 | tf_op jit(solution)/shard_map/ppermute | solution.py:19
  49.9 1.3 copy-start
Sparse Core Ops, SparseCore 0:
  8.9 25.9 all-gather.1
where the time goes:
time: 244 us; the launch traced here: 243 us
  local copies, waits for them, and re-layouts  111 us (45%)
  matrix products  45.5 us (19%)
  waiting for transfers between devices  34.5 us (14%)
  other arithmetic  33.2 us (14%)
  between operations  13.5 us (6%)
  starting transfers between devices  5.59 us (2%)
    reshape x1, local copies, waits for them, and re-layouts, cell_layout(): return block.reshape((shape[0], 2, shape[2] // 3, 3, shape[3] // 11, 11))  55.1 us
    dot_general x1, matrix products, pair_terms(): lax.dot_general(own_cells, other_cells, (((3, 5), (3, 5)), ((2, 4), (2, 4...  45.5 us
    reduce_sum x2, local copies, waits for them, and re-layouts, amplitude(): power = jnp.sum(values * values, axis=(1, 3, 5))  28.7 us
    all_gather x1, waiting for transfers between devices, per_device(): whole = lax.all_gather(slc, 'date', axis=0, tiled=True)  27.6 us
    reduce_sum x2, other arithmetic, amplitude(): power = jnp.sum(values * values, axis=(1, 3, 5))  14.7 us
    add x1, other arithmetic, pair_terms(): first = sums[:, :, :, 0, :, 0] + sums[:, :, :, 1, :, 1]  14.2 us
    dynamic_slice x1, local copies, waits for them, and re-layouts, per_device(): own_cells = lax.dynamic_slice_in_dim(all_cells, first_date, local_dates, 0)  11.3 us
    sub x1, local copies, waits for them, and re-layouts, pair_terms(): second = sums[:, :, :, 1, :, 0] - sums[:, :, :, 0, :, 1]  5.2 us
  transfers between devices with their start and end apart: 3, of which 3 were waited for; matrix products, arithmetic and copies ran while one was open for 1% of the time, Pallas kernels for 0%

commit v1 on v0

v1 whole, which is shorter than its diff:
```python
import functools

import jax
import jax.numpy as jnp
from jax import lax
from jax.experimental import pallas as pl
from jax.experimental.pallas import tpu as pltpu
from jax.sharding import PartitionSpec as P

EPS = 1e-06
LANES = 128
CELL = 11
STEPS = 33
VMEM = pltpu.MemorySpace.VMEM


def lane_tables():
    lane = lax.broadcasted_iota(jnp.int32, (8, LANES), 1)
    turn = lax.rem(lane * 3, CELL)
    bits = [(s, (turn & s) != 0) for s in (1, 2, 4, 8)]
    picks = [(lane * CELL + c) & (LANES - 1) for c in range(CELL)]
    return bits, picks


def unpack(dates, pieces, flat):
    def one(d, carry):
        for ref, src, dst in pieces:
            pair = ref[d, src].astype(jnp.float32)
            for m in range(CELL):
                flat[d, m, 2 * dst : 2 * dst + 2, :] = pair[:, m * LANES : (m + 1) * LANES]
        return carry

    lax.fori_loop(0, dates, one, 0)


def regroup(dates, flat, cells):
    bits, picks = lane_tables()

    def one(d, carry):
        for part in range(6):
            sub, ri = part // 2, part % 2
            v = [flat[d, m, pl.ds(part, 8, stride=6), :] for m in range(CELL)]
            for shift, mask in bits:
                v = [jnp.where(mask, v[(t + shift) % CELL], v[t]) for t in range(CELL)]
            for c in range(CELL):
                cells[d, ri, sub * CELL + c] = jnp.take_along_axis(
                    v[(8 * c) % CELL], picks[c], axis=1
                )
        return carry

    lax.fori_loop(0, dates, one, 0)


def box(first, second):
    sub = lax.broadcasted_iota(jnp.int32, (8, LANES), 0)
    lane = lax.broadcasted_iota(jnp.int32, (8, LANES), 1)
    first = first + pltpu.roll(first, 7, 0) + pltpu.roll(first, 6, 0)
    second = pltpu.roll(second, 4, 0) + pltpu.roll(second, 3, 0) + pltpu.roll(second, 2, 0)
    both = jnp.where(sub < 4, first, second)
    left = jnp.where(lane > 0, pltpu.roll(both, 1, 1), 0.0)
    right = jnp.where(lane < LANES - 1, pltpu.roll(both, LANES - 1, 1), 0.0)
    return both + left + right


def scales(dates, cells, out):
    def one(d, carry):
        def step(s, acc):
            re, im = cells[d, 0, s], cells[d, 1, s]
            return acc + re * re + im * im

        acc = lax.fori_loop(0, STEPS, step, jnp.zeros((8, LANES), jnp.float32), unroll=11)
        out[d] = lax.rsqrt(box(acc, acc) + EPS)
        return carry

    lax.fori_loop(0, dates, one, 0)


def products(rows, cols, row_cells, col_cells):
    count = len(rows) * len(cols)

    def step(s, acc):
        a = [row_cells[i, 0, s] for i in rows]
        b = [row_cells[i, 1, s] for i in rows]
        ab = [x + y for x, y in zip(a, b)]
        acc = list(acc)
        at = 0
        for j in cols:
            c, d = col_cells[j, 0, s], col_cells[j, 1, s]
            cd = c - d
            for i in range(len(rows)):
                acc[at] = acc[at] + a[i] * c
                acc[at + 1] = acc[at + 1] + b[i] * d
                acc[at + 2] = acc[at + 2] + ab[i] * cd
                at += 3
        return tuple(acc)

    zero = jnp.zeros((8, LANES), jnp.float32)
    acc = lax.fori_loop(0, STEPS, step, (zero,) * (3 * count), unroll=3)
    at = 0
    for j in cols:
        for i in rows:
            p, q, r = acc[at : at + 3]
            yield i, j, box(p + q, r - p + q)
            at += 3


def own_kernel(dates, x, up, dn, cells, scale, coh, flat):
    rows = x.shape[1]
    pieces = [(up, q, q) for q in range(3)]
    pieces += [(x, q, q + 3) for q in range(rows)]
    pieces += [(dn, q, q + 3 + rows) for q in range(3)]
    unpack(dates, pieces, flat)
    regroup(dates, flat, cells)
    scales(dates, cells, scale)
    sign = jnp.where(lax.broadcasted_iota(jnp.int32, (8, LANES), 0) < 4, 1.0, -1.0)
    half = dates // 2

    def one(n, carry):
        i = 2 * lax.div(n, 2)
        j0 = half * lax.rem(n, 2)

        @pl.when(i < j0 + half)
        def _():
            rows = [i, i + 1]
            cols = [j0 + t for t in range(half)]
            for a, b, both in products(rows, cols, cells, cells):
                both = both * (scale[a] * scale[b])
                coh[a, b] = both
                coh[b, a] = both * sign

        return carry

    lax.fori_loop(0, dates, one, 0)


def cross_kernel(dates, count, *refs):
    parts = refs[: 5 * (count - 1)]
    own, own_scale, own_coh, out, flat, cells, scale = refs[5 * (count - 1) :]
    me = lax.axis_index("date")
    first = me * dates

    def keep(i, carry):
        out[i, pl.ds(first, dates)] = own_coh[i]
        return carry

    lax.fori_loop(0, dates, keep, 0)
    half = dates // 2
    for t in range(1, count):
        head, tail, mid, up, dn = parts[5 * (t - 1) : 5 * t]
        pieces = [(up, q, q) for q in range(3)]
        pieces += [(head, q, q + 3) for q in range(3)]
        pieces += [(mid, q, q + 6) for q in range(mid.shape[1])]
        pieces += [(tail, q, q + 6 + mid.shape[1]) for q in range(3)]
        pieces += [(dn, q, q + 9 + mid.shape[1]) for q in range(3)]
        unpack(dates, pieces, flat)
        regroup(dates, flat, cells)
        scales(dates, cells, scale)
        base = lax.rem(me + count - t, count) * dates

        def one(n, carry):
            i = 2 * lax.div(n, 2)
            j0 = half * lax.rem(n, 2)
            rows = [i, i + 1]
            cols = [j0 + u for u in range(half)]
            for a, b, both in products(rows, cols, own, cells):
                out[a, base + b] = both * (own_scale[a] * scale[b])
            return carry

        lax.fori_loop(0, dates, one, 0)


def per_device(slc):
    dates, _, rows, width = slc.shape
    count = lax.axis_size("date")
    strips = lax.axis_size("strip")
    up_pairs = [(i, i + 1) for i in range(strips - 1)]
    dn_pairs = [(i + 1, i) for i in range(strips - 1)]
    x = jnp.transpose(slc, (0, 2, 1, 3))
    head, mid, tail = x[:, :3], x[:, 3 : rows - 3], x[:, rows - 3 :]
    parts = []
    for t in range(1, count):
        ring = [(i, (i + t) % count) for i in range(count)]
        h = lax.ppermute(head, "date", ring)
        l = lax.ppermute(tail, "date", ring)
        m = lax.ppermute(mid, "date", ring)
        u = lax.ppermute(l, "strip", up_pairs)
        d = lax.ppermute(h, "strip", dn_pairs)
        parts += [h, l, m, u, d]
    up = lax.ppermute(tail, "strip", up_pairs)
    dn = lax.ppermute(head, "strip", dn_pairs)
    f32 = jnp.float32
    vm = pl.BlockSpec(memory_space=VMEM)
    flat = pltpu.VMEM((dates, CELL, 48, LANES), f32)
    cells, scale, coh = pl.pallas_call(
        functools.partial(own_kernel, dates),
        out_shape=(
            jax.ShapeDtypeStruct((dates, 2, STEPS, 8, LANES), f32),
            jax.ShapeDtypeStruct((dates, 8, LANES), f32),
            jax.ShapeDtypeStruct((dates, dates, 8, LANES), f32),
        ),
        in_specs=[vm] * 3,
        out_specs=(vm,) * 3,
        scratch_shapes=[flat],
        compiler_params=pltpu.CompilerParams(vmem_limit_bytes=20 << 20),
        cost_estimate=pl.CostEstimate(flops=80_000_000, bytes_accessed=4_000_000, transcendentals=0),
        name="own_pairs",
    )(x, up, dn)
    out = pl.pallas_call(
        functools.partial(cross_kernel, dates, count),
        out_shape=jax.ShapeDtypeStruct((dates, dates * count, 8, LANES), f32),
        in_specs=[vm] * (len(parts) + 3),
        out_specs=vm,
        scratch_shapes=[
            flat,
            pltpu.VMEM((dates, 2, STEPS, 8, LANES), f32),
            pltpu.VMEM((dates, 8, LANES), f32),
        ],
        compiler_params=pltpu.CompilerParams(vmem_limit_bytes=48 << 20),
        cost_estimate=pl.CostEstimate(flops=150_000_000, bytes_accessed=5_000_000, transcendentals=0),
        name="cross_pairs",
    )(*parts, cells, scale, coh)
    return out.reshape(dates, dates * count, 2, 4, LANES)


def solution(mesh):
    return jax.shard_map(
        per_device,
        mesh=mesh,
        in_specs=(P("date", None, "strip", None),),
        out_specs=P("date", None, None, "strip", None),
        check_vma=False,
    )
```

time: 244 us -> 40 us (0.16)
  the two profiles are of different devices: /device:TPU:5 before, /device:TPU:8 now
where the time goes in v1:
time: 40 us; the launch traced here: 39.7 us
  Pallas kernels  19.5 us (49%)
  starting transfers between devices  16.6 us (42%)
  local copies, waits for them, and re-layouts  3.53 us (9%)
    pallas_call x1, Pallas kernels, per_device(): pl.pallas_call(functools.partial(cross_kernel, dates, count), out_shape=j...  10.7 us
    pallas_call x1, Pallas kernels, per_device(): pl.pallas_call(functools.partial(own_kernel, dates), out_shape=(jax.Shape...  8.79 us
    ppermute x1, starting transfers between devices, per_device(): dn = lax.ppermute(head, 'strip', dn_pairs)  4.54 us
    ppermute x1, starting transfers between devices, per_device(): d = lax.ppermute(h, 'strip', dn_pairs)  4.54 us
    slice x2, local copies, waits for them, and re-layouts, per_device(): head, mid, tail = (x[:, :3], x[:, 3:rows - 3], x[:, rows - 3:])  2.44 us
    ppermute x1, starting transfers between devices, per_device(): u = lax.ppermute(l, 'strip', up_pairs)  1.92 us
    ppermute x1, starting transfers between devices, per_device(): up = lax.ppermute(tail, 'strip', up_pairs)  1.91 us
    ppermute x1, starting transfers between devices, per_device(): l = lax.ppermute(tail, 'date', ring)  1.56 us
  transfers between devices with their start and end apart: 7, of which 0 were waited for; matrix products, arithmetic and copies ran while one was open for 3% of the time, Pallas kernels for 22%

profile of v1, /device:TPU:8, one launch (start us, length us, event | category | flops | bytes accessed | tf_op | source)
XLA Modules:
  0.0 39.7 jit_solution(673144554263258550)
XLA Ops:
  0.0 1.2 %fusion = (bf16[10,3,2,1408]{3,2,1,0:T(2,128)(2,1)S(1)}, bf16[10,3,2,1408]{3,2,1,0:T(2,128)(2,1)S(1)}) fusion(bf16[10,12,2,1408]{3,2,1,0:T(2,128)(2,1)} %bitcast.2), kind=kLoop, calls=%fused_computation | loop fusion | bytes 675840 | tf_op jit(solution)/shard_map/slice | solution.py:179
  1.2 1.6 %collective-permute-start.1 = (bf16[10,3,2,1408]{3,2,1,0:T(2,128)(2,1)S(1)}, bf16[10,3,2,1408]{3,2,1,0:T(2,128)(2,1)S(1)}, u32[]{:S(2)}, u32[]{:S(2)}) collective-permute-start(bf16[10,3,2,1408]{3,2,1,0:T(2,128)(2,1)S(1)} %get-tuple-element.11), channel_id=1, source_target_pairs={{0,16},{16,0},{1,17},{17,1},{2,18},{18,2},{3,19},{19,3},{4,20},{20... | collective-permute-start | bytes 506888 | tf_op jit(solution)/shard_map/ppermute | solution.py:184
  2.8 0.5 %collective-permute-start = (bf16[10,3,2,1408]{3,2,1,0:T(2,128)(2,1)S(1)}, bf16[10,3,2,1408]{3,2,1,0:T(2,128)(2,1)S(1)}, u32[]{:S(2)}, u32[]{:S(2)}) collective-permute-start(bf16[10,3,2,1408]{3,2,1,0:T(2,128)(2,1)S(1)} %get-tuple-element.12), channel_id=1, source_target_pairs={{0,16},{16,0},{1,17},{17,1},{2,18},{18,2},{3,19},{19,3},{4,20},{20... | collective-permute-start | bytes 506888 | tf_op jit(solution)/shard_map/ppermute | solution.py:183
  3.3 1.2 %slice.14 = bf16[10,6,2,1408]{3,2,1,0:T(2,128)(2,1)S(1)} slice(bf16[10,12,2,1408]{3,2,1,0:T(2,128)(2,1)} %bitcast.3), slice={[0:10], [3:9], [0:2], [0:1408]} | slice | bytes 675840 | tf_op jit(solution)/shard_map/slice | solution.py:179
  4.5 1.6 %collective-permute-start.2 = (bf16[10,6,2,1408]{3,2,1,0:T(2,128)(2,1)S(1)}, bf16[10,6,2,1408]{3,2,1,0:T(2,128)(2,1)S(1)}, u32[]{:S(2)}, u32[]{:S(2)}) collective-permute-start(bf16[10,6,2,1408]{3,2,1,0:T(2,128)(2,1)S(1)} %slice.14), channel_id=1, source_target_pairs={{0,16},{16,0},{1,17},{17,1},{2,18},{18,2},{3,19},{19,3},{4,20},{20... | collective-permute-start | bytes 1013768 | tf_op jit(solution)/shard_map/ppermute | solution.py:185
  6.1 1.9 %collective-permute-start.5 = (bf16[10,3,2,1408]{3,2,1,0:T(2,128)(2,1)S(1)}, bf16[10,3,2,1408]{3,2,1,0:T(2,128)(2,1)S(1)}, u32[]{:S(2)}, u32[]{:S(2)}) collective-permute-start(bf16[10,3,2,1408]{3,2,1,0:T(2,128)(2,1)S(1)} %get-tuple-element.11), channel_id=1, source_target_pairs={{0,1},{1,2},{2,3},{3,4},{4,5},{5,6},{6,7},{7,8},{8,9},{9,10},{10,1... | collective-permute-start | bytes 506888 | tf_op jit(solution)/shard_map/ppermute | solution.py:189
  8.0 4.5 %collective-permute-start.6 = (bf16[10,3,2,1408]{3,2,1,0:T(2,128)(2,1)S(1)}, bf16[10,3,2,1408]{3,2,1,0:T(2,128)(2,1)S(1)}, u32[]{:S(2)}, u32[]{:S(2)}) collective-permute-start(bf16[10,3,2,1408]{3,2,1,0:T(2,128)(2,1)S(1)} %get-tuple-element.12), channel_id=1, source_target_pairs={{1,0},{2,1},{3,2},{4,3},{5,4},{6,5},{7,6},{8,7},{9,8},{10,9},{11,1... | collective-permute-start | bytes 506888 | tf_op jit(solution)/shard_map/ppermute | solution.py:190
  12.6 0.0 collective-permute-done.1.refs_1_
  12.6 1.9 %collective-permute-start.3 = (bf16[10,3,2,1408]{3,2,1,0:T(2,128)(2,1)S(1)}, bf16[10,3,2,1408]{3,2,1,0:T(2,128)(2,1)S(1)}, u32[]{:S(2)}, u32[]{:S(2)}) collective-permute-start(bf16[10,3,2,1408]{3,2,1,0:T(2,128)(2,1)S(1)} %collective-permute-done.1.refs_1_), channel_id=1, source_target_pairs={{0,1},{1,2},{2,3},{3,4},{4,5},{5,6},{6,7},{7,8},{8,9},{9,10},{10,1... | collective-permute-start | bytes 506888 | tf_op jit(solution)/shard_map/ppermute | solution.py:186
  14.5 0.0 collective-permute-done.refs_0_
  14.5 4.5 %collective-permute-start.4 = (bf16[10,3,2,1408]{3,2,1,0:T(2,128)(2,1)S(1)}, bf16[10,3,2,1408]{3,2,1,0:T(2,128)(2,1)S(1)}, u32[]{:S(2)}, u32[]{:S(2)}) collective-permute-start(bf16[10,3,2,1408]{3,2,1,0:T(2,128)(2,1)S(1)} %collective-permute-done.refs_0_), channel_id=1, source_target_pairs={{1,0},{2,1},{3,2},{4,3},{5,4},{6,5},{7,6},{8,7},{9,8},{10,9},{11,1... | collective-permute-start | bytes 506888 | tf_op jit(solution)/shard_map/ppermute | solution.py:187
  19.1 0.0 collective-permute-done.5.up
  19.1 0.0 collective-permute-done.6.dn
  19.1 0.0 copy-start
  19.1 1.1 %copy-done = bf16[10,2,12,1408]{3,1,2,0:T(2,128)(2,1)S(1)} copy-done((bf16[10,2,12,1408]{3,1,2,0:T(2,128)(2,1)S(1)}, bf16[10,2,12,1408]{3,1,2,0:T(2,128)(2,1)}, u32[]{:S(2)}) %copy-start) | copy-done | bytes 675864
  20.2 8.8 %own_pairs.1 = (f32[10,2,33,8,128]{4,3,2,1,0:T(8,128)S(1)}, f32[10,8,128]{2,1,0:T(8,128)S(1)}, f32[10,10,8,128]{3,2,1,0:T(8,128)S(1)}) custom-call(bf16[10,12,2,1408]{3,2,1,0:T(2,128)(2,1)S(1)} %bitcast.4, bf16[10,3,2,1408]{3,2,1,0:T(2,128)(2,1)S(1)} %collective-permute-done.5.up, bf16[10,3,2,1408]{3,2,1,0:T(2,128)(2,1)S(1)} %collective-permute-done.6.dn), custom_call_target="tpu_custom_call" | custom-call | flops 80000000 | bytes 4000000 | tf_op jit(solution)/shard_map/own_pairs/pallas_call | solution.py:194
  29.0 0.0 collective-permute-done.3.refs_3_
  29.0 0.0 collective-permute-done.4.refs_4_
  29.0 0.0 collective-permute-done.2.refs_2_
  29.0 10.7 %cross_pairs.1 = f32[10,20,8,128]{3,2,1,0:T(8,128)} custom-call(bf16[10,3,2,1408]{3,2,1,0:T(2,128)(2,1)S(1)} %collective-permute-done.refs_0_, bf16[10,3,2,1408]{3,2,1,0:T(2,128)(2,1)S(1)} %collective-permute-done.1.refs_1_, bf16[10,6,2,1408]{3,2,1,0:T(2,128)(2,1)S(1)} %collective-permute-done.2.refs_2_, ...), custom_call_target="tpu_custom_call" | custom-call | flops 150000000 | bytes 5000000 | tf_op jit(solution)/shard_map/cross_pairs/pallas_call | solution.py:208
Async XLA Ops:
  1.2 11.3 %collective-permute-start.1 = (bf16[10,3,2,1408]{3,2,1,0:T(2,128)(2,1)S(1)}, bf16[10,3,2,1408]{3,2,1,0:T(2,128)(2,1)S(1)}, u32[]{:S(2)}, u32[]{:S(2)}) collective-permute-start(bf16[10,3,2,1408]{3,2,1,0:T(2,128)(2,1)S(1)} %get-tuple-element.11), channel_id=1, source_target_pairs={{0,16},{16,0},{1,17},{17,1},{2,18},{18,2},{3,19},{19,3},{4,20},{20... | collective-permute-start | bytes 506888 | tf_op jit(solution)/shard_map/ppermute | solution.py:184
  2.8 11.7 %collective-permute-start = (bf16[10,3,2,1408]{3,2,1,0:T(2,128)(2,1)S(1)}, bf16[10,3,2,1408]{3,2,1,0:T(2,128)(2,1)S(1)}, u32[]{:S(2)}, u32[]{:S(2)}) collective-permute-start(bf16[10,3,2,1408]{3,2,1,0:T(2,128)(2,1)S(1)} %get-tuple-element.12), channel_id=1, source_target_pairs={{0,16},{16,0},{1,17},{17,1},{2,18},{18,2},{3,19},{19,3},{4,20},{20... | collective-permute-start | bytes 506888 | tf_op jit(solution)/shard_map/ppermute | solution.py:183
  4.5 24.5 %collective-permute-start.2 = (bf16[10,6,2,1408]{3,2,1,0:T(2,128)(2,1)S(1)}, bf16[10,6,2,1408]{3,2,1,0:T(2,128)(2,1)S(1)}, u32[]{:S(2)}, u32[]{:S(2)}) collective-permute-start(bf16[10,6,2,1408]{3,2,1,0:T(2,128)(2,1)S(1)} %slice.14), channel_id=1, source_target_pairs={{0,16},{16,0},{1,17},{17,1},{2,18},{18,2},{3,19},{19,3},{4,20},{20... | collective-permute-start | bytes 1013768 | tf_op jit(solution)/shard_map/ppermute | solution.py:185
  6.1 13.0 %collective-permute-start.5 = (bf16[10,3,2,1408]{3,2,1,0:T(2,128)(2,1)S(1)}, bf16[10,3,2,1408]{3,2,1,0:T(2,128)(2,1)S(1)}, u32[]{:S(2)}, u32[]{:S(2)}) collective-permute-start(bf16[10,3,2,1408]{3,2,1,0:T(2,128)(2,1)S(1)} %get-tuple-element.11), channel_id=1, source_target_pairs={{0,1},{1,2},{2,3},{3,4},{4,5},{5,6},{6,7},{7,8},{8,9},{9,10},{10,1... | collective-permute-start | bytes 506888 | tf_op jit(solution)/shard_map/ppermute | solution.py:189
  8.0 11.1 %collective-permute-start.6 = (bf16[10,3,2,1408]{3,2,1,0:T(2,128)(2,1)S(1)}, bf16[10,3,2,1408]{3,2,1,0:T(2,128)(2,1)S(1)}, u32[]{:S(2)}, u32[]{:S(2)}) collective-permute-start(bf16[10,3,2,1408]{3,2,1,0:T(2,128)(2,1)S(1)} %get-tuple-element.12), channel_id=1, source_target_pairs={{1,0},{2,1},{3,2},{4,3},{5,4},{6,5},{7,6},{8,7},{9,8},{10,9},{11,1... | collective-permute-start | bytes 506888 | tf_op jit(solution)/shard_map/ppermute | solution.py:190
  12.6 16.4 %collective-permute-start.3 = (bf16[10,3,2,1408]{3,2,1,0:T(2,128)(2,1)S(1)}, bf16[10,3,2,1408]{3,2,1,0:T(2,128)(2,1)S(1)}, u32[]{:S(2)}, u32[]{:S(2)}) collective-permute-start(bf16[10,3,2,1408]{3,2,1,0:T(2,128)(2,1)S(1)} %collective-permute-done.1.refs_1_), channel_id=1, source_target_pairs={{0,1},{1,2},{2,3},{3,4},{4,5},{5,6},{6,7},{7,8},{8,9},{9,10},{10,1... | collective-permute-start | bytes 506888 | tf_op jit(solution)/shard_map/ppermute | solution.py:186
  14.5 14.5 %collective-permute-start.4 = (bf16[10,3,2,1408]{3,2,1,0:T(2,128)(2,1)S(1)}, bf16[10,3,2,1408]{3,2,1,0:T(2,128)(2,1)S(1)}, u32[]{:S(2)}, u32[]{:S(2)}) collective-permute-start(bf16[10,3,2,1408]{3,2,1,0:T(2,128)(2,1)S(1)} %collective-permute-done.refs_0_), channel_id=1, source_target_pairs={{1,0},{2,1},{3,2},{4,3},{5,4},{6,5},{7,6},{8,7},{9,8},{10,9},{11,1... | collective-permute-start | bytes 506888 | tf_op jit(solution)/shard_map/ppermute | solution.py:187
  19.1 1.1 %copy-start = (bf16[10,2,12,1408]{3,1,2,0:T(2,128)(2,1)S(1)}, bf16[10,2,12,1408]{3,1,2,0:T(2,128)(2,1)}, u32[]{:S(2)}) copy-start(bf16[10,2,12,1408]{3,1,2,0:T(2,128)(2,1)} %param.1) | copy-start | bytes 2027524

commit v2 on v0

v2 whole, which is shorter than its diff:
```python
import functools

import jax
import jax.numpy as jnp
from jax import lax
from jax.experimental import pallas as pl
from jax.experimental.pallas import tpu as pltpu
from jax.sharding import PartitionSpec as P

EPS = 1e-06
LANES = 128
CELL = 11
STEPS = 33
TILE = (8, LANES)
F32 = jnp.float32
VMEM = pltpu.MemorySpace.VMEM


def iota(dim):
    return lax.broadcasted_iota(jnp.int32, TILE, dim)


def put_rows(ref, date, row, flat, q, at):
    pair = ref[date, row].astype(F32)
    for m in range(CELL):
        flat[q, m, at : at + 2, :] = pair[:, m * LANES : (m + 1) * LANES]


def unpack_outer(dates, refs, flat):
    def one(q, carry):
        for half in range(2):
            for e, ref in enumerate(refs):
                for sub in range(3):
                    put_rows(ref, 2 * q + half, sub, flat, q, half * 24 + e * 6 + sub * 2)
        return carry

    lax.fori_loop(0, dates // 2, one, 0)


def unpack_inner(dates, mid, flat, first):
    def one(q, carry):
        for part in range(4):
            date = jnp.minimum(4 * q + part, dates - 1)
            for row in range(6):
                put_rows(mid, date, row, flat, first + q, part * 12 + row * 2)
        return carry

    lax.fori_loop(0, (dates + 3) // 4, one, 0)


def rotate(first, count, flat, cells):
    lane = iota(1)
    turn = lax.rem(lane * 3, CELL)
    bits = [(s, (turn & s) != 0) for s in (1, 2, 4, 8)]

    def one(q, carry):
        for part in range(6):
            v = [flat[q, m, pl.ds(part, 8, stride=6), :] for m in range(CELL)]
            for shift, mask in bits:
                v = [jnp.where(mask, v[(t + shift) % CELL], v[t]) for t in range(CELL)]
            for c in range(CELL):
                cells[q, part % 2, (part // 2) * CELL + c] = v[(8 * c) % CELL]
        return carry

    lax.fori_loop(first, first + count, one, 0)


def place(first, count, cells, spread=None):
    lane = iota(1)
    for c in range(CELL):
        pick = (lane * CELL + c) & (LANES - 1)

        def one(q, carry):
            for ri in range(2):
                for sub in range(3):
                    s = sub * CELL + c
                    v = jnp.take_along_axis(cells[q, ri, s], pick, axis=1)
                    cells[q, ri, s] = v
                    if spread is not None:
                        spread(q, ri, s, v)
            return carry

        lax.fori_loop(first, first + count, one, 0, unroll=count)


def spread_outer(rep):
    low = iota(0) < 4

    def put(q, ri, s, v):
        w = pltpu.roll(v, 4, 0)
        rep[2 * q, ri, s] = jnp.where(low, v, w)
        rep[2 * q + 1, ri, s] = jnp.where(low, w, v)

    return put


def spread_inner(rep, first):
    low = iota(0) < 4
    even = (iota(0) & 2) == 0

    def put(q, ri, s, v):
        a = jnp.where(even, v, pltpu.roll(v, 2, 0))
        b = jnp.where(even, pltpu.roll(v, 6, 0), v)
        c, d = pltpu.roll(a, 4, 0), pltpu.roll(b, 4, 0)
        at = 4 * (q - first)
        rep[at, ri, s] = jnp.where(low, a, c)
        rep[at + 1, ri, s] = jnp.where(low, b, d)
        rep[at + 2, ri, s] = jnp.where(low, c, a)
        rep[at + 3, ri, s] = jnp.where(low, d, b)

    return put


def products(rows, cols, rep, cells):
    count = len(rows) * len(cols)

    def step(s, acc):
        a = [rep[i, 0, s] for i in rows]
        b = [rep[i, 1, s] for i in rows]
        ab = [x + y for x, y in zip(a, b)]
        acc = list(acc)
        at = 0
        for q in cols:
            c, d = cells[q, 0, s], cells[q, 1, s]
            cd = c - d
            for i in range(len(rows)):
                acc[at] = acc[at] + a[i] * c
                acc[at + 1] = acc[at + 1] + b[i] * d
                acc[at + 2] = acc[at + 2] + ab[i] * cd
                at += 3
        return tuple(acc)

    acc = lax.fori_loop(0, STEPS, step, (jnp.zeros(TILE, F32),) * (3 * count), unroll=11)
    at = 0
    for j in range(len(cols)):
        for i in range(len(rows)):
            p, q, r = acc[at : at + 3]
            yield i, j, p + q, r - p + q
            at += 3


def powers(qs, cells):
    def step(s, acc):
        out = []
        for n, q in enumerate(qs):
            c, d = cells[q, 0, s], cells[q, 1, s]
            out.append(acc[n] + c * c + d * d)
        return tuple(out)

    return lax.fori_loop(0, STEPS, step, (jnp.zeros(TILE, F32),) * len(qs), unroll=11)


def put_outer(outer, group, at, first, second):
    low = iota(0) < 4
    pieces = (
        jnp.where(low, first, pltpu.roll(second, 4, 0)),
        jnp.where(low, pltpu.roll(first, 4, 0), second),
    )
    for n, piece in enumerate(pieces):
        p = at + n
        outer[group + p // 4, 8 * (p % 4) : 8 * (p % 4) + 8, :] = piece


def put_inner(inner, group, at, first, second, dates):
    sub = iota(0)

    def merge(x, y, z, w):
        return jnp.where(sub < 4, jnp.where(sub < 2, x, y), jnp.where(sub < 6, z, w))

    roll = pltpu.roll
    pieces = [merge(first, roll(second, 2, 0), roll(first, 2, 0), roll(second, 4, 0))]
    if dates > 2:
        pieces.append(merge(roll(first, 4, 0), roll(second, 6, 0), roll(first, 6, 0), second))
    for n, piece in enumerate(pieces):
        p = at + 2 * n
        inner[group + p // 4, 4 * (p % 4) : 4 * (p % 4) + 8, :] = piece


def window(first, count, outer, inner, sums):
    lane = iota(1)
    left, right = lane > 0, lane < LANES - 1

    def one(g, carry):
        e = [outer[g, pl.ds(x, 8, stride=4), :] for x in range(4)]
        m = [inner[g, pl.ds(x, 8, stride=2), :] for x in range(2)]
        t, u = e[1] + m[0], m[1] + e[2]
        for r, v in enumerate((e[0] + t, t + m[1], m[0] + u, u + e[3])):
            v = (
                v
                + jnp.where(left, pltpu.roll(v, 1, 1), 0.0)
                + jnp.where(right, pltpu.roll(v, LANES - 1, 1), 0.0)
            )
            sums[g, pl.ds(r, 8, stride=4), :] = v
        return carry

    lax.fori_loop(first, first + count, one, 0, unroll=4)


def sum_at(sums, group, p):
    return sums[group + p // 4, 8 * (p % 4) : 8 * (p % 4) + 8, :]


def inner_chunks(dates):
    return [(q, min(4, dates - 4 * q)) for q in range((dates + 3) // 4)]


def inside_kernel(dates, mid, cells, rep, flat):
    ins = (dates + 3) // 4
    unpack_inner(dates, mid, flat, 0)
    rotate(0, ins, flat, cells)
    place(0, ins, cells, spread_inner(rep, 0))


def outside_kernel(dates, head, tail, up, dn, cells, rep, flat):
    outs = dates // 2
    unpack_outer(dates, (up, head, tail, dn), flat)
    rotate(0, outs, flat, cells)
    place(0, outs, cells, spread_outer(rep))


def own_kernel(
    dates, cells_outer, cells_inner, rep_outer, rep_inner, scale, coh, outer, inner, sums
):
    outs = dates // 2
    groups = dates // 2
    sign = jnp.where(iota(0) < 4, 1.0, -1.0)
    for n, pw in enumerate(powers(range(outs), cells_outer)):
        put_outer(outer, outs * groups, 2 * n, pw, pw)
    chunks = inner_chunks(dates)
    for (q, size), pw in zip(chunks, powers([q for q, _ in chunks], cells_inner)):
        put_inner(inner, outs * groups, 4 * q, pw, pw, size)
    for b in range(outs):
        rows = [2 * b, 2 * b + 1]
        cols = list(range(b, outs))
        for i, j, re, im in products(rows, cols, rep_outer, cells_outer):
            put_outer(outer, groups * b, dates * i + 2 * cols[j], re, im)
        picks = [c for c in chunks if 4 * c[0] + c[1] > 2 * b]
        for i, j, re, im in products(rows, [q for q, _ in picks], rep_inner, cells_inner):
            put_inner(inner, groups * b, dates * i + 4 * picks[j][0], re, im, picks[j][1])
    window(0, outs * groups + (dates + 3) // 4, outer, inner, sums)
    for j in range(dates):
        scale[j] = lax.rsqrt(sum_at(sums, outs * groups, j) + EPS)

    for b in range(outs):
        for i in range(2):
            for j in range(2 * b + i, dates):
                v = sum_at(sums, groups * b, dates * i + j) * (scale[2 * b + i] * scale[j])
                coh[2 * b + i, j] = v
                if j != 2 * b + i:
                    coh[j, 2 * b + i] = v * sign


def outer_kernel(dates, rep_outer, head, tail, up, dn, outer, flat, cells):
    outs = dates // 2
    groups = dates // 2
    unpack_outer(dates, (up, head, tail, dn), flat)
    rotate(0, outs, flat, cells)
    place(0, outs, cells)
    for n, pw in enumerate(powers(range(outs), cells)):
        put_outer(outer, outs * groups, 2 * n, pw, pw)

    def one(b, carry):
        rows = [2 * b, 2 * b + 1]
        for i, j, re, im in products(rows, range(outs), rep_outer, cells):
            put_outer(outer, groups * b, dates * i + 2 * j, re, im)
        return carry

    lax.fori_loop(0, outs, one, 0)


def inner_kernel(dates, count, turn, rep_inner, own_scale, mid, outer, before, out, flat, cells, inner, sums):
    outs = dates // 2
    groups = dates // 2
    chunks = inner_chunks(dates)
    me = lax.axis_index("date")
    unpack_inner(dates, mid, flat, 0)
    rotate(0, len(chunks), flat, cells)
    place(0, len(chunks), cells)
    for (q, size), pw in zip(chunks, powers([q for q, _ in chunks], cells)):
        put_inner(inner, outs * groups, 4 * q, pw, pw, size)

    def one(b, carry):
        rows = [2 * b, 2 * b + 1]
        for i, j, re, im in products(rows, range(len(chunks)), rep_inner, cells):
            put_inner(inner, groups * b, dates * i + 4 * j, re, im, chunks[j][1])
        return carry

    lax.fori_loop(0, outs, one, 0)
    window(0, outs * groups + (dates + 3) // 4, outer, inner, sums)
    base = lax.rem(me + count - turn, count) * dates
    scale = [lax.rsqrt(sum_at(sums, outs * groups, j) + EPS) for j in range(dates)]

    def finish(b, carry):
        for i in range(2):
            mine = own_scale[2 * b + i]
            for j in range(dates):
                v = sum_at(sums, groups * b, dates * i + j)
                out[2 * b + i, base + j] = v * (mine * scale[j])
        return carry

    lax.fori_loop(0, outs, finish, 0)
    if turn == 1:

        def keep(i, carry):
            out[i, pl.ds(me * dates, dates)] = before[i]
            return carry

    else:

        def keep(i, carry):
            for t in [0] + list(range(1, turn)):
                at = lax.rem(me + count - t, count) * dates
                out[i, pl.ds(at, dates)] = before[i, pl.ds(at, dates)]
            return carry

    lax.fori_loop(0, dates, keep, 0)


def call(kernel, name, args, outs, scratch=(), flops=0, limit=32):
    vm = pl.BlockSpec(memory_space=VMEM)
    size = sum(a.size * a.dtype.itemsize for a in (*args, *outs))
    return pl.pallas_call(
        kernel,
        out_shape=tuple(outs),
        in_specs=[vm] * len(args),
        out_specs=(vm,) * len(outs),
        scratch_shapes=list(scratch),
        compiler_params=pltpu.CompilerParams(vmem_limit_bytes=limit << 20),
        cost_estimate=pl.CostEstimate(flops=flops, bytes_accessed=size, transcendentals=0),
        name=name,
    )(*args)


def per_device(slc):
    dates, _, rows, width = slc.shape
    count = lax.axis_size("date")
    strips = lax.axis_size("strip")
    up_pairs = [(i, i + 1) for i in range(strips - 1)]
    dn_pairs = [(i + 1, i) for i in range(strips - 1)]
    outs, ins = dates // 2, (dates + 3) // 4
    total = outs * outs + (dates + 3) // 4
    shape = jax.ShapeDtypeStruct

    x = jnp.transpose(slc, (0, 2, 1, 3))
    head, tail, mid = x[:, :3], x[:, rows - 3 :], x[:, 3 : rows - 3]
    heads, tails, mids = [], [], []
    for t in range(1, count):
        ring = [(i, (i + t) % count) for i in range(count)]
        heads.append(lax.ppermute(head, "date", ring))
        tails.append(lax.ppermute(tail, "date", ring))
        mids.append(lax.ppermute(mid, "date", ring))
    up = lax.ppermute(tail, "strip", up_pairs)
    dn = lax.ppermute(head, "strip", dn_pairs)

    def flat(q):
        return pltpu.VMEM((q, CELL, 48, LANES), F32)

    def cell(q):
        return (q, 2, STEPS, *TILE)

    cells_inner, rep_inner = call(
        functools.partial(inside_kernel, dates),
        "inside",
        (mid,),
        (shape(cell(ins), F32), shape(cell(4 * ins), F32)),
        [flat(ins)],
        flops=3_000_000,
    )
    heads, tails, cells_inner = lax.optimization_barrier((heads, tails, cells_inner))
    cells_outer, rep_outer = call(
        functools.partial(outside_kernel, dates),
        "outside",
        (head, tail, up, dn),
        (shape(cell(outs), F32), shape(cell(2 * outs), F32)),
        [flat(outs)],
        flops=3_000_000,
    )
    ups = [lax.ppermute(v, "strip", up_pairs) for v in tails]
    dns = [lax.ppermute(v, "strip", dn_pairs) for v in heads]
    pads = [pltpu.VMEM((total, r, LANES), F32) for r in (32, 16, 32)]
    scale, out = call(
        functools.partial(own_kernel, dates),
        "own_pairs",
        (cells_outer, cells_inner, rep_outer, rep_inner),
        (shape((dates, *TILE), F32), shape((dates, dates, *TILE), F32)),
        pads,
        flops=15_000_000,
    )
    for t in range(1, count):
        (outer,) = call(
            functools.partial(outer_kernel, dates),
            "outer_pairs",
            (rep_outer, heads[t - 1], tails[t - 1], ups[t - 1], dns[t - 1]),
            (shape((total, 32, LANES), F32),),
            [flat(outs), pltpu.VMEM(cell(outs), F32)],
            flops=15_000_000,
        )
        (out,) = call(
            functools.partial(inner_kernel, dates, count, t),
            "inner_pairs",
            (rep_inner, scale, mids[t - 1], outer, out),
            (shape((dates, dates * count, *TILE), F32),),
            [flat(ins), pltpu.VMEM(cell(ins), F32)] + pads[1:],
            flops=15_000_000,
        )
    return out.reshape(dates, dates * count, 2, 4, LANES)


def solution(mesh):
    return jax.shard_map(
        per_device,
        mesh=mesh,
        in_specs=(P("date", None, "strip", None),),
        out_specs=P("date", None, None, "strip", None),
        check_vma=False,
    )
```

time: 244 us -> 29.5 us (0.12)
  local copies, waits for them, and re-layouts: 111 us -> 2.44 us
  matrix products: 45.5 us -> 0 us
  waiting for transfers between devices: 34.5 us -> 0.02 us
  other arithmetic: 33.2 us -> 0 us
  between operations: 13.5 us -> 0.12 us
  Pallas kernels: 0 us -> 10.9 us
  starting transfers between devices: 5.59 us -> 15.7 us
    reshape x1 -> x0, local copies, waits for them, and re-layouts: 55.1 us -> none  [cell_layout(): return block.reshape((shape[0], 2, shape[2] // 3, 3, shape[3] // 11, 11))]
    dot_general x1 -> x0, matrix products: 45.5 us -> none  [pair_terms(): lax.dot_general(own_cells, other_cells, (((3, 5), (3, 5)), ((2, 4), (2, 4...]
    reduce_sum x2 -> x0, local copies, waits for them, and re-layouts: 28.7 us -> none  [amplitude(): power = jnp.sum(values * values, axis=(1, 3, 5))]
    all_gather x1 -> x0, waiting for transfers between devices: 27.6 us -> none  [per_device(): whole = lax.all_gather(slc, 'date', axis=0, tiled=True)]
    add x3 -> x0, other arithmetic: 16.9 us -> none  [the longest x1 14.2 us: pair_terms(): first = sums[:, :, :, 0, :, 0] + sums[:, :, :, 1, :, 1]]
    reduce_sum x2 -> x0, other arithmetic: 14.7 us -> none  [amplitude(): power = jnp.sum(values * values, axis=(1, 3, 5))]
    dynamic_slice x2 -> x0, local copies, waits for them, and re-layouts: 11.3 us -> none  [the longest x1 11.3 us: per_device(): own_cells = lax.dynamic_slice_in_dim(all_cells, first_date, local_dates, 0)]
    pallas_call x0 -> x5, Pallas kernels: none -> 10.9 us  [call(): pl.pallas_call(kernel, out_shape=tuple(outs), in_specs=[vm] * len(args),...]
  transfers between devices with their start and end apart: 3 -> 7, of which waited for: 3 -> 0; matrix products, arithmetic and copies ran while one was open for 1% -> 4% of each run, Pallas kernels for 0% -> 25%
where the time goes in v2:
time: 29.5 us; the launch traced here: 29.3 us
  starting transfers between devices  15.7 us (53%)
  Pallas kernels  10.9 us (37%)
  local copies, waits for them, and re-layouts  2.44 us (8%)
    pallas_call x5, Pallas kernels, call(): pl.pallas_call(kernel, out_shape=tuple(outs), in_specs=[vm] * len(args),...  10.9 us
    ppermute x1, starting transfers between devices, per_device(): up = lax.ppermute(tail, 'strip', up_pairs)  4.54 us
    ppermute x1, starting transfers between devices, per_device(): ups = [lax.ppermute(v, 'strip', up_pairs) for v in tails]  3.94 us
    ppermute x1, starting transfers between devices, per_device(): dns = [lax.ppermute(v, 'strip', dn_pairs) for v in heads]  2.52 us
    slice x2, local copies, waits for them, and re-layouts, per_device(): head, tail, mid = (x[:, :3], x[:, rows - 3:], x[:, 3:rows - 3])  2.44 us
    ppermute x1, starting transfers between devices, per_device(): dn = lax.ppermute(head, 'strip', dn_pairs)  1.92 us
    ppermute x1, starting transfers between devices, per_device(): tails.append(lax.ppermute(tail, 'date', ring))  1.28 us
    ppermute x1, starting transfers between devices, per_device(): mids.append(lax.ppermute(mid, 'date', ring))  1.28 us
  transfers between devices with their start and end apart: 7, of which 0 were waited for; matrix products, arithmetic and copies ran while one was open for 4% of the time, Pallas kernels for 25%

profile of v2, /device:TPU:5, one launch (start us, length us, event | category | flops | bytes accessed | tf_op | source)
XLA Modules:
  0.0 29.3 jit_solution(9563858112913329219)
XLA Ops:
  0.0 1.2 %fusion = (bf16[10,3,2,1408]{3,2,1,0:T(2,128)(2,1)S(1)}, bf16[10,3,2,1408]{3,2,1,0:T(2,128)(2,1)S(1)}) fusion(bf16[10,12,2,1408]{3,2,1,0:T(2,128)(2,1)} %bitcast.2), kind=kLoop, calls=%fused_computation | loop fusion | bytes 675840 | tf_op jit(solution)/shard_map/slice | solution.py:345
  1.2 1.3 %collective-permute-start.3 = (bf16[10,3,2,1408]{3,2,1,0:T(2,128)(2,1)S(1)}, bf16[10,3,2,1408]{3,2,1,0:T(2,128)(2,1)S(1)}, u32[]{:S(2)}, u32[]{:S(2)}) collective-permute-start(bf16[10,3,2,1408]{3,2,1,0:T(2,128)(2,1)S(1)} %get-tuple-element.23.tail), channel_id=1, source_target_pairs={{0,16},{16,0},{1,17},{17,1},{2,18},{18,2},{3,19},{19,3},{4,20},{20... | collective-permute-start | bytes 506888 | tf_op jit(solution)/shard_map/ppermute | solution.py:350
  2.5 0.3 collective-permute-start.2
  2.8 1.2 %slice.12.mid = bf16[10,6,2,1408]{3,2,1,0:T(2,128)(2,1)S(1)} slice(bf16[10,12,2,1408]{3,2,1,0:T(2,128)(2,1)} %bitcast.3), slice={[0:10], [3:9], [0:2], [0:1408]} | slice | bytes 675840 | tf_op jit(solution)/shard_map/slice | solution.py:345
  4.0 1.3 %collective-permute-start.4 = (bf16[10,6,2,1408]{3,2,1,0:T(2,128)(2,1)S(1)}, bf16[10,6,2,1408]{3,2,1,0:T(2,128)(2,1)S(1)}, u32[]{:S(2)}, u32[]{:S(2)}) collective-permute-start(bf16[10,6,2,1408]{3,2,1,0:T(2,128)(2,1)S(1)} %slice.12.mid), channel_id=1, source_target_pairs={{0,16},{16,0},{1,17},{17,1},{2,18},{18,2},{3,19},{19,3},{4,20},{20... | collective-permute-start | bytes 1013768 | tf_op jit(solution)/shard_map/ppermute | solution.py:351
  5.3 4.5 %collective-permute-start = (bf16[10,3,2,1408]{3,2,1,0:T(2,128)(2,1)S(1)}, bf16[10,3,2,1408]{3,2,1,0:T(2,128)(2,1)S(1)}, u32[]{:S(2)}, u32[]{:S(2)}) collective-permute-start(bf16[10,3,2,1408]{3,2,1,0:T(2,128)(2,1)S(1)} %get-tuple-element.23.tail), channel_id=1, source_target_pairs={{0,1},{1,2},{2,3},{3,4},{4,5},{5,6},{6,7},{7,8},{8,9},{9,10},{10,1... | collective-permute-start | bytes 506888 | tf_op jit(solution)/shard_map/ppermute | solution.py:352
  9.8 1.9 %collective-permute-start.1 = (bf16[10,3,2,1408]{3,2,1,0:T(2,128)(2,1)S(1)}, bf16[10,3,2,1408]{3,2,1,0:T(2,128)(2,1)S(1)}, u32[]{:S(2)}, u32[]{:S(2)}) collective-permute-start(bf16[10,3,2,1408]{3,2,1,0:T(2,128)(2,1)S(1)} %get-tuple-element.24.head), channel_id=1, source_target_pairs={{1,0},{2,1},{3,2},{4,3},{5,4},{6,5},{7,6},{8,7},{9,8},{10,9},{11,1... | collective-permute-start | bytes 506888 | tf_op jit(solution)/shard_map/ppermute | solution.py:353
  11.7 0.7 %inside.1 = (f32[3,2,33,8,128]{4,3,2,1,0:T(8,128)S(1)}, f32[12,2,33,8,128]{4,3,2,1,0:T(8,128)S(1)}) custom-call(bf16[10,6,2,1408]{3,2,1,0:T(2,128)(2,1)S(1)} %slice.12.mid), custom_call_target="tpu_custom_call" | custom-call | flops 3000000 | bytes 4392960 | tf_op jit(solution)/shard_map/inside/pallas_call | solution.py:322
  12.4 0.0 collective-permute-done.3.tail
  12.5 0.0 collective-permute-done.2.head
  12.5 2.5 %collective-permute-start.6 = (bf16[10,3,2,1408]{3,2,1,0:T(2,128)(2,1)S(1)}, bf16[10,3,2,1408]{3,2,1,0:T(2,128)(2,1)S(1)}, u32[]{:S(2)}, u32[]{:S(2)}) collective-permute-start(bf16[10,3,2,1408]{3,2,1,0:T(2,128)(2,1)S(1)} %collective-permute-done.2.head), channel_id=1, source_target_pairs={{1,0},{2,1},{3,2},{4,3},{5,4},{6,5},{7,6},{8,7},{9,8},{10,9},{11,1... | collective-permute-start | bytes 506888 | tf_op jit(solution)/shard_map/ppermute | solution.py:379
  15.0 3.9 %collective-permute-start.5 = (bf16[10,3,2,1408]{3,2,1,0:T(2,128)(2,1)S(1)}, bf16[10,3,2,1408]{3,2,1,0:T(2,128)(2,1)S(1)}, u32[]{:S(2)}, u32[]{:S(2)}) collective-permute-start(bf16[10,3,2,1408]{3,2,1,0:T(2,128)(2,1)S(1)} %collective-permute-done.3.tail), channel_id=1, source_target_pairs={{0,1},{1,2},{2,3},{3,4},{4,5},{5,6},{6,7},{7,8},{8,9},{9,10},{10,1... | collective-permute-start | bytes 506888 | tf_op jit(solution)/shard_map/ppermute | solution.py:378
  18.9 0.0 collective-permute-done.up
  18.9 0.0 collective-permute-done.1.dn
  19.0 1.0 %outside.1 = (f32[5,2,33,8,128]{4,3,2,1,0:T(8,128)S(1)}, f32[10,2,33,8,128]{4,3,2,1,0:T(8,128)S(1)}) custom-call(bf16[10,3,2,1408]{3,2,1,0:T(2,128)(2,1)S(1)} %get-tuple-element.24.head, bf16[10,3,2,1408]{3,2,1,0:T(2,128)(2,1)S(1)} %get-tuple-element.23.tail, bf16[10,3,2,1408]{3,2,1,0:T(2,128)(2,1)S(1)} %collective-permute-done.up, ...), custom_call_target="tpu_custom_call" | custom-call | flops 3000000 | bytes 4730880 | tf_op jit(solution)/shard_map/outside/pallas_call | solution.py:322
  20.0 2.8 %own_pairs.1 = (f32[10,8,128]{2,1,0:T(8,128)S(1)}, f32[10,10,8,128]{3,2,1,0:T(8,128)S(1)}) custom-call(f32[5,2,33,8,128]{4,3,2,1,0:T(8,128)S(1)} %get-tuple-element.15.cells_outer, f32[3,2,33,8,128]{4,3,2,1,0:T(8,128)S(1)} %get-tuple-element.17.cells_inner, f32[10,2,33,8,128]{4,3,2,1,0:T(8,128)S(1)} %get-tuple-element.18.rep_outer, ...), custom_call_target="tpu_custom_call" | custom-call | flops 15000000 | bytes 8560640 | tf_op jit(solution)/shard_map/own_pairs/pallas_call | solution.py:322
  22.8 0.0 collective-permute-done.6.dn
  22.8 0.0 collective-permute-done.5.up
  22.8 2.8 %outer_pairs.1.outer = f32[28,32,128]{2,1,0:T(8,128)S(1)} custom-call(f32[10,2,33,8,128]{4,3,2,1,0:T(8,128)S(1)} %get-tuple-element.18.rep_outer, bf16[10,3,2,1408]{3,2,1,0:T(2,128)(2,1)S(1)} %collective-permute-done.2.head, bf16[10,3,2,1408]{3,2,1,0:T(2,128)(2,1)S(1)} %collective-permute-done.3.tail, ...), custom_call_target="tpu_custom_call" | custom-call | flops 15000000 | bytes 3837952 | tf_op jit(solution)/shard_map/outer_pairs/pallas_call | solution.py:322
  25.7 0.0 collective-permute-done.4.mid
  25.7 3.6 %inner_pairs.1 = f32[10,20,8,128]{3,2,1,0:T(8,128)} custom-call(f32[12,2,33,8,128]{4,3,2,1,0:T(8,128)S(1)} %get-tuple-element.14.rep_inner, f32[10,8,128]{2,1,0:T(8,128)S(1)} %get-tuple-element.19.own_scale, bf16[10,6,2,1408]{3,2,1,0:T(2,128)(2,1)S(1)} %collective-permute-done.4.mid, f32[28,32,128]{2,1,0:T(8,128)S(1)} %outer_pairs.1.outer, ...), custom_call_target="tpu_custom_call" | custom-call | flops 15000000 | bytes 5310464 | tf_op jit(solution)/shard_map/inner_pairs/pallas_call | solution.py:322
Async XLA Ops:
  1.2 11.2 %collective-permute-start.3 = (bf16[10,3,2,1408]{3,2,1,0:T(2,128)(2,1)S(1)}, bf16[10,3,2,1408]{3,2,1,0:T(2,128)(2,1)S(1)}, u32[]{:S(2)}, u32[]{:S(2)}) collective-permute-start(bf16[10,3,2,1408]{3,2,1,0:T(2,128)(2,1)S(1)} %get-tuple-element.23.tail), channel_id=1, source_target_pairs={{0,16},{16,0},{1,17},{17,1},{2,18},{18,2},{3,19},{19,3},{4,20},{20... | collective-permute-start | bytes 506888 | tf_op jit(solution)/shard_map/ppermute | solution.py:350
  2.5 9.9 %collective-permute-start.2 = (bf16[10,3,2,1408]{3,2,1,0:T(2,128)(2,1)S(1)}, bf16[10,3,2,1408]{3,2,1,0:T(2,128)(2,1)S(1)}, u32[]{:S(2)}, u32[]{:S(2)}) collective-permute-start(bf16[10,3,2,1408]{3,2,1,0:T(2,128)(2,1)S(1)} %get-tuple-element.24.head), channel_id=1, source_target_pairs={{0,16},{16,0},{1,17},{17,1},{2,18},{18,2},{3,19},{19,3},{4,20},{20... | collective-permute-start | bytes 506888 | tf_op jit(solution)/shard_map/ppermute | solution.py:349
  4.0 21.7 %collective-permute-start.4 = (bf16[10,6,2,1408]{3,2,1,0:T(2,128)(2,1)S(1)}, bf16[10,6,2,1408]{3,2,1,0:T(2,128)(2,1)S(1)}, u32[]{:S(2)}, u32[]{:S(2)}) collective-permute-start(bf16[10,6,2,1408]{3,2,1,0:T(2,128)(2,1)S(1)} %slice.12.mid), channel_id=1, source_target_pairs={{0,16},{16,0},{1,17},{17,1},{2,18},{18,2},{3,19},{19,3},{4,20},{20... | collective-permute-start | bytes 1013768 | tf_op jit(solution)/shard_map/ppermute | solution.py:351
  5.3 13.7 %collective-permute-start = (bf16[10,3,2,1408]{3,2,1,0:T(2,128)(2,1)S(1)}, bf16[10,3,2,1408]{3,2,1,0:T(2,128)(2,1)S(1)}, u32[]{:S(2)}, u32[]{:S(2)}) collective-permute-start(bf16[10,3,2,1408]{3,2,1,0:T(2,128)(2,1)S(1)} %get-tuple-element.23.tail), channel_id=1, source_target_pairs={{0,1},{1,2},{2,3},{3,4},{4,5},{5,6},{6,7},{7,8},{8,9},{9,10},{10,1... | collective-permute-start | bytes 506888 | tf_op jit(solution)/shard_map/ppermute | solution.py:352
  9.8 9.1 %collective-permute-start.1 = (bf16[10,3,2,1408]{3,2,1,0:T(2,128)(2,1)S(1)}, bf16[10,3,2,1408]{3,2,1,0:T(2,128)(2,1)S(1)}, u32[]{:S(2)}, u32[]{:S(2)}) collective-permute-start(bf16[10,3,2,1408]{3,2,1,0:T(2,128)(2,1)S(1)} %get-tuple-element.24.head), channel_id=1, source_target_pairs={{1,0},{2,1},{3,2},{4,3},{5,4},{6,5},{7,6},{8,7},{9,8},{10,9},{11,1... | collective-permute-start | bytes 506888 | tf_op jit(solution)/shard_map/ppermute | solution.py:353
  12.5 10.4 %collective-permute-start.6 = (bf16[10,3,2,1408]{3,2,1,0:T(2,128)(2,1)S(1)}, bf16[10,3,2,1408]{3,2,1,0:T(2,128)(2,1)S(1)}, u32[]{:S(2)}, u32[]{:S(2)}) collective-permute-start(bf16[10,3,2,1408]{3,2,1,0:T(2,128)(2,1)S(1)} %collective-permute-done.2.head), channel_id=1, source_target_pairs={{1,0},{2,1},{3,2},{4,3},{5,4},{6,5},{7,6},{8,7},{9,8},{10,9},{11,1... | collective-permute-start | bytes 506888 | tf_op jit(solution)/shard_map/ppermute | solution.py:379
  15.0 7.8 %collective-permute-start.5 = (bf16[10,3,2,1408]{3,2,1,0:T(2,128)(2,1)S(1)}, bf16[10,3,2,1408]{3,2,1,0:T(2,128)(2,1)S(1)}, u32[]{:S(2)}, u32[]{:S(2)}) collective-permute-start(bf16[10,3,2,1408]{3,2,1,0:T(2,128)(2,1)S(1)} %collective-permute-done.3.tail), channel_id=1, source_target_pairs={{0,1},{1,2},{2,3},{3,4},{4,5},{5,6},{6,7},{7,8},{8,9},{9,10},{10,1... | collective-permute-start | bytes 506888 | tf_op jit(solution)/shard_map/ppermute | solution.py:378

commit v3 on v2

--- a/solution.py
+++ b/solution.py
@@ -179,12 +179,17 @@
 def window(first, count, outer, inner, sums):
     lane = iota(1)
     left, right = lane > 0, lane < LANES - 1
+    odd = iota(0) * 0 + lax.rem(lax.axis_index("strip"), 2) == 1
+
+    def flip(v):
+        n = len(v)
+        return [jnp.where(odd, v[r], v[n - 1 - r]) for r in range(n)]
 
     def one(g, carry):
         e = [outer[g, pl.ds(x, 8, stride=4), :] for x in range(4)]
-        m = [inner[g, pl.ds(x, 8, stride=2), :] for x in range(2)]
+        m = flip([inner[g, pl.ds(x, 8, stride=2), :] for x in range(2)])
         t, u = e[1] + m[0], m[1] + e[2]
-        for r, v in enumerate((e[0] + t, t + m[1], m[0] + u, u + e[3])):
+        for r, v in enumerate(flip([e[0] + t, t + m[1], m[0] + u, u + e[3]])):
             v = (
                 v
                 + jnp.where(left, pltpu.roll(v, 1, 1), 0.0)
@@ -204,43 +209,37 @@
     return [(q, min(4, dates - 4 * q)) for q in range((dates + 3) // 4)]
 
 
-def inside_kernel(dates, mid, cells, rep, flat):
-    ins = (dates + 3) // 4
+def inside_kernel(dates, mid, rep, inner, flat, cells):
+    outs = groups = dates // 2
+    chunks = inner_chunks(dates)
     unpack_inner(dates, mid, flat, 0)
-    rotate(0, ins, flat, cells)
-    place(0, ins, cells, spread_inner(rep, 0))
-
-
-def outside_kernel(dates, head, tail, up, dn, cells, rep, flat):
-    outs = dates // 2
-    unpack_outer(dates, (up, head, tail, dn), flat)
-    rotate(0, outs, flat, cells)
-    place(0, outs, cells, spread_outer(rep))
-
-
-def own_kernel(
-    dates, cells_outer, cells_inner, rep_outer, rep_inner, scale, coh, outer, inner, sums
-):
-    outs = dates // 2
-    groups = dates // 2
-    sign = jnp.where(iota(0) < 4, 1.0, -1.0)
-    for n, pw in enumerate(powers(range(outs), cells_outer)):
-        put_outer(outer, outs * groups, 2 * n, pw, pw)
-    chunks = inner_chunks(dates)
-    for (q, size), pw in zip(chunks, powers([q for q, _ in chunks], cells_inner)):
+    rotate(0, len(chunks), flat, cells)
+    place(0, len(chunks), cells, spread_inner(rep, 0))
+    for (q, size), pw in zip(chunks, powers([q for q, _ in chunks], cells)):
         put_inner(inner, outs * groups, 4 * q, pw, pw, size)
     for b in range(outs):
         rows = [2 * b, 2 * b + 1]
+        picks = [c for c in chunks if 4 * c[0] + c[1] > 2 * b]
+        for i, j, re, im in products(rows, [q for q, _ in picks], rep, cells):
+            put_inner(inner, groups * b, dates * i + 4 * picks[j][0], re, im, picks[j][1])
+
+
+def own_kernel(dates, near, far, near_halo, far_halo, inner, rep, scale, coh, flat, cells, outer, sums):
+    outs = groups = dates // 2
+    sign = jnp.where(iota(0) < 4, 1.0, -1.0)
+    unpack_outer(dates, (near_halo, near, far, far_halo), flat)
+    rotate(0, outs, flat, cells)
+    place(0, outs, cells, spread_outer(rep))
+    for n, pw in enumerate(powers(range(outs), cells)):
+        put_outer(outer, outs * groups, 2 * n, pw, pw)
+    for b in range(outs):
+        rows = [2 * b, 2 * b + 1]
         cols = list(range(b, outs))
-        for i, j, re, im in products(rows, cols, rep_outer, cells_outer):
+        for i, j, re, im in products(rows, cols, rep, cells):
             put_outer(outer, groups * b, dates * i + 2 * cols[j], re, im)
-        picks = [c for c in chunks if 4 * c[0] + c[1] > 2 * b]
-        for i, j, re, im in products(rows, [q for q, _ in picks], rep_inner, cells_inner):
-            put_inner(inner, groups * b, dates * i + 4 * picks[j][0], re, im, picks[j][1])
     window(0, outs * groups + (dates + 3) // 4, outer, inner, sums)
     for j in range(dates):
         scale[j] = lax.rsqrt(sum_at(sums, outs * groups, j) + EPS)
-
     for b in range(outs):
         for i in range(2):
             for j in range(2 * b + i, dates):
@@ -250,10 +249,9 @@
                     coh[j, 2 * b + i] = v * sign
 
 
-def outer_kernel(dates, rep_outer, head, tail, up, dn, outer, flat, cells):
-    outs = dates // 2
-    groups = dates // 2
-    unpack_outer(dates, (up, head, tail, dn), flat)
+def outer_kernel(dates, rep, near, far, near_halo, far_halo, outer, flat, cells):
+    outs = groups = dates // 2
+    unpack_outer(dates, (near_halo, near, far, far_halo), flat)
     rotate(0, outs, flat, cells)
     place(0, outs, cells)
     for n, pw in enumerate(powers(range(outs), cells)):
@@ -261,7 +259,7 @@
 
     def one(b, carry):
         rows = [2 * b, 2 * b + 1]
-        for i, j, re, im in products(rows, range(outs), rep_outer, cells):
+        for i, j, re, im in products(rows, range(outs), rep, cells):
             put_outer(outer, groups * b, dates * i + 2 * j, re, im)
         return carry
 
@@ -335,62 +333,61 @@
     dates, _, rows, width = slc.shape
     count = lax.axis_size("date")
     strips = lax.axis_size("strip")
-    up_pairs = [(i, i + 1) for i in range(strips - 1)]
-    dn_pairs = [(i + 1, i) for i in range(strips - 1)]
+    chip = [(i, i ^ 1) for i in range(strips)]
+    chips = [(i, i + 1 if i % 2 else i - 1) for i in range(1, strips - 1)]
     outs, ins = dates // 2, (dates + 3) // 4
     total = outs * outs + (dates + 3) // 4
     shape = jax.ShapeDtypeStruct
 
+    def flat(q):
+        return pltpu.VMEM((q, CELL, 48, LANES), F32)
+
+    def cell(q):
+        return (q, 2, STEPS, *TILE)
+
     x = jnp.transpose(slc, (0, 2, 1, 3))
-    head, tail, mid = x[:, :3], x[:, rows - 3 :], x[:, 3 : rows - 3]
-    heads, tails, mids = [], [], []
+    odd = lax.rem(lax.axis_index("strip"), 2)
+    near = lax.dynamic_slice_in_dim(x, (1 - odd) * (rows - 3), 3, 1)
+    far = lax.dynamic_slice_in_dim(x, odd * (rows - 3), 3, 1)
+    mid = x[:, 3 : rows - 3]
+    nears, fars, mids = [], [], []
     for t in range(1, count):
         ring = [(i, (i + t) % count) for i in range(count)]
-        heads.append(lax.ppermute(head, "date", ring))
-        tails.append(lax.ppermute(tail, "date", ring))
+        fars.append(lax.ppermute(far, "date", ring))
+        nears.append(lax.ppermute(near, "date", ring))
         mids.append(lax.ppermute(mid, "date", ring))
-    up = lax.ppermute(tail, "strip", up_pairs)
-    dn = lax.ppermute(head, "strip", dn_pairs)
-
-    def flat(q):
-        return pltpu.VMEM((q, CELL, 48, LANES), F32)
-
-    def cell(q):
-        return (q, 2, STEPS, *TILE)
-
-    cells_inner, rep_inner = call(
+    rep_inner, own_inner = call(
         functools.partial(inside_kernel, dates),
         "inside",
         (mid,),
-        (shape(cell(ins), F32), shape(cell(4 * ins), F32)),
-        [flat(ins)],
-        flops=3_000_000,
+        (shape(cell(4 * ins), F32), shape((total, 16, LANES), F32)),
+        [flat(ins), pltpu.VMEM(cell(ins), F32)],
+        flops=15_000_000,
     )
-    heads, tails, cells_inner = lax.optimization_barrier((heads, tails, cells_inner))
-    cells_outer, rep_outer = call(
-        functools.partial(outside_kernel, dates),
-        "outside",
-        (head, tail, up, dn),
-        (shape(cell(outs), F32), shape(cell(2 * outs), F32)),
-        [flat(outs)],
-        flops=3_000_000,
-    )
-    ups = [lax.ppermute(v, "strip", up_pairs) for v in tails]
-    dns = [lax.ppermute(v, "strip", dn_pairs) for v in heads]
-    pads = [pltpu.VMEM((total, r, LANES), F32) for r in (32, 16, 32)]
-    scale, out = call(
+    fars, own_far, rep_inner = lax.optimization_barrier((fars, far, rep_inner))
+    far_halo = lax.ppermute(own_far, "strip", chips)
+    far_halos = [lax.ppermute(v, "strip", chips) for v in fars]
+    nears, own_near = lax.optimization_barrier((nears, near))
+    near_halo = lax.ppermute(own_near, "strip", chip)
+    near_halos = [lax.ppermute(v, "strip", chip) for v in nears]
+    sums = pltpu.VMEM((total, 32, LANES), F32)
+    rep_outer, scale, out = call(
         functools.partial(own_kernel, dates),
         "own_pairs",
-        (cells_outer, cells_inner, rep_outer, rep_inner),
-        (shape((dates, *TILE), F32), shape((dates, dates, *TILE), F32)),
-        pads,
+        (near, far, near_halo, far_halo, own_inner),
+        (
+            shape(cell(2 * outs), F32),
+            shape((dates, *TILE), F32),
+            shape((dates, dates, *TILE), F32),
+        ),
+        [flat(outs), pltpu.VMEM(cell(outs), F32), sums, sums],
         flops=15_000_000,
     )
     for t in range(1, count):
         (outer,) = call(
             functools.partial(outer_kernel, dates),
             "outer_pairs",
-            (rep_outer, heads[t - 1], tails[t - 1], ups[t - 1], dns[t - 1]),
+            (rep_outer, nears[t - 1], fars[t - 1], near_halos[t - 1], far_halos[t - 1]),
             (shape((total, 32, LANES), F32),),
             [flat(outs), pltpu.VMEM(cell(outs), F32)],
             flops=15_000_000,
@@ -400,7 +397,7 @@
             "inner_pairs",
             (rep_inner, scale, mids[t - 1], outer, out),
             (shape((dates, dates * count, *TILE), F32),),
-            [flat(ins), pltpu.VMEM(cell(ins), F32)] + pads[1:],
+            [flat(ins), pltpu.VMEM(cell(ins), F32), pltpu.VMEM((total, 16, LANES), F32), sums],
             flops=15_000_000,
         )
     return out.reshape(dates, dates * count, 2, 4, LANES)

time: 29.5 us -> 27.9 us (0.946)
  the two profiles are of different devices: /device:TPU:5 before, /device:TPU:9 now
where the time goes in v3:
time: 27.9 us; the launch traced here: 27.7 us
  starting transfers between devices  12.2 us (44%)
  Pallas kernels  11 us (39%)
  local copies, waits for them, and re-layouts  2.44 us (9%)
  waiting for transfers between devices  2.03 us (7%)
    pallas_call x4, Pallas kernels, call(): pl.pallas_call(kernel, out_shape=tuple(outs), in_specs=[vm] * len(args),...  11 us
    ppermute x1, starting transfers between devices, per_device(): far_halo = lax.ppermute(own_far, 'strip', chips)  5.34 us
    ppermute x1, starting transfers between devices, per_device(): far_halos = [lax.ppermute(v, 'strip', chips) for v in fars]  3.02 us
    ppermute x1, starting transfers between devices, per_device(): fars.append(lax.ppermute(far, 'date', ring))  1.28 us
    ppermute x1, starting transfers between devices, per_device(): mids.append(lax.ppermute(mid, 'date', ring))  1.28 us
    dynamic_slice x1, local copies, waits for them, and re-layouts, per_device(): near = lax.dynamic_slice_in_dim(x, (1 - odd) * (rows - 3), 3, 1)  1.23 us
    slice x1, local copies, waits for them, and re-layouts, per_device(): mid = x[:, 3:rows - 3]  1.21 us
    ppermute x1, waiting for transfers between devices, per_device(): far_halo = lax.ppermute(own_far, 'strip', chips)  1.07 us
  transfers between devices with their start and end apart: 7, of which 2 were waited for; matrix products, arithmetic and copies ran while one was open for 4% of the time, Pallas kernels for 27%

profile of v3, /device:TPU:9, one launch (start us, length us, event | category | flops | bytes accessed | tf_op | source)
XLA Modules:
  0.0 27.7 jit_solution(18222492793055697388)
XLA Ops:
  0.0 1.2 %dynamic-slice_bitcast_fusion = (bf16[10,3,2,1408]{3,2,1,0:T(2,128)(2,1)S(1)}, bf16[10,3,2,1408]{3,2,1,0:T(2,128)(2,1)S(1)}) fusion(bf16[10,2,12,1408]{3,1,2,0:T(2,128)(2,1)} %param.1, s32[]{:T(128)S(6)} %select_n.7, s32[]{:T(128)S(6)} %select_n.6), kind=kLoop, calls=%fused_computation | loop fusion | bytes 675848 | tf_op jit(solution)/shard_map/dynamic_slice | solution.py:350
  1.2 1.3 %collective-permute-start = (bf16[10,3,2,1408]{3,2,1,0:T(2,128)(2,1)S(1)}, bf16[10,3,2,1408]{3,2,1,0:T(2,128)(2,1)S(1)}, u32[]{:S(2)}, u32[]{:S(2)}) collective-permute-start(bf16[10,3,2,1408]{3,2,1,0:T(2,128)(2,1)S(1)} %get-tuple-element.18.far), channel_id=1, source_target_pairs={{0,16},{16,0},{1,17},{17,1},{2,18},{18,2},{3,19},{19,3},{4,20},{20... | collective-permute-start | bytes 506888 | tf_op jit(solution)/shard_map/ppermute | solution.py:356
  2.5 0.3 collective-permute-start.1
  2.8 1.2 %slice.4.mid = bf16[10,6,2,1408]{3,2,1,0:T(2,128)(2,1)S(1)} slice(bf16[10,12,2,1408]{3,2,1,0:T(2,128)(2,1)} %bitcast.6), slice={[0:10], [3:9], [0:2], [0:1408]} | slice | bytes 675840 | tf_op jit(solution)/shard_map/slice | solution.py:352
  4.0 1.3 %collective-permute-start.4 = (bf16[10,6,2,1408]{3,2,1,0:T(2,128)(2,1)S(1)}, bf16[10,6,2,1408]{3,2,1,0:T(2,128)(2,1)S(1)}, u32[]{:S(2)}, u32[]{:S(2)}) collective-permute-start(bf16[10,6,2,1408]{3,2,1,0:T(2,128)(2,1)S(1)} %slice.4.mid), channel_id=1, source_target_pairs={{0,16},{16,0},{1,17},{17,1},{2,18},{18,2},{3,19},{19,3},{4,20},{20... | collective-permute-start | bytes 1013768 | tf_op jit(solution)/shard_map/ppermute | solution.py:358
  5.3 1.6 %inside.1 = (f32[12,2,33,8,128]{4,3,2,1,0:T(8,128)S(1)}, f32[28,16,128]{2,1,0:T(8,128)S(1)}) custom-call(bf16[10,6,2,1408]{3,2,1,0:T(2,128)(2,1)S(1)} %slice.4.mid), custom_call_target="tpu_custom_call" | custom-call | flops 15000000 | bytes 3811328 | tf_op jit(solution)/shard_map/inside/pallas_call | solution.py:320
  6.8 0.0 collective-permute-done.far
  6.9 5.3 %collective-permute-start.3 = (bf16[10,3,2,1408]{3,2,1,0:T(2,128)(2,1)S(1)}, bf16[10,3,2,1408]{3,2,1,0:T(2,128)(2,1)S(1)}, u32[]{:S(2)}, u32[]{:S(2)}) collective-permute-start(bf16[10,3,2,1408]{3,2,1,0:T(2,128)(2,1)S(1)} %get-tuple-element.18.far), channel_id=1, source_target_pairs={{1,2},{2,1},{3,4},{4,3},{5,6},{6,5},{7,8},{8,7},{9,10},{10,9},{11,... | collective-permute-start | bytes 506888 | tf_op jit(solution)/shard_map/ppermute | solution.py:368
  12.2 0.0 collective-permute-done.1.near
  12.2 0.6 %collective-permute-start.2 = (bf16[10,3,2,1408]{3,2,1,0:T(2,128)(2,1)S(1)}, bf16[10,3,2,1408]{3,2,1,0:T(2,128)(2,1)S(1)}, u32[]{:S(2)}, u32[]{:S(2)}) collective-permute-start(bf16[10,3,2,1408]{3,2,1,0:T(2,128)(2,1)S(1)} %get-tuple-element.17.near), channel_id=1, source_target_pairs={{0,1},{1,0},{2,3},{3,2},{4,5},{5,4},{6,7},{7,6},{8,9},{9,8},{10,11... | collective-permute-start | bytes 506888 | tf_op jit(solution)/shard_map/ppermute | solution.py:371
  12.8 3.0 %collective-permute-start.6 = (bf16[10,3,2,1408]{3,2,1,0:T(2,128)(2,1)S(1)}, bf16[10,3,2,1408]{3,2,1,0:T(2,128)(2,1)S(1)}, u32[]{:S(2)}, u32[]{:S(2)}) collective-permute-start(bf16[10,3,2,1408]{3,2,1,0:T(2,128)(2,1)S(1)} %collective-permute-done.far), channel_id=1, source_target_pairs={{1,2},{2,1},{3,4},{4,3},{5,6},{6,5},{7,8},{8,7},{9,10},{10,9},{11,... | collective-permute-start | bytes 506888 | tf_op jit(solution)/shard_map/ppermute | solution.py:369
  15.8 0.5 %collective-permute-start.5 = (bf16[10,3,2,1408]{3,2,1,0:T(2,128)(2,1)S(1)}, bf16[10,3,2,1408]{3,2,1,0:T(2,128)(2,1)S(1)}, u32[]{:S(2)}, u32[]{:S(2)}) collective-permute-start(bf16[10,3,2,1408]{3,2,1,0:T(2,128)(2,1)S(1)} %collective-permute-done.1.near), channel_id=1, source_target_pairs={{0,1},{1,0},{2,3},{3,2},{4,5},{5,4},{6,7},{7,6},{8,9},{9,8},{10,11... | collective-permute-start | bytes 506888 | tf_op jit(solution)/shard_map/ppermute | solution.py:372
  16.3 1.1 %collective-permute-done.3.far_halo = bf16[10,3,2,1408]{3,2,1,0:T(2,128)(2,1)S(1)} collective-permute-done((bf16[10,3,2,1408]{3,2,1,0:T(2,128)(2,1)S(1)}, bf16[10,3,2,1408]{3,2,1,0:T(2,128)(2,1)S(1)}, u32[]{:S(2)}, u32[]{:S(2)}) %collective-permute-start.3) | collective-permute-done | bytes 168992 | tf_op jit(solution)/shard_map/ppermute | solution.py:368
  17.4 0.0 collective-permute-done.2.near_halo
  17.4 3.0 %own_pairs.1 = (f32[10,2,33,8,128]{4,3,2,1,0:T(8,128)S(1)}, f32[10,8,128]{2,1,0:T(8,128)S(1)}, f32[10,10,8,128]{3,2,1,0:T(8,128)S(1)}) custom-call(bf16[10,3,2,1408]{3,2,1,0:T(2,128)(2,1)S(1)} %get-tuple-element.17.near, bf16[10,3,2,1408]{3,2,1,0:T(2,128)(2,1)S(1)} %get-tuple-element.18.far, bf16[10,3,2,1408]{3,2,1,0:T(2,128)(2,1)S(1)} %collective-permute-done.2.near_halo, ...), custom_call_target="tpu_custom_call" | custom-call | flops 15000000 | bytes 4059136 | tf_op jit(solution)/shard_map/own_pairs/pallas_call | solution.py:320
  20.3 1.0 %collective-permute-done.6.far_halo = bf16[10,3,2,1408]{3,2,1,0:T(2,128)(2,1)S(1)} collective-permute-done((bf16[10,3,2,1408]{3,2,1,0:T(2,128)(2,1)S(1)}, bf16[10,3,2,1408]{3,2,1,0:T(2,128)(2,1)S(1)}, u32[]{:S(2)}, u32[]{:S(2)}) %collective-permute-start.6) | collective-permute-done | bytes 168992 | tf_op jit(solution)/shard_map/ppermute | solution.py:369
  21.3 0.0 collective-permute-done.5.near_halo
  21.3 2.8 %outer_pairs.1.outer = f32[28,32,128]{2,1,0:T(8,128)S(1)} custom-call(f32[10,2,33,8,128]{4,3,2,1,0:T(8,128)S(1)} %get-tuple-element.21.rep, bf16[10,3,2,1408]{3,2,1,0:T(2,128)(2,1)S(1)} %collective-permute-done.1.near, bf16[10,3,2,1408]{3,2,1,0:T(2,128)(2,1)S(1)} %collective-permute-done.far, bf16[10,3,2,1408]{3,2,1,0:T(2,128)(2,1)S(1)} %collective-permute-done.5.near_halo, ...), custom_call_target="tpu_custom_call" | custom-call | flops 15000000 | bytes 3837952 | tf_op jit(solution)/shard_map/outer_pairs/pallas_call | solution.py:320
  24.1 0.0 collective-permute-done.4.mid
  24.1 3.6 %inner_pairs.1 = f32[10,20,8,128]{3,2,1,0:T(8,128)} custom-call(f32[12,2,33,8,128]{4,3,2,1,0:T(8,128)S(1)} %get-tuple-element.16.rep_inner, f32[10,8,128]{2,1,0:T(8,128)S(1)} %get-tuple-element.20.own_scale, bf16[10,6,2,1408]{3,2,1,0:T(2,128)(2,1)S(1)} %collective-permute-done.4.mid, f32[28,32,128]{2,1,0:T(8,128)S(1)} %outer_pairs.1.outer, ...), custom_call_target="tpu_custom_call" | custom-call | flops 15000000 | bytes 5310464 | tf_op jit(solution)/shard_map/inner_pairs/pallas_call | solution.py:320
Async XLA Ops:
  1.2 5.6 %collective-permute-start = (bf16[10,3,2,1408]{3,2,1,0:T(2,128)(2,1)S(1)}, bf16[10,3,2,1408]{3,2,1,0:T(2,128)(2,1)S(1)}, u32[]{:S(2)}, u32[]{:S(2)}) collective-permute-start(bf16[10,3,2,1408]{3,2,1,0:T(2,128)(2,1)S(1)} %get-tuple-element.18.far), channel_id=1, source_target_pairs={{0,16},{16,0},{1,17},{17,1},{2,18},{18,2},{3,19},{19,3},{4,20},{20... | collective-permute-start | bytes 506888 | tf_op jit(solution)/shard_map/ppermute | solution.py:356
  2.5 9.7 %collective-permute-start.1 = (bf16[10,3,2,1408]{3,2,1,0:T(2,128)(2,1)S(1)}, bf16[10,3,2,1408]{3,2,1,0:T(2,128)(2,1)S(1)}, u32[]{:S(2)}, u32[]{:S(2)}) collective-permute-start(bf16[10,3,2,1408]{3,2,1,0:T(2,128)(2,1)S(1)} %get-tuple-element.17.near), channel_id=1, source_target_pairs={{0,16},{16,0},{1,17},{17,1},{2,18},{18,2},{3,19},{19,3},{4,20},{20... | collective-permute-start | bytes 506888 | tf_op jit(solution)/shard_map/ppermute | solution.py:357
  4.0 20.1 %collective-permute-start.4 = (bf16[10,6,2,1408]{3,2,1,0:T(2,128)(2,1)S(1)}, bf16[10,6,2,1408]{3,2,1,0:T(2,128)(2,1)S(1)}, u32[]{:S(2)}, u32[]{:S(2)}) collective-permute-start(bf16[10,6,2,1408]{3,2,1,0:T(2,128)(2,1)S(1)} %slice.4.mid), channel_id=1, source_target_pairs={{0,16},{16,0},{1,17},{17,1},{2,18},{18,2},{3,19},{19,3},{4,20},{20... | collective-permute-start | bytes 1013768 | tf_op jit(solution)/shard_map/ppermute | solution.py:358
  6.9 10.5 %collective-permute-start.3 = (bf16[10,3,2,1408]{3,2,1,0:T(2,128)(2,1)S(1)}, bf16[10,3,2,1408]{3,2,1,0:T(2,128)(2,1)S(1)}, u32[]{:S(2)}, u32[]{:S(2)}) collective-permute-start(bf16[10,3,2,1408]{3,2,1,0:T(2,128)(2,1)S(1)} %get-tuple-element.18.far), channel_id=1, source_target_pairs={{1,2},{2,1},{3,4},{4,3},{5,6},{6,5},{7,8},{8,7},{9,10},{10,9},{11,... | collective-permute-start | bytes 506888 | tf_op jit(solution)/shard_map/ppermute | solution.py:368
  12.2 5.1 %collective-permute-start.2 = (bf16[10,3,2,1408]{3,2,1,0:T(2,128)(2,1)S(1)}, bf16[10,3,2,1408]{3,2,1,0:T(2,128)(2,1)S(1)}, u32[]{:S(2)}, u32[]{:S(2)}) collective-permute-start(bf16[10,3,2,1408]{3,2,1,0:T(2,128)(2,1)S(1)} %get-tuple-element.17.near), channel_id=1, source_target_pairs={{0,1},{1,0},{2,3},{3,2},{4,5},{5,4},{6,7},{7,6},{8,9},{9,8},{10,11... | collective-permute-start | bytes 506888 | tf_op jit(solution)/shard_map/ppermute | solution.py:371
  12.8 8.5 %collective-permute-start.6 = (bf16[10,3,2,1408]{3,2,1,0:T(2,128)(2,1)S(1)}, bf16[10,3,2,1408]{3,2,1,0:T(2,128)(2,1)S(1)}, u32[]{:S(2)}, u32[]{:S(2)}) collective-permute-start(bf16[10,3,2,1408]{3,2,1,0:T(2,128)(2,1)S(1)} %collective-permute-done.far), channel_id=1, source_target_pairs={{1,2},{2,1},{3,4},{4,3},{5,6},{6,5},{7,8},{8,7},{9,10},{10,9},{11,... | collective-permute-start | bytes 506888 | tf_op jit(solution)/shard_map/ppermute | solution.py:369
  15.8 5.5 %collective-permute-start.5 = (bf16[10,3,2,1408]{3,2,1,0:T(2,128)(2,1)S(1)}, bf16[10,3,2,1408]{3,2,1,0:T(2,128)(2,1)S(1)}, u32[]{:S(2)}, u32[]{:S(2)}) collective-permute-start(bf16[10,3,2,1408]{3,2,1,0:T(2,128)(2,1)S(1)} %collective-permute-done.1.near), channel_id=1, source_target_pairs={{0,1},{1,0},{2,3},{3,2},{4,5},{5,4},{6,7},{7,6},{8,9},{9,8},{10,11... | collective-permute-start | bytes 506888 | tf_op jit(solution)/shard_map/ppermute | solution.py:372

commit v4 on v3

v4 whole, which is shorter than its diff:
```python
import functools

import jax
import jax.numpy as jnp
from jax import lax
from jax.experimental import pallas as pl
from jax.experimental.pallas import tpu as pltpu
from jax.sharding import PartitionSpec as P

EPS = 1e-06
LANES = 128
CELL = 11
STEPS = 33
TILE = (8, LANES)
F32 = jnp.float32
VMEM = pltpu.MemorySpace.VMEM


def iota(dim):
    return lax.broadcasted_iota(jnp.int32, TILE, dim)


def put_rows(ref, date, row, flat, q, at):
    pair = ref[date, row].astype(F32)
    for m in range(CELL):
        flat[q, m, at : at + 2, :] = pair[:, m * LANES : (m + 1) * LANES]


def unpack(dates, refs, flat):
    def one(q, carry):
        for part in range(4):
            date = jnp.minimum(4 * q + part, dates - 1)
            for e, (ref, first) in enumerate(refs):
                for sub in range(3):
                    put_rows(ref, date, first + sub, flat, q, part * 12 + e * 6 + sub * 2)
        return carry

    lax.fori_loop(0, (dates + 3) // 4, one, 0)


def rotate(count, flat, cells):
    lane = iota(1)
    turn = lax.rem(lane * 3, CELL)
    bits = [(s, (turn & s) != 0) for s in (1, 2, 4, 8)]

    def one(q, carry):
        for part in range(6):
            v = [flat[q, m, pl.ds(part, 8, stride=6), :] for m in range(CELL)]
            for shift, mask in bits:
                v = [jnp.where(mask, v[(t + shift) % CELL], v[t]) for t in range(CELL)]
            for c in range(CELL):
                cells[q, part % 2, (part // 2) * CELL + c] = v[(8 * c) % CELL]
        return carry

    lax.fori_loop(0, count, one, 0)


def place(count, cells, rep=None):
    lane = iota(1)
    low = iota(0) < 4
    even = (iota(0) & 2) == 0

    def spread(q, ri, s, v):
        a = jnp.where(even, v, pltpu.roll(v, 2, 0))
        b = jnp.where(even, pltpu.roll(v, 6, 0), v)
        c, d = pltpu.roll(a, 4, 0), pltpu.roll(b, 4, 0)
        rep[4 * q, ri, s] = jnp.where(low, a, c)
        rep[4 * q + 1, ri, s] = jnp.where(low, b, d)
        rep[4 * q + 2, ri, s] = jnp.where(low, c, a)
        rep[4 * q + 3, ri, s] = jnp.where(low, d, b)

    for c in range(CELL):
        pick = (lane * CELL + c) & (LANES - 1)

        def one(q, carry):
            for ri in range(2):
                for sub in range(3):
                    s = sub * CELL + c
                    v = jnp.take_along_axis(cells[q, ri, s], pick, axis=1)
                    cells[q, ri, s] = v
                    if rep is not None:
                        spread(q, ri, s, v)
            return carry

        lax.fori_loop(0, count, one, 0, unroll=count)


def products(rows, cols, rep, cells):
    count = len(rows) * len(cols)

    def step(s, acc):
        a = [rep[i, 0, s] for i in rows]
        b = [rep[i, 1, s] for i in rows]
        ab = [x + y for x, y in zip(a, b)]
        acc = list(acc)
        at = 0
        for q in cols:
            c, d = cells[q, 0, s], cells[q, 1, s]
            cd = c - d
            for i in range(len(rows)):
                acc[at] = acc[at] + a[i] * c
                acc[at + 1] = acc[at + 1] + b[i] * d
                acc[at + 2] = acc[at + 2] + ab[i] * cd
                at += 3
        return tuple(acc)

    acc = lax.fori_loop(0, STEPS, step, (jnp.zeros(TILE, F32),) * (3 * count), unroll=11)
    at = 0
    for j in range(len(cols)):
        for i in range(len(rows)):
            p, q, r = acc[at : at + 3]
            yield i, j, p + q, r - p + q
            at += 3


def powers(qs, cells):
    def step(s, acc):
        out = []
        for n, q in enumerate(qs):
            c, d = cells[q, 0, s], cells[q, 1, s]
            out.append(acc[n] + c * c + d * d)
        return tuple(out)

    return lax.fori_loop(0, STEPS, step, (jnp.zeros(TILE, F32),) * len(qs), unroll=11)


def put(sums, group, at, first, second, dates):
    sub = iota(0)
    roll = pltpu.roll

    def merge(x, y, z, w):
        return jnp.where(sub < 4, jnp.where(sub < 2, x, y), jnp.where(sub < 6, z, w))

    pieces = [merge(first, roll(second, 2, 0), roll(first, 2, 0), roll(second, 4, 0))]
    if dates > 2:
        pieces.append(merge(roll(first, 4, 0), roll(second, 6, 0), roll(first, 6, 0), second))
    for n, piece in enumerate(pieces):
        p = at + 2 * n
        sums[group + p // 4, 4 * (p % 4) : 4 * (p % 4) + 8, :] = piece


def window(first, count, mids, edges, halos, out):
    lane = iota(1)
    left, right = lane > 0, lane < LANES - 1
    odd = iota(0) * 0 + lax.rem(lax.axis_index("strip"), 2) == 1

    def flip(v):
        n = len(v)
        return [jnp.where(odd, v[r], v[n - 1 - r]) for r in range(n)]

    def one(n, carry):
        g = first + n
        m, e, h = ([ref[g, pl.ds(x, 8, stride=2), :] for x in range(2)] for ref in (mids, edges, halos))
        m = flip(m)
        t, u = e[0] + m[0], m[1] + e[1]
        for r, v in enumerate(flip([h[0] + t, t + m[1], m[0] + u, u + h[1]])):
            v = (
                v
                + jnp.where(left, pltpu.roll(v, 1, 1), 0.0)
                + jnp.where(right, pltpu.roll(v, LANES - 1, 1), 0.0)
            )
            out[g, pl.ds(r, 8, stride=4), :] = v
        return carry

    lax.fori_loop(0, count, one, 0, unroll=min(count, 5))


def sum_at(sums, group, p):
    return sums[group + p // 4, 8 * (p % 4) : 8 * (p % 4) + 8, :]


def chunks_of(dates):
    return [(q, min(4, dates - 4 * q)) for q in range((dates + 3) // 4)]


def put_powers(dates, cells, sums):
    chunks = chunks_of(dates)
    for (q, size), pw in zip(chunks, powers([q for q, _ in chunks], cells)):
        put(sums, dates * dates // 4, 4 * q, pw, pw, size)


def regroup(dates, refs, flat, cells, rep=None):
    count = (dates + 3) // 4
    unpack(dates, refs, flat)
    rotate(count, flat, cells)
    place(count, cells, rep)


def own_class(dates, refs, rep, sums, flat, cells):
    outs = dates // 2
    regroup(dates, refs, flat, cells, rep)
    put_powers(dates, cells, sums)
    for b in range(outs):
        rows = [2 * b, 2 * b + 1]
        picks = [c for c in chunks_of(dates) if 4 * c[0] + c[1] > 2 * b]
        for i, j, re, im in products(rows, [q for q, _ in picks], rep, cells):
            put(sums, outs * b, dates * i + 4 * picks[j][0], re, im, picks[j][1])


def cross_block(dates, b, rep, cells, sums):
    chunks = chunks_of(dates)
    for i, j, re, im in products([2 * b, 2 * b + 1], range(len(chunks)), rep, cells):
        put(sums, dates // 2 * b, dates * i + 4 * j, re, im, chunks[j][1])


def own_mid_kernel(dates, mid, rep, sums, flat, cells):
    own_class(dates, ((mid, 0), (mid, 3)), rep, sums, flat, cells)


def own_edge_kernel(dates, near, far, rep, sums, flat, cells):
    own_class(dates, ((near, 0), (far, 0)), rep, sums, flat, cells)


def own_halo_kernel(dates, near, far, mids, edges, rep, scale, coh, flat, cells, halos, out):
    outs = dates // 2
    own_class(dates, ((near, 0), (far, 0)), rep, halos, flat, cells)
    window(0, outs * outs + (dates + 3) // 4, mids, edges, halos, out)
    sign = jnp.where(iota(0) < 4, 1.0, -1.0)
    for j in range(dates):
        scale[j] = lax.rsqrt(sum_at(out, outs * outs, j) + EPS)
    for b in range(outs):
        for i in range(2):
            for j in range(2 * b + i, dates):
                v = sum_at(out, outs * b, dates * i + j) * (scale[2 * b + i] * scale[j])
                coh[2 * b + i, j] = v
                if j != 2 * b + i:
                    coh[j, 2 * b + i] = v * sign


def cross_kernel(dates, rep, near, far, sums, flat, cells):
    regroup(dates, ((near, 0), (far, 0)), flat, cells)
    put_powers(dates, cells, sums)

    def one(b, carry):
        cross_block(dates, b, rep, cells, sums)
        return carry

    lax.fori_loop(0, dates // 2, one, 0)


def last_kernel(
    dates, count, turn, rep, own_scale, mid, edges, halos, before, out, flat, cells, mids, wide, scale, stage, sem
):
    outs = dates // 2
    me = lax.axis_index("date")
    if turn == 1:
        keep = pltpu.make_async_copy(before, out.at[:, pl.ds(me * dates, dates)], sem.at[outs])
        keep.start()
    regroup(dates, ((mid, 0), (mid, 3)), flat, cells)
    put_powers(dates, cells, mids)
    window(outs * outs, (dates + 3) // 4, mids, edges, halos, wide)
    for j in range(dates):
        scale[j] = lax.rsqrt(sum_at(wide, outs * outs, j) + EPS)
    base = lax.rem(me + count - turn, count) * dates

    def copy(b):
        rows = pl.ds(2 * b, 2)
        return pltpu.make_async_copy(stage.at[rows], out.at[rows, pl.ds(base, dates)], sem.at[b])

    def one(b, carry):
        cross_block(dates, b, rep, cells, mids)
        window(outs * b, outs, mids, edges, halos, wide)
        for i in range(2):
            mine = own_scale[2 * b + i]
            for j in range(dates):
                stage[2 * b + i, j] = sum_at(wide, outs * b, dates * i + j) * (mine * scale[j])
        copy(b).start()
        return carry

    lax.fori_loop(0, outs, one, 0)
    for b in range(outs):
        copy(b).wait()
    if turn == 1:
        keep.wait()


def call(kernel, name, args, outs, scratch=(), flops=0, limit=32, hbm=False, aliases=None):
    vm = pl.BlockSpec(memory_space=VMEM)
    far = pl.BlockSpec(memory_space=pltpu.MemorySpace.HBM)
    ins = [vm] * len(args)
    for n in aliases or {}:
        ins[n] = far
    size = sum(a.size * a.dtype.itemsize for a in (*args, *outs))
    return pl.pallas_call(
        kernel,
        out_shape=tuple(outs),
        in_specs=ins,
        out_specs=(far if hbm else vm,) * len(outs),
        scratch_shapes=list(scratch),
        input_output_aliases=aliases or {},
        compiler_params=pltpu.CompilerParams(vmem_limit_bytes=limit << 20),
        cost_estimate=pl.CostEstimate(flops=flops, bytes_accessed=size, transcendentals=0),
        name=name,
    )(*args)


def per_device(slc):
    dates, _, rows, width = slc.shape
    count = lax.axis_size("date")
    strips = lax.axis_size("strip")
    chip = [(i, i ^ 1) for i in range(strips)]
    chips = [(i, i + 1 if i % 2 else i - 1) for i in range(1, strips - 1)]
    groups, quads = dates // 2, (dates + 3) // 4
    total = groups * groups + quads
    shape = jax.ShapeDtypeStruct
    sums = shape((total, 16, LANES), F32)
    rep = shape((4 * quads, 2, STEPS, *TILE), F32)
    flat = pltpu.VMEM((quads, CELL, 48, LANES), F32)
    cells = pltpu.VMEM((quads, 2, STEPS, *TILE), F32)
    wide = pltpu.VMEM((total, 32, LANES), F32)
    scales = shape((dates, *TILE), F32)

    def run(kernel, name, args, outs, scratch=(), **options):
        return call(functools.partial(kernel, dates), name, args, outs, (flat, cells, *scratch), flops=15_000_000, **options)

    x = jnp.transpose(slc, (0, 2, 1, 3))
    odd = lax.rem(lax.axis_index("strip"), 2)
    far = lax.dynamic_slice_in_dim(x, odd * (rows - 3), 3, 1)
    x, far = lax.optimization_barrier((x, far))
    near = lax.dynamic_slice_in_dim(x, (1 - odd) * (rows - 3), 3, 1)
    mid = x[:, 3 : rows - 3]
    near, mid = lax.optimization_barrier((near, mid))
    nears, fars, mids = [], [], []
    for t in range(1, count):
        ring = [(i, (i + t) % count) for i in range(count)]
        fars.append(lax.ppermute(far, "date", ring))
        nears.append(lax.ppermute(near, "date", ring))
        mids.append(lax.ppermute(mid, "date", ring))
    rep_mid, own_mid = run(own_mid_kernel, "own_mid", (mid,), (rep, sums))
    fars, own_far, rep_mid = lax.optimization_barrier((fars, far, rep_mid))
    far_halo = lax.ppermute(own_far, "strip", chips)
    far_halos = [lax.ppermute(v, "strip", chips) for v in fars]
    far_halo, far_halos = lax.optimization_barrier((far_halo, far_halos))
    rep_edge, own_edge = run(own_edge_kernel, "own_edge", (near, own_far), (rep, sums))
    nears, own_near, rep_edge = lax.optimization_barrier((nears, near, rep_edge))
    near_halo = lax.ppermute(own_near, "strip", chip)
    near_halos = [lax.ppermute(v, "strip", chip) for v in nears]
    near_halo, near_halos = lax.optimization_barrier((near_halo, near_halos))
    halo_sums = pltpu.VMEM(sums.shape, F32)
    rep_halo, scale, out = run(
        own_halo_kernel,
        "own_halo",
        (near_halo, far_halo, own_mid, own_edge),
        (rep, scales, shape((dates, dates, *TILE), F32)),
        (halo_sums, wide),
    )
    for t in range(1, count):
        (edge,) = run(cross_kernel, "cross_edge", (rep_edge, nears[t - 1], fars[t - 1]), (sums,))
        (halo,) = run(
            cross_kernel, "cross_halo", (rep_halo, near_halos[t - 1], far_halos[t - 1]), (sums,)
        )
        (out,) = call(
            functools.partial(last_kernel, dates, count, t),
            "cross_mid",
            (rep_mid, scale, mids[t - 1], edge, halo, out),
            (shape((dates, dates * count, *TILE), F32),),
            (
                flat,
                cells,
                halo_sums,
                wide,
                pltpu.VMEM(scales.shape, F32),
                pltpu.VMEM((dates, dates, *TILE), F32),
                pltpu.SemaphoreType.DMA((groups + 1,)),
            ),
            flops=15_000_000,
            hbm=True,
            aliases={5: 0} if t > 1 else None,
        )
    return out.reshape(dates, dates * count, 2, 4, LANES)


def solution(mesh):
    return jax.shard_map(
        per_device,
        mesh=mesh,
        in_specs=(P("date", None, "strip", None),),
        out_specs=P("date", None, None, "strip", None),
        check_vma=False,
    )
```

time: 27.9 us -> 28.5 us (1.022)
  the two profiles are of different devices: /device:TPU:9 before, /device:TPU:1 now
where the time goes in v4:
time: 28.5 us; the launch traced here: 28.3 us
  Pallas kernels  12.4 us (44%)
  starting transfers between devices  10.7 us (38%)
  local copies, waits for them, and re-layouts  3.29 us (12%)
  waiting for transfers between devices  1.81 us (6%)
    pallas_call x6, Pallas kernels, call(): pl.pallas_call(kernel, out_shape=tuple(outs), in_specs=ins, out_specs=(fa...  12.4 us
    ppermute x1, starting transfers between devices, per_device(): far_halo = lax.ppermute(own_far, 'strip', chips)  4.55 us
    ppermute x1, starting transfers between devices, per_device(): fars.append(lax.ppermute(far, 'date', ring))  2.11 us
    ppermute x1, starting transfers between devices, per_device(): far_halos = [lax.ppermute(v, 'strip', chips) for v in fars]  1.92 us
    ppermute x1, waiting for transfers between devices, per_device(): far_halos = [lax.ppermute(v, 'strip', chips) for v in fars]  1.8 us
    ppermute x1, starting transfers between devices, per_device(): mids.append(lax.ppermute(mid, 'date', ring))  1.44 us
    slice x1, local copies, waits for them, and re-layouts, per_device(): mid = x[:, 3:rows - 3]  1.22 us
    dynamic_slice x1, local copies, waits for them, and re-layouts, per_device(): far = lax.dynamic_slice_in_dim(x, odd * (rows - 3), 3, 1)  1.04 us
  transfers between devices with their start and end apart: 7, of which 1 were waited for; matrix products, arithmetic and copies ran while one was open for 8% of the time, Pallas kernels for 32%

profile of v4, /device:TPU:1, one launch (start us, length us, event | category | flops | bytes accessed | tf_op | source)
XLA Modules:
  0.0 28.3 jit_solution(8174129658897355097)
XLA Ops:
  0.0 1.0 %dynamic-slice_bitcast_fusion.far = bf16[10,3,2,1408]{3,2,1,0:T(2,128)(2,1)S(1)} fusion(bf16[10,2,12,1408]{3,1,2,0:T(2,128)(2,1)} %param.1, s32[]{:T(128)S(6)} %select_n.6), kind=kLoop, calls=%fused_computation | loop fusion | bytes 337924 | tf_op jit(solution)/shard_map/dynamic_slice | solution.py:318
  1.0 2.1 %collective-permute-start = (bf16[10,3,2,1408]{3,2,1,0:T(2,128)(2,1)S(1)}, bf16[10,3,2,1408]{3,2,1,0:T(2,128)(2,1)S(1)}, u32[]{:S(2)}, u32[]{:S(2)}) collective-permute-start(bf16[10,3,2,1408]{3,2,1,0:T(2,128)(2,1)S(1)} %dynamic-slice_bitcast_fusion.far), channel_id=1, source_target_pairs={{0,16},{16,0},{1,17},{17,1},{2,18},{18,2},{3,19},{19,3},{4,20},{20... | collective-permute-start | bytes 506888 | tf_op jit(solution)/shard_map/ppermute | solution.py:326
  3.1 1.0 %constant_dynamic-slice_fusion.near = bf16[10,3,2,1408]{3,2,1,0:T(2,128)(2,1)S(1)} fusion(bf16[10,12,2,1408]{3,2,1,0:T(2,128)(2,1)} %bitcast.4, s32[]{:T(128)S(6)} %select_n.7), kind=kLoop, calls=%fused_computation.1 | loop fusion | bytes 337924 | tf_op jit(solution)/shard_map/dynamic_slice | solution.py:320
  4.2 1.2 %slice.3.mid = bf16[10,6,2,1408]{3,2,1,0:T(2,128)(2,1)S(1)} slice(bf16[10,12,2,1408]{3,2,1,0:T(2,128)(2,1)} %bitcast.5), slice={[0:10], [3:9], [0:2], [0:1408]} | slice | bytes 675840 | tf_op jit(solution)/shard_map/slice | solution.py:321
  5.4 0.1 collective-permute-start.1
  5.5 1.4 %collective-permute-start.6 = (bf16[10,6,2,1408]{3,2,1,0:T(2,128)(2,1)S(1)}, bf16[10,6,2,1408]{3,2,1,0:T(2,128)(2,1)S(1)}, u32[]{:S(2)}, u32[]{:S(2)}) collective-permute-start(bf16[10,6,2,1408]{3,2,1,0:T(2,128)(2,1)S(1)} %slice.3.mid), channel_id=1, source_target_pairs={{0,16},{16,0},{1,17},{17,1},{2,18},{18,2},{3,19},{19,3},{4,20},{20... | collective-permute-start | bytes 1013768 | tf_op jit(solution)/shard_map/ppermute | solution.py:328
  6.9 1.6 %own_mid.1 = (f32[12,2,33,8,128]{4,3,2,1,0:T(8,128)S(1)}, f32[28,16,128]{2,1,0:T(8,128)S(1)}) custom-call(bf16[10,6,2,1408]{3,2,1,0:T(2,128)(2,1)S(1)} %slice.3.mid), custom_call_target="tpu_custom_call" | custom-call | flops 15000000 | bytes 3811328 | tf_op jit(solution)/shard_map/own_mid/pallas_call | solution.py:284
  8.5 0.0 collective-permute-done.far
  8.5 4.5 %collective-permute-start.4 = (bf16[10,3,2,1408]{3,2,1,0:T(2,128)(2,1)S(1)}, bf16[10,3,2,1408]{3,2,1,0:T(2,128)(2,1)S(1)}, u32[]{:S(2)}, u32[]{:S(2)}) collective-permute-start(bf16[10,3,2,1408]{3,2,1,0:T(2,128)(2,1)S(1)} %dynamic-slice_bitcast_fusion.far), channel_id=1, source_target_pairs={{1,2},{2,1},{3,4},{4,3},{5,6},{6,5},{7,8},{8,7},{9,10},{10,9},{11,... | collective-permute-start | bytes 506888 | tf_op jit(solution)/shard_map/ppermute | solution.py:331
  13.1 1.9 %collective-permute-start.5 = (bf16[10,3,2,1408]{3,2,1,0:T(2,128)(2,1)S(1)}, bf16[10,3,2,1408]{3,2,1,0:T(2,128)(2,1)S(1)}, u32[]{:S(2)}, u32[]{:S(2)}) collective-permute-start(bf16[10,3,2,1408]{3,2,1,0:T(2,128)(2,1)S(1)} %collective-permute-done.far), channel_id=1, source_target_pairs={{1,2},{2,1},{3,4},{4,3},{5,6},{6,5},{7,8},{8,7},{9,10},{10,9},{11,... | collective-permute-start | bytes 506888 | tf_op jit(solution)/shard_map/ppermute | solution.py:332
  15.0 1.6 %own_edge.1 = (f32[12,2,33,8,128]{4,3,2,1,0:T(8,128)S(1)}, f32[28,16,128]{2,1,0:T(8,128)S(1)}) custom-call(bf16[10,3,2,1408]{3,2,1,0:T(2,128)(2,1)S(1)} %constant_dynamic-slice_fusion.near, bf16[10,3,2,1408]{3,2,1,0:T(2,128)(2,1)S(1)} %dynamic-slice_bitcast_fusion.far), custom_call_target="tpu_custom_call" | custom-call | flops 15000000 | bytes 3811328 | tf_op jit(solution)/shard_map/own_edge/pallas_call | solution.py:284
  16.6 0.0 collective-permute-done.1.near
  16.6 0.1 collective-permute-start.2
  16.7 0.5 %collective-permute-start.3 = (bf16[10,3,2,1408]{3,2,1,0:T(2,128)(2,1)S(1)}, bf16[10,3,2,1408]{3,2,1,0:T(2,128)(2,1)S(1)}, u32[]{:S(2)}, u32[]{:S(2)}) collective-permute-start(bf16[10,3,2,1408]{3,2,1,0:T(2,128)(2,1)S(1)} %collective-permute-done.1.near), channel_id=1, source_target_pairs={{0,1},{1,0},{2,3},{3,2},{4,5},{5,4},{6,7},{7,6},{8,9},{9,8},{10,11... | collective-permute-start | bytes 506888 | tf_op jit(solution)/shard_map/ppermute | solution.py:337
  17.2 1.8 %cross_edge.1.edges = f32[28,16,128]{2,1,0:T(8,128)S(1)} custom-call(f32[12,2,33,8,128]{4,3,2,1,0:T(8,128)S(1)} %get-tuple-element.42.rep, bf16[10,3,2,1408]{3,2,1,0:T(2,128)(2,1)S(1)} %collective-permute-done.1.near, bf16[10,3,2,1408]{3,2,1,0:T(2,128)(2,1)S(1)} %collective-permute-done.far), custom_call_target="tpu_custom_call" | custom-call | flops 15000000 | bytes 3811328 | tf_op jit(solution)/shard_map/cross_edge/pallas_call | solution.py:284
  19.0 0.0 collective-permute-done.4.far
  19.0 1.8 %collective-permute-done.5.far = bf16[10,3,2,1408]{3,2,1,0:T(2,128)(2,1)S(1)} collective-permute-done((bf16[10,3,2,1408]{3,2,1,0:T(2,128)(2,1)S(1)}, bf16[10,3,2,1408]{3,2,1,0:T(2,128)(2,1)S(1)}, u32[]{:S(2)}, u32[]{:S(2)}) %collective-permute-start.5) | collective-permute-done | bytes 168992 | tf_op jit(solution)/shard_map/ppermute | solution.py:332
  20.8 0.0 collective-permute-done.2.near
  20.8 0.0 collective-permute-done.3.near
  20.8 2.4 %own_halo.1 = (f32[12,2,33,8,128]{4,3,2,1,0:T(8,128)S(1)}, f32[10,8,128]{2,1,0:T(8,128)S(1)}, f32[10,10,8,128]{3,2,1,0:T(8,128)S(1)}) custom-call(bf16[10,3,2,1408]{3,2,1,0:T(2,128)(2,1)S(1)} %collective-permute-done.2.near, bf16[10,3,2,1408]{3,2,1,0:T(2,128)(2,1)S(1)} %collective-permute-done.4.far, f32[28,16,128]{2,1,0:T(8,128)S(1)} %get-tuple-element.39.mids, ...), custom_call_target="tpu_custom_call" | custom-call | flops 15000000 | bytes 4491264 | tf_op jit(solution)/shard_map/own_halo/pallas_call | solution.py:284
  23.2 1.8 %cross_halo.1.halos = f32[28,16,128]{2,1,0:T(8,128)S(1)} custom-call(f32[12,2,33,8,128]{4,3,2,1,0:T(8,128)S(1)} %get-tuple-element.43.rep, bf16[10,3,2,1408]{3,2,1,0:T(2,128)(2,1)S(1)} %collective-permute-done.3.near, bf16[10,3,2,1408]{3,2,1,0:T(2,128)(2,1)S(1)} %collective-permute-done.5.far), custom_call_target="tpu_custom_call" | custom-call | flops 15000000 | bytes 3811328 | tf_op jit(solution)/shard_map/cross_halo/pallas_call | solution.py:284
  25.1 0.0 collective-permute-done.6.mid
  25.1 3.2 %cross_mid.1 = f32[10,20,8,128]{3,2,1,0:T(8,128)} custom-call(f32[12,2,33,8,128]{4,3,2,1,0:T(8,128)S(1)} %get-tuple-element.30.rep, f32[10,8,128]{2,1,0:T(8,128)S(1)} %get-tuple-element.41.own_scale, bf16[10,6,2,1408]{3,2,1,0:T(2,128)(2,1)S(1)} %collective-permute-done.6.mid, f32[28,16,128]{2,1,0:T(8,128)S(1)} %cross_edge.1.edges, ...), custom_call_target="tpu_custom_call" | custom-call | flops 15000000 | bytes 5310464 | tf_op jit(solution)/shard_map/cross_mid/pallas_call | solution.py:284
Async XLA Ops:
  1.0 7.5 %collective-permute-start = (bf16[10,3,2,1408]{3,2,1,0:T(2,128)(2,1)S(1)}, bf16[10,3,2,1408]{3,2,1,0:T(2,128)(2,1)S(1)}, u32[]{:S(2)}, u32[]{:S(2)}) collective-permute-start(bf16[10,3,2,1408]{3,2,1,0:T(2,128)(2,1)S(1)} %dynamic-slice_bitcast_fusion.far), channel_id=1, source_target_pairs={{0,16},{16,0},{1,17},{17,1},{2,18},{18,2},{3,19},{19,3},{4,20},{20... | collective-permute-start | bytes 506888 | tf_op jit(solution)/shard_map/ppermute | solution.py:326
  5.4 11.2 %collective-permute-start.1 = (bf16[10,3,2,1408]{3,2,1,0:T(2,128)(2,1)S(1)}, bf16[10,3,2,1408]{3,2,1,0:T(2,128)(2,1)S(1)}, u32[]{:S(2)}, u32[]{:S(2)}) collective-permute-start(bf16[10,3,2,1408]{3,2,1,0:T(2,128)(2,1)S(1)} %constant_dynamic-slice_fusion.near), channel_id=1, source_target_pairs={{0,16},{16,0},{1,17},{17,1},{2,18},{18,2},{3,19},{19,3},{4,20},{20... | collective-permute-start | bytes 506888 | tf_op jit(solution)/shard_map/ppermute | solution.py:327
  5.5 19.6 %collective-permute-start.6 = (bf16[10,6,2,1408]{3,2,1,0:T(2,128)(2,1)S(1)}, bf16[10,6,2,1408]{3,2,1,0:T(2,128)(2,1)S(1)}, u32[]{:S(2)}, u32[]{:S(2)}) collective-permute-start(bf16[10,6,2,1408]{3,2,1,0:T(2,128)(2,1)S(1)} %slice.3.mid), channel_id=1, source_target_pairs={{0,16},{16,0},{1,17},{17,1},{2,18},{18,2},{3,19},{19,3},{4,20},{20... | collective-permute-start | bytes 1013768 | tf_op jit(solution)/shard_map/ppermute | solution.py:328
  8.5 10.5 %collective-permute-start.4 = (bf16[10,3,2,1408]{3,2,1,0:T(2,128)(2,1)S(1)}, bf16[10,3,2,1408]{3,2,1,0:T(2,128)(2,1)S(1)}, u32[]{:S(2)}, u32[]{:S(2)}) collective-permute-start(bf16[10,3,2,1408]{3,2,1,0:T(2,128)(2,1)S(1)} %dynamic-slice_bitcast_fusion.far), channel_id=1, source_target_pairs={{1,2},{2,1},{3,4},{4,3},{5,6},{6,5},{7,8},{8,7},{9,10},{10,9},{11,... | collective-permute-start | bytes 506888 | tf_op jit(solution)/shard_map/ppermute | solution.py:331
  13.1 7.7 %collective-permute-start.5 = (bf16[10,3,2,1408]{3,2,1,0:T(2,128)(2,1)S(1)}, bf16[10,3,2,1408]{3,2,1,0:T(2,128)(2,1)S(1)}, u32[]{:S(2)}, u32[]{:S(2)}) collective-permute-start(bf16[10,3,2,1408]{3,2,1,0:T(2,128)(2,1)S(1)} %collective-permute-done.far), channel_id=1, source_target_pairs={{1,2},{2,1},{3,4},{4,3},{5,6},{6,5},{7,8},{8,7},{9,10},{10,9},{11,... | collective-permute-start | bytes 506888 | tf_op jit(solution)/shard_map/ppermute | solution.py:332
  16.6 4.2 %collective-permute-start.2 = (bf16[10,3,2,1408]{3,2,1,0:T(2,128)(2,1)S(1)}, bf16[10,3,2,1408]{3,2,1,0:T(2,128)(2,1)S(1)}, u32[]{:S(2)}, u32[]{:S(2)}) collective-permute-start(bf16[10,3,2,1408]{3,2,1,0:T(2,128)(2,1)S(1)} %constant_dynamic-slice_fusion.near), channel_id=1, source_target_pairs={{0,1},{1,0},{2,3},{3,2},{4,5},{5,4},{6,7},{7,6},{8,9},{9,8},{10,11... | collective-permute-start | bytes 506888 | tf_op jit(solution)/shard_map/ppermute | solution.py:336
  16.7 4.1 %collective-permute-start.3 = (bf16[10,3,2,1408]{3,2,1,0:T(2,128)(2,1)S(1)}, bf16[10,3,2,1408]{3,2,1,0:T(2,128)(2,1)S(1)}, u32[]{:S(2)}, u32[]{:S(2)}) collective-permute-start(bf16[10,3,2,1408]{3,2,1,0:T(2,128)(2,1)S(1)} %collective-permute-done.1.near), channel_id=1, source_target_pairs={{0,1},{1,0},{2,3},{3,2},{4,5},{5,4},{6,7},{7,6},{8,9},{9,8},{10,11... | collective-permute-start | bytes 506888 | tf_op jit(solution)/shard_map/ppermute | solution.py:337

commit v5 on v4

v5 whole, which is shorter than its diff:
```python
import functools

import jax
import jax.numpy as jnp
from jax import lax
from jax.experimental import pallas as pl
from jax.experimental.pallas import tpu as pltpu
from jax.sharding import PartitionSpec as P

EPS = 1e-06
LANES = 128
CELL = 11
STEPS = 33
TILE = (8, LANES)
F32 = jnp.float32
VMEM = pltpu.MemorySpace.VMEM


def iota(dim):
    return lax.broadcasted_iota(jnp.int32, TILE, dim)


def put_rows(ref, date, row, flat, q, at):
    pair = ref[date, row].astype(F32)
    for m in range(CELL):
        flat[q, m, at : at + 2, :] = pair[:, m * LANES : (m + 1) * LANES]


def unpack(dates, refs, flat):
    def one(q, carry):
        for part in range(4):
            date = jnp.minimum(4 * q + part, dates - 1)
            for e, (ref, first) in enumerate(refs):
                for sub in range(3):
                    put_rows(ref, date, first + sub, flat, q, part * 12 + e * 6 + sub * 2)
        return carry

    lax.fori_loop(0, (dates + 3) // 4, one, 0)


def rotate(count, flat, cells):
    lane = iota(1)
    turn = lax.rem(lane * 3, CELL)
    bits = [(s, (turn & s) != 0) for s in (1, 2, 4, 8)]

    def one(q, carry):
        for part in range(6):
            v = [flat[q, m, pl.ds(part, 8, stride=6), :] for m in range(CELL)]
            for shift, mask in bits:
                v = [jnp.where(mask, v[(t + shift) % CELL], v[t]) for t in range(CELL)]
            for c in range(CELL):
                cells[q, part % 2, (part // 2) * CELL + c] = v[(8 * c) % CELL]
        return carry

    lax.fori_loop(0, count, one, 0)


def place(count, cells, rep=None):
    lane = iota(1)
    low = iota(0) < 4
    even = (iota(0) & 2) == 0

    def spread(q, ri, s, v):
        a = jnp.where(even, v, pltpu.roll(v, 2, 0))
        b = jnp.where(even, pltpu.roll(v, 6, 0), v)
        c, d = pltpu.roll(a, 4, 0), pltpu.roll(b, 4, 0)
        rep[4 * q, ri, s] = jnp.where(low, a, c)
        rep[4 * q + 1, ri, s] = jnp.where(low, b, d)
        rep[4 * q + 2, ri, s] = jnp.where(low, c, a)
        rep[4 * q + 3, ri, s] = jnp.where(low, d, b)

    for c in range(CELL):
        pick = (lane * CELL + c) & (LANES - 1)

        def one(q, carry):
            for ri in range(2):
                for sub in range(3):
                    s = sub * CELL + c
                    v = jnp.take_along_axis(cells[q, ri, s], pick, axis=1)
                    cells[q, ri, s] = v
                    if rep is not None:
                        spread(q, ri, s, v)
            return carry

        lax.fori_loop(0, count, one, 0, unroll=count)


def products(rows, cols, rep, cells):
    count = len(rows) * len(cols)

    def step(s, acc):
        a = [rep[i, 0, s] for i in rows]
        b = [rep[i, 1, s] for i in rows]
        ab = [x + y for x, y in zip(a, b)]
        acc = list(acc)
        at = 0
        for q in cols:
            c, d = cells[q, 0, s], cells[q, 1, s]
            cd = c - d
            for i in range(len(rows)):
                acc[at] = acc[at] + a[i] * c
                acc[at + 1] = acc[at + 1] + b[i] * d
                acc[at + 2] = acc[at + 2] + ab[i] * cd
                at += 3
        return tuple(acc)

    acc = lax.fori_loop(0, STEPS, step, (jnp.zeros(TILE, F32),) * (3 * count), unroll=11)
    at = 0
    for j in range(len(cols)):
        for i in range(len(rows)):
            p, q, r = acc[at : at + 3]
            yield i, j, p + q, r - p + q
            at += 3


def powers(qs, cells):
    def step(s, acc):
        out = []
        for n, q in enumerate(qs):
            c, d = cells[q, 0, s], cells[q, 1, s]
            out.append(acc[n] + c * c + d * d)
        return tuple(out)

    return lax.fori_loop(0, STEPS, step, (jnp.zeros(TILE, F32),) * len(qs), unroll=11)


def split(first, second):
    even = (iota(0) & 1) == 0
    return (
        jnp.where(even, first, pltpu.roll(second, 1, 0)),
        jnp.where(even, pltpu.roll(first, 7, 0), second),
    )


def odd_strip():
    return iota(0) * 0 + lax.rem(lax.axis_index("strip"), 2) == 1


def put(sums, group, first, second):
    low, high = split(first, second)
    sums[0][group] = low
    sums[1][group] = high
    if len(sums) == 4:
        odd = odd_strip()
        sums[2][group] = jnp.where(odd, low, high)
        sums[3][group] = jnp.where(odd, high, low)


def window(first, count, edges, mids, halos, out):
    lane = iota(1)
    left, right = lane > 0, lane < LANES - 1
    odd = odd_strip()

    def one(n, carry):
        g = first + n
        a, d = (ref[g] for ref in edges)
        b, c = (ref[g] for ref in mids)
        near, far = (ref[g] for ref in halos)
        over, under = jnp.where(odd, near, far), jnp.where(odd, far, near)
        bc = b + c
        for r, v in enumerate((over + (a + b), a + bc, bc + d, (c + d) + under)):
            v = (
                v
                + jnp.where(left, pltpu.roll(v, 1, 1), 0.0)
                + jnp.where(right, pltpu.roll(v, LANES - 1, 1), 0.0)
            )
            out[g, pl.ds(r, 8, stride=4), :] = v
        return carry

    lax.fori_loop(0, count, one, 0, unroll=min(count, 6))


def quads_of(dates):
    return (dates + 3) // 4


def sum_at(out, dates, i, j):
    return out[quads_of(dates) * i + j // 4, 8 * (j % 4) : 8 * (j % 4) + 8, :]


def regroup(dates, refs, flat, cells, rep=None):
    count = quads_of(dates)
    unpack(dates, refs, flat)
    rotate(count, flat, cells)
    place(count, cells, rep)


def put_powers(dates, cells, sums):
    quads = quads_of(dates)
    for q, pw in enumerate(powers(range(quads), cells)):
        put(sums, quads * dates + q, pw, pw)


def own_class(dates, refs, rep, sums, flat, cells):
    quads = quads_of(dates)
    regroup(dates, refs, flat, cells, rep)
    put_powers(dates, cells, sums)
    for b in range(dates // 2):
        picks = range(2 * b // 4, quads)
        for i, j, re, im in products([2 * b, 2 * b + 1], picks, rep, cells):
            put(sums, quads * (2 * b + i) + picks[j], re, im)


def cross_block(dates, b, rep, cells, sums):
    quads = quads_of(dates)
    for i, q, re, im in products([2 * b, 2 * b + 1], range(quads), rep, cells):
        put(sums, quads * (2 * b + i) + q, re, im)


def own_mid_kernel(dates, upper, lower, rep, low, high, flat, cells):
    own_class(dates, ((upper, 0), (lower, 0)), rep, (low, high), flat, cells)


def own_edge_kernel(dates, edge, rep, low, high, near, far, flat, cells):
    own_class(dates, ((edge, 0), (edge, 3)), rep, (low, high, near, far), flat, cells)


def own_final_kernel(dates, a, d, b, c, near, far, scale, coh, out):
    quads = quads_of(dates)
    window(0, quads * (dates + 1), (a, d), (b, c), (near, far), out)
    sign = jnp.where(iota(0) < 4, 1.0, -1.0)
    for j in range(dates):
        scale[j] = lax.rsqrt(sum_at(out, dates, dates, j) + EPS)
    for i in range(dates):
        for j in range(i, dates):
            v = sum_at(out, dates, i, j) * (scale[i] * scale[j])
            coh[i, j] = v
            if j != i:
                coh[j, i] = v * sign


def cross_edge_kernel(dates, rep, edge, low, high, near, far, flat, cells):
    sums = (low, high, near, far)
    regroup(dates, ((edge, 0), (edge, 3)), flat, cells)
    put_powers(dates, cells, sums)

    def one(b, carry):
        cross_block(dates, b, rep, cells, sums)
        return carry

    lax.fori_loop(0, dates // 2, one, 0)


def cross_mid_kernel(dates, rep, upper, lower, low, high, flat, cells):
    sums = (low, high)
    regroup(dates, ((upper, 0), (lower, 0)), flat, cells)
    put_powers(dates, cells, sums)

    def one(b, carry):
        cross_block(dates, b, rep, cells, sums)
        return carry

    lax.fori_loop(0, dates // 2, one, 0)


def last_kernel(dates, count, turn, own_scale, a, d, b, c, near, far, before, out, wide, scale, stage, sem):
    outs = dates // 2
    quads = quads_of(dates)
    me = lax.axis_index("date")
    sources = ((a, d), (b, c), (near, far))
    if turn == 1:
        keep = pltpu.make_async_copy(before, out.at[:, pl.ds(me * dates, dates)], sem.at[outs])
        keep.start()
    window(quads * dates, quads, *sources, wide)
    for j in range(dates):
        scale[j] = lax.rsqrt(sum_at(wide, dates, dates, j) + EPS)
    base = lax.rem(me + count - turn, count) * dates

    def copy(b):
        rows = pl.ds(2 * b, 2)
        return pltpu.make_async_copy(stage.at[rows], out.at[rows, pl.ds(base, dates)], sem.at[b])

    def one(b, carry):
        window(2 * quads * b, 2 * quads, *sources, wide)
        for i in range(2):
            mine = own_scale[2 * b + i]
            for j in range(dates):
                stage[2 * b + i, j] = sum_at(wide, dates, 2 * b + i, j) * (mine * scale[j])
        copy(b).start()
        return carry

    lax.fori_loop(0, outs, one, 0)
    for b in range(outs):
        copy(b).wait()
    if turn == 1:
        keep.wait()


def call(kernel, name, args, outs, scratch=(), flops=0, limit=32, hbm=False, aliases=None):
    vm = pl.BlockSpec(memory_space=VMEM)
    far = pl.BlockSpec(memory_space=pltpu.MemorySpace.HBM)
    ins = [vm] * len(args)
    for n in aliases or {}:
        ins[n] = far
    size = sum(a.size * a.dtype.itemsize for a in (*args, *outs))
    return pl.pallas_call(
        kernel,
        out_shape=tuple(outs),
        in_specs=ins,
        out_specs=(far if hbm else vm,) * len(outs),
        scratch_shapes=list(scratch),
        input_output_aliases=aliases or {},
        compiler_params=pltpu.CompilerParams(vmem_limit_bytes=limit << 20),
        cost_estimate=pl.CostEstimate(flops=flops, bytes_accessed=size, transcendentals=0),
        name=name,
    )(*args)


def per_device(slc):
    dates, _, rows, width = slc.shape
    count = lax.axis_size("date")
    strips = lax.axis_size("strip")
    chip = [(i, i ^ 1) for i in range(strips)]
    chips = [(i, i + 1 if i % 2 else i - 1) for i in range(1, strips - 1)]
    quads = quads_of(dates)
    shape = jax.ShapeDtypeStruct
    sums = shape((quads * (dates + 1), *TILE), F32)
    rep = shape((4 * quads, 2, STEPS, *TILE), F32)
    flat = pltpu.VMEM((quads, CELL, 48, LANES), F32)
    cells = pltpu.VMEM((quads, 2, STEPS, *TILE), F32)
    wide = pltpu.VMEM((quads * (dates + 1), 32, LANES), F32)
    scales = shape((dates, *TILE), F32)
    block = shape((dates, dates, *TILE), F32)

    def run(kernel, name, args, outs, scratch=(flat, cells), **options):
        return call(functools.partial(kernel, dates), name, args, outs, scratch, flops=15_000_000, **options)

    def swap(near, far):
        return lax.ppermute(near, "strip", chip), lax.ppermute(far, "strip", chips)

    x = jnp.transpose(slc, (0, 2, 1, 3))
    triples = x.reshape(dates, rows // 3, 3, 2, width)
    edge = triples[:, :: rows // 3 - 1].reshape(dates, 6, 2, width)
    rings = [[(i, (i + t) % count) for i in range(count)] for t in range(1, count)]
    rows_edge = [lax.ppermute(edge, "date", ring) for ring in rings]
    rep_edge, *own_edges, near, far = run(own_edge_kernel, "own_edge", (edge,), (rep,) + (sums,) * 4)
    x, edge = lax.optimization_barrier((x, edge))
    upper, lower = x[:, 3:6], x[:, 6:9]
    rows_mid = [(lax.ppermute(upper, "date", ring), lax.ppermute(lower, "date", ring)) for ring in rings]
    own_halos = swap(near, far)
    rep_mid, *own_mids = run(own_mid_kernel, "own_mid", (upper, lower), (rep, sums, sums))
    rows_edge, rep_mid = lax.optimization_barrier((rows_edge, rep_mid))
    edges, halos = [], []
    for t in range(1, count):
        *both, near, far = run(cross_edge_kernel, "cross_edge", (rep_edge, rows_edge[t - 1]), (sums,) * 4)
        edges.append(both)
        halos.append(swap(near, far))
    scale, out = run(
        own_final_kernel, "own_final", (*own_edges, *own_mids, *own_halos), (scales, block), (wide,)
    )
    for t in range(1, count):
        inner = run(cross_mid_kernel, "cross_mid", (rep_mid, *rows_mid[t - 1]), (sums, sums))
        (out,) = call(
            functools.partial(last_kernel, dates, count, t),
            "finish",
            (scale, *edges[t - 1], *inner, *halos[t - 1], out),
            (shape((dates, dates * count, *TILE), F32),),
            (
                wide,
                pltpu.VMEM(scales.shape, F32),
                pltpu.VMEM(block.shape, F32),
                pltpu.SemaphoreType.DMA((dates // 2 + 1,)),
            ),
            flops=5_000_000,
            hbm=True,
            aliases={7: 0} if t > 1 else None,
        )
    return out.reshape(dates, dates * count, 2, 4, LANES)


def solution(mesh):
    return jax.shard_map(
        per_device,
        mesh=mesh,
        in_specs=(P("date", None, "strip", None),),
        out_specs=P("date", None, None, "strip", None),
        check_vma=False,
    )
```

time: 28.5 us -> 24.5 us (0.86)
  the two profiles are of different devices: /device:TPU:1 before, /device:TPU:9 now
where the time goes in v5:
time: 24.5 us; the launch traced here: 24.3 us
  starting transfers between devices  11 us (45%)
  Pallas kernels  9.34 us (38%)
  local copies, waits for them, and re-layouts  2.44 us (10%)
  waiting for transfers between devices  1.43 us (6%)
    pallas_call x6, Pallas kernels, call(): pl.pallas_call(kernel, out_shape=tuple(outs), in_specs=ins, out_specs=(fa...  9.34 us
    ppermute x2, starting transfers between devices, swap(): lax.ppermute(far, 'strip', chips)  7.11 us
    ppermute x2, waiting for transfers between devices, swap(): lax.ppermute(far, 'strip', chips)  1.42 us
    ppermute x1, starting transfers between devices, per_device(): rows_edge = [lax.ppermute(edge, 'date', ring) for ring in rings]  1.28 us
    slice x1, local copies, waits for them, and re-layouts, per_device(): upper, lower = (x[:, 3:6], x[:, 6:9])  1.23 us
    ppermute x1, starting transfers between devices, per_device(): lax.ppermute(upper, 'date', ring)  1.21 us
    slice x1, local copies, waits for them, and re-layouts, per_device(): edge = triples[:, ::rows // 3 - 1].reshape(dates, 6, 2, width)  1.21 us
    ppermute x2, starting transfers between devices, swap(): lax.ppermute(near, 'strip', chip)  1.09 us
  transfers between devices with their start and end apart: 7, of which 1 were waited for; matrix products, arithmetic and copies ran while one was open for 5% of the time, Pallas kernels for 32%

profile of v5, /device:TPU:9, one launch (start us, length us, event | category | flops | bytes accessed | tf_op | source)
XLA Modules:
  0.0 24.3 jit_solution(16891626131785769376)
XLA Ops:
  0.0 1.2 %slice.9 = bf16[10,2,3,2,1408]{4,3,2,1,0:T(2,128)(2,1)S(1)} slice(bf16[10,4,3,2,1408]{4,3,2,1,0:T(2,128)(2,1)} %bitcast.7), slice={[0:10:1], [0:4:3], [0:3:1], [0:2:1], [0:1408:1]} | slice | bytes 675840 | tf_op jit(solution)/shard_map/slice | solution.py:333
  1.2 1.3 %collective-permute-start.2 = (bf16[10,6,2,1408]{3,2,1,0:T(2,128)(2,1)S(1)}, bf16[10,6,2,1408]{3,2,1,0:T(2,128)(2,1)S(1)}, u32[]{:S(2)}, u32[]{:S(2)}) collective-permute-start(bf16[10,6,2,1408]{3,2,1,0:T(2,128)(2,1)S(1)} %bitcast.5), channel_id=1, source_target_pairs={{0,16},{16,0},{1,17},{17,1},{2,18},{18,2},{3,19},{19,3},{4,20},{20... | collective-permute-start | bytes 1013768 | tf_op jit(solution)/shard_map/ppermute | solution.py:335
  2.5 1.6 %own_edge.1 = (f32[12,2,33,8,128]{4,3,2,1,0:T(8,128)S(1)}, f32[33,8,128]{2,1,0:T(8,128)S(1)}, f32[33,8,128]{2,1,0:T(8,128)S(1)}, f32[33,8,128]{2,1,0:T(8,128)S(1)}, f32[33,8,128]{2,1,0:T(8,128)S(1)}) custom-call(bf16[10,6,2,1408]{3,2,1,0:T(2,128)(2,1)S(1)} %bitcast.6), custom_call_target="tpu_custom_call" | custom-call | flops 15000000 | bytes 4122624 | tf_op jit(solution)/shard_map/own_edge/pallas_call | solution.py:296
  4.1 1.0 %collective-permute-start = (f32[33,8,128]{2,1,0:T(8,128)S(1)}, f32[33,8,128]{2,1,0:T(8,128)S(1)}, u32[]{:S(2)}, u32[]{:S(2)}) collective-permute-start(f32[33,8,128]{2,1,0:T(8,128)S(1)} %get-tuple-element.29), channel_id=1, source_target_pairs={{0,1},{1,0},{2,3},{3,2},{4,5},{5,4},{6,7},{7,6},{8,9},{9,8},{10,11... | collective-permute-start | bytes 405512 | tf_op jit(solution)/shard_map/ppermute | solution.py:329
  5.1 1.2 %fusion = (bf16[10,3,2,1408]{3,2,1,0:T(2,128)(2,1)S(1)}, bf16[10,3,2,1408]{3,2,1,0:T(2,128)(2,1)S(1)}) fusion(bf16[10,12,2,1408]{3,2,1,0:T(2,128)(2,1)} %bitcast.8), kind=kLoop, calls=%fused_computation | loop fusion | bytes 675840 | tf_op jit(solution)/shard_map/slice | solution.py:338
  6.4 0.3 %collective-permute-start.4 = (bf16[10,3,2,1408]{3,2,1,0:T(2,128)(2,1)S(1)}, bf16[10,3,2,1408]{3,2,1,0:T(2,128)(2,1)S(1)}, u32[]{:S(2)}, u32[]{:S(2)}) collective-permute-start(bf16[10,3,2,1408]{3,2,1,0:T(2,128)(2,1)S(1)} %get-tuple-element.43.lower), channel_id=1, source_target_pairs={{0,16},{16,0},{1,17},{17,1},{2,18},{18,2},{3,19},{19,3},{4,20},{20... | collective-permute-start | bytes 506888 | tf_op jit(solution)/shard_map/ppermute | solution.py:339
  6.7 1.2 %collective-permute-start.3 = (bf16[10,3,2,1408]{3,2,1,0:T(2,128)(2,1)S(1)}, bf16[10,3,2,1408]{3,2,1,0:T(2,128)(2,1)S(1)}, u32[]{:S(2)}, u32[]{:S(2)}) collective-permute-start(bf16[10,3,2,1408]{3,2,1,0:T(2,128)(2,1)S(1)} %get-tuple-element.44.upper), channel_id=1, source_target_pairs={{0,16},{16,0},{1,17},{17,1},{2,18},{18,2},{3,19},{19,3},{4,20},{20... | collective-permute-start | bytes 506888 | tf_op jit(solution)/shard_map/ppermute | solution.py:339
  7.9 3.6 %collective-permute-start.1 = (f32[33,8,128]{2,1,0:T(8,128)S(1)}, f32[33,8,128]{2,1,0:T(8,128)S(1)}, u32[]{:S(2)}, u32[]{:S(2)}) collective-permute-start(f32[33,8,128]{2,1,0:T(8,128)S(1)} %get-tuple-element.30), channel_id=1, source_target_pairs={{1,2},{2,1},{3,4},{4,3},{5,6},{6,5},{7,8},{8,7},{9,10},{10,9},{11,... | collective-permute-start | bytes 405512 | tf_op jit(solution)/shard_map/ppermute | solution.py:329
  11.5 1.6 %own_mid.1 = (f32[12,2,33,8,128]{4,3,2,1,0:T(8,128)S(1)}, f32[33,8,128]{2,1,0:T(8,128)S(1)}, f32[33,8,128]{2,1,0:T(8,128)S(1)}) custom-call(bf16[10,3,2,1408]{3,2,1,0:T(2,128)(2,1)S(1)} %get-tuple-element.44.upper, bf16[10,3,2,1408]{3,2,1,0:T(2,128)(2,1)S(1)} %get-tuple-element.43.lower), custom_call_target="tpu_custom_call" | custom-call | flops 15000000 | bytes 3852288 | tf_op jit(solution)/shard_map/own_mid/pallas_call | solution.py:296
  13.1 0.0 collective-permute-done.2.edge
  13.1 1.9 %cross_edge.1 = (f32[33,8,128]{2,1,0:T(8,128)S(1)}, f32[33,8,128]{2,1,0:T(8,128)S(1)}, f32[33,8,128]{2,1,0:T(8,128)S(1)}, f32[33,8,128]{2,1,0:T(8,128)S(1)}) custom-call(f32[12,2,33,8,128]{4,3,2,1,0:T(8,128)S(1)} %get-tuple-element.32.rep, bf16[10,6,2,1408]{3,2,1,0:T(2,128)(2,1)S(1)} %collective-permute-done.2.edge), custom_call_target="tpu_custom_call" | custom-call | flops 15000000 | bytes 4122624 | tf_op jit(solution)/shard_map/cross_edge/pallas_call | solution.py:296
  15.0 0.1 collective-permute-start.5
  15.0 0.0 collective-permute-done.near
  15.0 3.5 %collective-permute-start.6 = (f32[33,8,128]{2,1,0:T(8,128)S(1)}, f32[33,8,128]{2,1,0:T(8,128)S(1)}, u32[]{:S(2)}, u32[]{:S(2)}) collective-permute-start(f32[33,8,128]{2,1,0:T(8,128)S(1)} %get-tuple-element.41), channel_id=1, source_target_pairs={{1,2},{2,1},{3,4},{4,3},{5,6},{6,5},{7,8},{8,7},{9,10},{10,9},{11,... | collective-permute-start | bytes 405512 | tf_op jit(solution)/shard_map/ppermute | solution.py:329
  18.6 0.0 collective-permute-done.1.far
  18.6 0.9 %own_final.1 = (f32[10,8,128]{2,1,0:T(8,128)S(1)}, f32[10,10,8,128]{3,2,1,0:T(8,128)S(1)}) custom-call(f32[33,8,128]{2,1,0:T(8,128)S(1)} %get-tuple-element.24.a, f32[33,8,128]{2,1,0:T(8,128)S(1)} %get-tuple-element.25.d, f32[33,8,128]{2,1,0:T(8,128)S(1)} %get-tuple-element.27.b, f32[33,8,128]{2,1,0:T(8,128)S(1)} %get-tuple-element.28.c, ...), custom_call_target="tpu_custom_call" | custom-call | flops 15000000 | bytes 1261568 | tf_op jit(solution)/shard_map/own_final/pallas_call | solution.py:296
  19.5 0.0 collective-permute-done.4.lower
  19.5 0.0 collective-permute-done.3.upper
  19.5 1.9 %cross_mid.1 = (f32[33,8,128]{2,1,0:T(8,128)S(1)}, f32[33,8,128]{2,1,0:T(8,128)S(1)}) custom-call(f32[12,2,33,8,128]{4,3,2,1,0:T(8,128)S(1)} %get-tuple-element.37.rep, bf16[10,3,2,1408]{3,2,1,0:T(2,128)(2,1)S(1)} %collective-permute-done.3.upper, bf16[10,3,2,1408]{3,2,1,0:T(2,128)(2,1)S(1)} %collective-permute-done.4.lower), custom_call_target="tpu_custom_call" | custom-call | flops 15000000 | bytes 3852288 | tf_op jit(solution)/shard_map/cross_mid/pallas_call | solution.py:296
  21.4 0.0 collective-permute-done.5.near
  21.4 1.4 %collective-permute-done.6.far = f32[33,8,128]{2,1,0:T(8,128)S(1)} collective-permute-done((f32[33,8,128]{2,1,0:T(8,128)S(1)}, f32[33,8,128]{2,1,0:T(8,128)S(1)}, u32[]{:S(2)}, u32[]{:S(2)}) %collective-permute-start.6) | collective-permute-done | bytes 135200 | tf_op jit(solution)/shard_map/ppermute | solution.py:329
  22.8 1.5 %finish.1 = f32[10,20,8,128]{3,2,1,0:T(8,128)} custom-call(f32[10,8,128]{2,1,0:T(8,128)S(1)} %get-tuple-element.31.own_scale, f32[33,8,128]{2,1,0:T(8,128)S(1)} %get-tuple-element.35.a, f32[33,8,128]{2,1,0:T(8,128)S(1)} %get-tuple-element.36.d, f32[33,8,128]{2,1,0:T(8,128)S(1)} %get-tuple-element.38.b, f32[33,8,128]{2,1,0:T(8,128)S(1)} %get-tuple-element.39.c, ...), custom_call_target="tpu_custom_call" | custom-call | flops 5000000 | bytes 2080768 | tf_op jit(solution)/shard_map/finish/pallas_call | solution.py:296
Async XLA Ops:
  1.2 11.9 %collective-permute-start.2 = (bf16[10,6,2,1408]{3,2,1,0:T(2,128)(2,1)S(1)}, bf16[10,6,2,1408]{3,2,1,0:T(2,128)(2,1)S(1)}, u32[]{:S(2)}, u32[]{:S(2)}) collective-permute-start(bf16[10,6,2,1408]{3,2,1,0:T(2,128)(2,1)S(1)} %bitcast.5), channel_id=1, source_target_pairs={{0,16},{16,0},{1,17},{17,1},{2,18},{18,2},{3,19},{19,3},{4,20},{20... | collective-permute-start | bytes 1013768 | tf_op jit(solution)/shard_map/ppermute | solution.py:335
  4.1 10.9 %collective-permute-start = (f32[33,8,128]{2,1,0:T(8,128)S(1)}, f32[33,8,128]{2,1,0:T(8,128)S(1)}, u32[]{:S(2)}, u32[]{:S(2)}) collective-permute-start(f32[33,8,128]{2,1,0:T(8,128)S(1)} %get-tuple-element.29), channel_id=1, source_target_pairs={{0,1},{1,0},{2,3},{3,2},{4,5},{5,4},{6,7},{7,6},{8,9},{9,8},{10,11... | collective-permute-start | bytes 405512 | tf_op jit(solution)/shard_map/ppermute | solution.py:329
  6.4 13.1 %collective-permute-start.4 = (bf16[10,3,2,1408]{3,2,1,0:T(2,128)(2,1)S(1)}, bf16[10,3,2,1408]{3,2,1,0:T(2,128)(2,1)S(1)}, u32[]{:S(2)}, u32[]{:S(2)}) collective-permute-start(bf16[10,3,2,1408]{3,2,1,0:T(2,128)(2,1)S(1)} %get-tuple-element.43.lower), channel_id=1, source_target_pairs={{0,16},{16,0},{1,17},{17,1},{2,18},{18,2},{3,19},{19,3},{4,20},{20... | collective-permute-start | bytes 506888 | tf_op jit(solution)/shard_map/ppermute | solution.py:339
  6.7 12.8 %collective-permute-start.3 = (bf16[10,3,2,1408]{3,2,1,0:T(2,128)(2,1)S(1)}, bf16[10,3,2,1408]{3,2,1,0:T(2,128)(2,1)S(1)}, u32[]{:S(2)}, u32[]{:S(2)}) collective-permute-start(bf16[10,3,2,1408]{3,2,1,0:T(2,128)(2,1)S(1)} %get-tuple-element.44.upper), channel_id=1, source_target_pairs={{0,16},{16,0},{1,17},{17,1},{2,18},{18,2},{3,19},{19,3},{4,20},{20... | collective-permute-start | bytes 506888 | tf_op jit(solution)/shard_map/ppermute | solution.py:339
  7.9 10.7 %collective-permute-start.1 = (f32[33,8,128]{2,1,0:T(8,128)S(1)}, f32[33,8,128]{2,1,0:T(8,128)S(1)}, u32[]{:S(2)}, u32[]{:S(2)}) collective-permute-start(f32[33,8,128]{2,1,0:T(8,128)S(1)} %get-tuple-element.30), channel_id=1, source_target_pairs={{1,2},{2,1},{3,4},{4,3},{5,6},{6,5},{7,8},{8,7},{9,10},{10,9},{11,... | collective-permute-start | bytes 405512 | tf_op jit(solution)/shard_map/ppermute | solution.py:329
  15.0 6.4 %collective-permute-start.5 = (f32[33,8,128]{2,1,0:T(8,128)S(1)}, f32[33,8,128]{2,1,0:T(8,128)S(1)}, u32[]{:S(2)}, u32[]{:S(2)}) collective-permute-start(f32[33,8,128]{2,1,0:T(8,128)S(1)} %get-tuple-element.40), channel_id=1, source_target_pairs={{0,1},{1,0},{2,3},{3,2},{4,5},{5,4},{6,7},{7,6},{8,9},{9,8},{10,11... | collective-permute-start | bytes 405512 | tf_op jit(solution)/shard_map/ppermute | solution.py:329
  15.0 7.8 %collective-permute-start.6 = (f32[33,8,128]{2,1,0:T(8,128)S(1)}, f32[33,8,128]{2,1,0:T(8,128)S(1)}, u32[]{:S(2)}, u32[]{:S(2)}) collective-permute-start(f32[33,8,128]{2,1,0:T(8,128)S(1)} %get-tuple-element.41), channel_id=1, source_target_pairs={{1,2},{2,1},{3,4},{4,3},{5,6},{6,5},{7,8},{8,7},{9,10},{10,9},{11,... | collective-permute-start | bytes 405512 | tf_op jit(solution)/shard_map/ppermute | solution.py:329

commit v6 on v5

v6 whole, which is shorter than its diff:
```python
import functools

import jax
import jax.numpy as jnp
from jax import lax
from jax.experimental import pallas as pl
from jax.experimental.pallas import tpu as pltpu
from jax.sharding import PartitionSpec as P

EPS = 1e-06
LANES = 128
CELL = 11
STEPS = 33
TILE = (8, LANES)
F32 = jnp.float32
VMEM = pltpu.MemorySpace.VMEM


def iota(dim):
    return lax.broadcasted_iota(jnp.int32, TILE, dim)


def put_rows(ref, date, row, flat, q, at):
    pair = ref[date, row].astype(F32)
    for m in range(CELL):
        flat[q, m, at : at + 2, :] = pair[:, m * LANES : (m + 1) * LANES]


def unpack_mid(dates, mid, flat):
    def one(q, carry):
        for part in range(4):
            date = jnp.minimum(4 * q + part, dates - 1)
            for row in range(6):
                put_rows(mid, date, row, flat, q, part * 12 + row * 2)
        return carry

    lax.fori_loop(0, quads_of(dates), one, 0)


def unpack_edge(dates, own, other, flat):
    for j in range(2 * dates):
        ref, date = (own, j) if j < dates else (other, j - dates)
        for sub in range(3):
            put_rows(ref, date, sub, flat, j // 8, (j % 8) * 6 + sub * 2)


def rotate(count, flat, cells):
    lane = iota(1)
    turn = lax.rem(lane * 3, CELL)
    bits = [(s, (turn & s) != 0) for s in (1, 2, 4, 8)]

    def one(q, carry):
        for part in range(6):
            v = [flat[q, m, pl.ds(part, 8, stride=6), :] for m in range(CELL)]
            for shift, mask in bits:
                v = [jnp.where(mask, v[(t + shift) % CELL], v[t]) for t in range(CELL)]
            for c in range(CELL):
                cells[q, part % 2, (part // 2) * CELL + c] = v[(8 * c) % CELL]
        return carry

    lax.fori_loop(0, count, one, 0)


def place(count, cells, spread=None):
    lane = iota(1)
    for c in range(CELL):
        pick = (lane * CELL + c) & (LANES - 1)

        def one(q, carry):
            for ri in range(2):
                for sub in range(3):
                    s = sub * CELL + c
                    v = jnp.take_along_axis(cells[q, ri, s], pick, axis=1)
                    cells[q, ri, s] = v
                    if spread is not None:
                        spread(q, ri, s, v)
            return carry

        lax.fori_loop(0, count, one, 0, unroll=count)


def spread_mid(rep):
    low = iota(0) < 4
    even = (iota(0) & 2) == 0

    def spread(q, ri, s, v):
        a = jnp.where(even, v, pltpu.roll(v, 2, 0))
        b = jnp.where(even, pltpu.roll(v, 6, 0), v)
        c, d = pltpu.roll(a, 4, 0), pltpu.roll(b, 4, 0)
        rep[4 * q, ri, s] = jnp.where(low, a, c)
        rep[4 * q + 1, ri, s] = jnp.where(low, b, d)
        rep[4 * q + 2, ri, s] = jnp.where(low, c, a)
        rep[4 * q + 3, ri, s] = jnp.where(low, d, b)

    return spread


def spread_edge(dates, cells, rep):
    def one(s, carry):
        for i in range(dates):
            for ri in range(2):
                rep[i, ri, s] = jnp.broadcast_to(cells[i // 8, ri, s, i % 8 : i % 8 + 1, :], TILE)
        return carry

    lax.fori_loop(0, STEPS, one, 0, unroll=3)


def products(rows, cols, rep, cells):
    count = len(rows) * len(cols)

    def step(s, acc):
        a = [rep[i, 0, s] for i in rows]
        b = [rep[i, 1, s] for i in rows]
        ab = [x + y for x, y in zip(a, b)]
        acc = list(acc)
        at = 0
        for q in cols:
            c, d = cells[q, 0, s], cells[q, 1, s]
            cd = c - d
            for i in range(len(rows)):
                acc[at] = acc[at] + a[i] * c
                acc[at + 1] = acc[at + 1] + b[i] * d
                acc[at + 2] = acc[at + 2] + ab[i] * cd
                at += 3
        return tuple(acc)

    acc = lax.fori_loop(0, STEPS, step, (jnp.zeros(TILE, F32),) * (3 * count), unroll=11)
    at = 0
    for j in range(len(cols)):
        for i in range(len(rows)):
            p, q, r = acc[at : at + 3]
            yield i, j, p + q, r - p + q
            at += 3


def powers(qs, cells):
    def step(s, acc):
        out = []
        for n, q in enumerate(qs):
            c, d = cells[q, 0, s], cells[q, 1, s]
            out.append(acc[n] + c * c + d * d)
        return tuple(out)

    return lax.fori_loop(0, STEPS, step, (jnp.zeros(TILE, F32),) * len(qs), unroll=11)


def quads_of(dates):
    return (dates + 3) // 4


def octs_of(dates):
    return (2 * dates + 7) // 8


def edge_kernel(dates, own, other, sums, flat, cells, rep):
    octs = octs_of(dates)
    unpack_edge(dates, own, other, flat)
    rotate(octs, flat, cells)
    place(octs, cells)
    spread_edge(dates, cells, rep)
    for o, pw in enumerate(powers(range(octs), cells)):
        sums[2 * octs * dates + o] = pw

    def one(b, carry):
        for i, o, re, im in products([2 * b, 2 * b + 1], range(octs), rep, cells):
            at = 2 * octs * (2 * b + i) + o
            sums[at] = re
            sums[at + octs] = im
        return carry

    lax.fori_loop(0, dates // 2, one, 0)


def put_mid(dates, rep, cells, sums):
    quads = quads_of(dates)
    for q, pw in enumerate(powers(range(quads), cells)):
        sums[2 * dates, 8 * q : 8 * q + 8, :] = pw

    def one(b, carry):
        for i, q, re, im in products([2 * b, 2 * b + 1], range(quads), rep, cells):
            sums[4 * b + 2 * i, 8 * q : 8 * q + 8, :] = re
            sums[4 * b + 2 * i + 1, 8 * q : 8 * q + 8, :] = im
        return carry

    lax.fori_loop(0, dates // 2, one, 0)


def own_mid_kernel(dates, mid, rep, sums, flat, cells):
    unpack_mid(dates, mid, flat)
    rotate(quads_of(dates), flat, cells)
    place(quads_of(dates), cells, spread_mid(rep))
    put_mid(dates, rep, cells, sums)


def cross_mid_kernel(dates, rep, mid, own, sums, flat, cells, part):
    unpack_mid(dates, mid, flat)
    rotate(quads_of(dates), flat, cells)
    place(quads_of(dates), cells)
    put_mid(dates, rep, cells, part)

    def join(n, carry):
        sums[n, : 2 * dates, :] = own[n, : 2 * dates, :]
        sums[n, 2 * dates : 4 * dates, :] = part[n, : 2 * dates, :]
        return carry

    lax.fori_loop(0, 2 * dates + 1, join, 0, unroll=3)


def window(edges, halos, mids, vreg, mid, octo):
    lane = iota(1)
    odd = iota(0) * 0 + lax.rem(lax.axis_index("strip"), 2) == 1
    near, far = edges[0][vreg], edges[1][vreg]
    near_halo, far_halo = halos[0][vreg], halos[1][vreg]
    a, d = jnp.where(odd, near, far), jnp.where(odd, far, near)
    over, under = jnp.where(odd, near_halo, far_halo), jnp.where(odd, far_halo, near_halo)
    b, c = (mids[mid, pl.ds(16 * octo + e, 8, stride=2), :] for e in range(2))
    bc = b + c
    out = []
    for v in (over + (a + b), a + bc, bc + d, (c + d) + under):
        left = jnp.where(lane > 0, pltpu.roll(v, 1, 1), 0.0)
        right = jnp.where(lane < LANES - 1, pltpu.roll(v, LANES - 1, 1), 0.0)
        out.append(v + left + right)
    return out


def scales(dates, edges, halos, mids, octs, wide, scale):
    total = octs_of(dates)
    for o in octs:
        for r, v in enumerate(window(edges, halos, mids, 2 * total * dates + o, 2 * dates, o)):
            v = lax.rsqrt(v + EPS)
            wide[o, pl.ds(r, 8, stride=8), :] = v
            wide[o, pl.ds(4 + r, 8, stride=8), :] = v
        for j in range(8 * o, min(8 * o + 8, 2 * dates)):
            scale[j] = wide[o, 8 * (j % 8) : 8 * (j % 8) + 8, :]


def sums_of_date(dates, i, edges, halos, mids, octs, wide, at):
    total = octs_of(dates)
    for o in octs:
        for comp in range(2):
            vreg = 2 * total * i + total * comp + o
            for r, v in enumerate(window(edges, halos, mids, vreg, 2 * i + comp, o)):
                wide[at, pl.ds(64 * o + 4 * comp + r, 8, stride=8), :] = v


def early_kernel(dates, near, far, near_halo, far_halo, mids, scale, coh, wide, tall):
    first = min(8, dates)
    edges, halos = (near, far), (near_halo, far_halo)
    scales(dates, edges, halos, mids, range((dates + 7) // 8), wide, scale)

    def one(i, carry):
        sums_of_date(dates, i, edges, halos, mids, [0], tall, i)
        for j in range(first):
            coh[i, j] = tall[i, 8 * j : 8 * j + 8, :] * (scale[i] * scale[j])
        return carry

    lax.fori_loop(0, dates, one, 0, unroll=2)


def last_kernel(
    dates, count, turn, near, far, near_halo, far_halo, mids, before, out, wide, tall, scale, mine, stage, sem
):
    first = min(8, dates)
    octs = octs_of(dates)
    me = lax.axis_index("date")
    base = lax.rem(me + count - turn, count) * dates
    edges, halos = (near, far), (near_halo, far_halo)
    if turn == 1:
        keep = pltpu.make_async_copy(before, out.at[:, pl.ds(me * dates, first)], sem.at[dates])
        keep.start()
    scales(dates, edges, halos, mids, range(octs), wide, scale)

    def copies(b):
        rows = pl.ds(2 * b, 2)
        yield pltpu.make_async_copy(stage.at[rows], out.at[rows, pl.ds(base, dates)], sem.at[b])
        if turn == 1 and dates > first:
            rest = out.at[rows, pl.ds(me * dates + first, dates - first)]
            yield pltpu.make_async_copy(mine.at[rows], rest, sem.at[dates // 2 + b])

    def one(b, carry):
        for i in (2 * b, 2 * b + 1):
            sums_of_date(dates, i, edges, halos, mids, range(1, octs), tall, i)
            for j in range(first, 2 * dates):
                v = tall[i, 8 * j : 8 * j + 8, :] * (scale[i] * scale[j])
                if j < dates:
                    mine[i, j - first] = v
                else:
                    stage[i, j - dates] = v
        for copy in copies(b):
            copy.start()
        return carry

    lax.fori_loop(0, dates // 2, one, 0)
    for b in range(dates // 2):
        for copy in copies(b):
            copy.wait()
    if turn == 1:
        keep.wait()


def call(kernel, name, args, outs, scratch=(), flops=0, limit=32, hbm=False, aliases=None):
    vm = pl.BlockSpec(memory_space=VMEM)
    far = pl.BlockSpec(memory_space=pltpu.MemorySpace.HBM)
    ins = [vm] * len(args)
    for n in aliases or {}:
        ins[n] = far
    size = sum(a.size * a.dtype.itemsize for a in (*args, *outs))
    return pl.pallas_call(
        kernel,
        out_shape=tuple(outs),
        in_specs=ins,
        out_specs=(far if hbm else vm,) * len(outs),
        scratch_shapes=list(scratch),
        input_output_aliases=aliases or {},
        compiler_params=pltpu.CompilerParams(vmem_limit_bytes=limit << 20),
        cost_estimate=pl.CostEstimate(flops=flops, bytes_accessed=size, transcendentals=0),
        name=name,
    )(*args)


def per_device(slc):
    dates, _, rows, width = slc.shape
    count = lax.axis_size("date")
    strips = lax.axis_size("strip")
    chip = [(i, i ^ 1) for i in range(strips)]
    chips = [(i, i + 1 if i % 2 else i - 1) for i in range(1, strips - 1)]
    quads, octs = quads_of(dates), octs_of(dates)
    shape = jax.ShapeDtypeStruct
    edge_sums = shape((octs * (2 * dates + 1), *TILE), F32)
    mid_sums = shape((2 * dates + 1, 16 * ((dates + 7) // 8), LANES), F32)
    all_sums = shape((2 * dates + 1, 16 * octs, LANES), F32)
    rep = shape((4 * quads, 2, STEPS, *TILE), F32)
    wide = pltpu.VMEM((octs, 64, LANES), F32)
    tall = pltpu.VMEM((dates, 64 * octs, LANES), F32)
    first = min(8, dates)
    pairs = shape((dates, first, *TILE), F32)

    def work(n):
        return pltpu.VMEM((n, CELL, 48, LANES), F32), pltpu.VMEM((n, 2, STEPS, *TILE), F32)

    def run(kernel, name, args, outs, scratch):
        return call(functools.partial(kernel, dates), name, args, outs, scratch, flops=15_000_000)

    x = jnp.transpose(slc, (0, 2, 1, 3))
    odd = lax.rem(lax.axis_index("strip"), 2)
    far = lax.dynamic_slice_in_dim(x, odd * (rows - 3), 3, 1)
    x, far = lax.optimization_barrier((x, far))
    near = lax.dynamic_slice_in_dim(x, (1 - odd) * (rows - 3), 3, 1)
    mid = x[:, 3 : rows - 3]
    rings = [[(i, (i + t) % count) for i in range(count)] for t in range(1, count)]
    fars = [lax.ppermute(far, "date", ring) for ring in rings]
    nears = [lax.ppermute(near, "date", ring) for ring in rings]
    middles = [lax.ppermute(mid, "date", ring) for ring in rings]
    rep_mid, own_mid = run(own_mid_kernel, "own_mid", (mid,), (rep, mid_sums), work(quads))
    fars, rep_mid = lax.optimization_barrier((fars, rep_mid))
    edges = []
    for t in range(1, count):
        scratch = (*work(octs), pltpu.VMEM((dates, 2, STEPS, *TILE), F32))
        (far_sums,) = run(edge_kernel, "far_pairs", (far, fars[t - 1]), (edge_sums,), scratch)
        nears[t - 1], far_sums = lax.optimization_barrier((nears[t - 1], far_sums))
        far_halo = lax.ppermute(far_sums, "strip", chips)
        (near_sums,) = run(edge_kernel, "near_pairs", (near, nears[t - 1]), (edge_sums,), scratch)
        near_halo = lax.ppermute(near_sums, "strip", chip)
        edges.append((near_sums, far_sums, near_halo, far_halo))
    _, out = run(
        early_kernel, "early", (*edges[0], own_mid), (shape((8 * ((dates + 7) // 8), *TILE), F32), pairs), (wide, tall)
    )
    middles, out = lax.optimization_barrier((middles, out))
    for t in range(1, count):
        (mids,) = run(
            cross_mid_kernel,
            "cross_mid",
            (rep_mid, middles[t - 1], own_mid),
            (all_sums,),
            (*work(quads), pltpu.VMEM(mid_sums.shape, F32)),
        )
        (out,) = call(
            functools.partial(last_kernel, dates, count, t),
            "finish",
            (*edges[t - 1], mids, out),
            (shape((dates, dates * count, *TILE), F32),),
            (
                wide,
                tall,
                pltpu.VMEM((8 * octs, *TILE), F32),
                pltpu.VMEM((dates, max(1, dates - first), *TILE), F32),
                pltpu.VMEM((dates, dates, *TILE), F32),
                pltpu.SemaphoreType.DMA((dates + 1,)),
            ),
            flops=5_000_000,
            hbm=True,
            aliases={5: 0} if t > 1 else None,
        )
    return out.reshape(dates, dates * count, 2, 4, LANES)


def solution(mesh):
    return jax.shard_map(
        per_device,
        mesh=mesh,
        in_specs=(P("date", None, "strip", None),),
        out_specs=P("date", None, None, "strip", None),
        check_vma=False,
    )
```

time: 24.5 us -> 29.9 us (1.22)
  waiting for transfers between devices: 1.43 us -> 7.35 us
  starting transfers between devices: 11 us -> 8.64 us
  Pallas kernels: 9.34 us -> 10.3 us
  local copies, waits for them, and re-layouts: 2.44 us -> 3.28 us
    ppermute x7 -> x5, waiting for transfers between devices: 1.43 us -> 7.35 us  [the longest x1 7.34 us: per_device(): far_halo = lax.ppermute(far_sums, 'strip', chips)]
    ppermute x7 -> x5, starting transfers between devices: 11 us -> 8.64 us  [the longest x1 3.05 us: per_device(): far_halo = lax.ppermute(far_sums, 'strip', chips)]
    dynamic_slice x0 -> x2, local copies, waits for them, and re-layouts: none -> 2.07 us  [the longest x1 1.04 us: per_device(): near = lax.dynamic_slice_in_dim(x, (1 - odd) * (rows - 3), 3, 1)]
    slice x2 -> x1, local copies, waits for them, and re-layouts: 2.44 us -> 1.21 us  [per_device(): mid = x[:, 3:rows - 3]]
    pallas_call x6, Pallas kernels: 9.34 us -> 10.3 us  [call(): pl.pallas_call(kernel, out_shape=tuple(outs), in_specs=ins, out_specs=(fa...]
  transfers between devices with their start and end apart: 7 -> 5, of which waited for: 1 -> 1; matrix products, arithmetic and copies ran while one was open for 5% -> 8% of each run, Pallas kernels for 32% -> 23%
where the time goes in v6:
time: 29.9 us; the launch traced here: 29.7 us
  Pallas kernels  10.3 us (34%)
  starting transfers between devices  8.64 us (29%)
  waiting for transfers between devices  7.35 us (25%)
  local copies, waits for them, and re-layouts  3.28 us (11%)
    pallas_call x6, Pallas kernels, call(): pl.pallas_call(kernel, out_shape=tuple(outs), in_specs=ins, out_specs=(fa...  10.3 us
    ppermute x1, waiting for transfers between devices, per_device(): far_halo = lax.ppermute(far_sums, 'strip', chips)  7.34 us
    ppermute x1, starting transfers between devices, per_device(): far_halo = lax.ppermute(far_sums, 'strip', chips)  3.05 us
    ppermute x1, starting transfers between devices, per_device(): near_halo = lax.ppermute(near_sums, 'strip', chip)  2.72 us
    ppermute x1, starting transfers between devices, per_device(): fars = [lax.ppermute(far, 'date', ring) for ring in rings]  1.28 us
    ppermute x1, starting transfers between devices, per_device(): middles = [lax.ppermute(mid, 'date', ring) for ring in rings]  1.28 us
    slice x1, local copies, waits for them, and re-layouts, per_device(): mid = x[:, 3:rows - 3]  1.21 us
    dynamic_slice x1, local copies, waits for them, and re-layouts, per_device(): near = lax.dynamic_slice_in_dim(x, (1 - odd) * (rows - 3), 3, 1)  1.04 us
  transfers between devices with their start and end apart: 5, of which 1 were waited for; matrix products, arithmetic and copies ran while one was open for 8% of the time, Pallas kernels for 23%

profile of v6, /device:TPU:9, one launch (start us, length us, event | category | flops | bytes accessed | tf_op | source)
XLA Modules:
  0.0 29.7 jit_solution(11580888375139391800)
XLA Ops:
  0.0 1.0 %dynamic-slice_bitcast_fusion.own = bf16[10,3,2,1408]{3,2,1,0:T(2,128)(2,1)S(1)} fusion(bf16[10,2,12,1408]{3,1,2,0:T(2,128)(2,1)} %param.1, s32[]{:T(128)S(6)} %select_n.6), kind=kLoop, calls=%fused_computation | loop fusion | bytes 337924 | tf_op jit(solution)/shard_map/dynamic_slice | solution.py:346
  1.0 1.3 %collective-permute-start.1 = (bf16[10,3,2,1408]{3,2,1,0:T(2,128)(2,1)S(1)}, bf16[10,3,2,1408]{3,2,1,0:T(2,128)(2,1)S(1)}, u32[]{:S(2)}, u32[]{:S(2)}) collective-permute-start(bf16[10,3,2,1408]{3,2,1,0:T(2,128)(2,1)S(1)} %dynamic-slice_bitcast_fusion.own), channel_id=1, source_target_pairs={{0,16},{16,0},{1,17},{17,1},{2,18},{18,2},{3,19},{19,3},{4,20},{20... | collective-permute-start | bytes 506888 | tf_op jit(solution)/shard_map/ppermute | solution.py:351
  2.3 1.0 %constant_dynamic-slice_fusion.own = bf16[10,3,2,1408]{3,2,1,0:T(2,128)(2,1)S(1)} fusion(bf16[10,12,2,1408]{3,2,1,0:T(2,128)(2,1)} %bitcast.4, s32[]{:T(128)S(6)} %select_n.7), kind=kLoop, calls=%fused_computation.1 | loop fusion | bytes 337924 | tf_op jit(solution)/shard_map/dynamic_slice | solution.py:348
  3.4 0.3 %collective-permute-start = (bf16[10,3,2,1408]{3,2,1,0:T(2,128)(2,1)S(1)}, bf16[10,3,2,1408]{3,2,1,0:T(2,128)(2,1)S(1)}, u32[]{:S(2)}, u32[]{:S(2)}) collective-permute-start(bf16[10,3,2,1408]{3,2,1,0:T(2,128)(2,1)S(1)} %constant_dynamic-slice_fusion.own), channel_id=1, source_target_pairs={{0,16},{16,0},{1,17},{17,1},{2,18},{18,2},{3,19},{19,3},{4,20},{20... | collective-permute-start | bytes 506888 | tf_op jit(solution)/shard_map/ppermute | solution.py:352
  3.7 1.2 %slice.3.mid = bf16[10,6,2,1408]{3,2,1,0:T(2,128)(2,1)S(1)} slice(bf16[10,12,2,1408]{3,2,1,0:T(2,128)(2,1)} %bitcast.5), slice={[0:10], [3:9], [0:2], [0:1408]} | slice | bytes 675840 | tf_op jit(solution)/shard_map/slice | solution.py:349
  4.9 1.3 %collective-permute-start.4 = (bf16[10,6,2,1408]{3,2,1,0:T(2,128)(2,1)S(1)}, bf16[10,6,2,1408]{3,2,1,0:T(2,128)(2,1)S(1)}, u32[]{:S(2)}, u32[]{:S(2)}) collective-permute-start(bf16[10,6,2,1408]{3,2,1,0:T(2,128)(2,1)S(1)} %slice.3.mid), channel_id=1, source_target_pairs={{0,16},{16,0},{1,17},{17,1},{2,18},{18,2},{3,19},{19,3},{4,20},{20... | collective-permute-start | bytes 1013768 | tf_op jit(solution)/shard_map/ppermute | solution.py:353
  6.2 1.8 %own_mid.1 = (f32[12,2,33,8,128]{4,3,2,1,0:T(8,128)S(1)}, f32[21,32,128]{2,1,0:T(8,128)S(1)}) custom-call(bf16[10,6,2,1408]{3,2,1,0:T(2,128)(2,1)S(1)} %slice.3.mid), custom_call_target="tpu_custom_call" | custom-call | flops 15000000 | bytes 3926016 | tf_op jit(solution)/shard_map/own_mid/pallas_call | solution.py:308
  8.0 0.0 collective-permute-done.1.other
  8.0 1.9 %far_pairs.1.far = f32[63,8,128]{2,1,0:T(8,128)S(1)} custom-call(bf16[10,3,2,1408]{3,2,1,0:T(2,128)(2,1)S(1)} %dynamic-slice_bitcast_fusion.own, bf16[10,3,2,1408]{3,2,1,0:T(2,128)(2,1)S(1)} %collective-permute-done.1.other), custom_call_target="tpu_custom_call" | custom-call | flops 15000000 | bytes 595968 | tf_op jit(solution)/shard_map/far_pairs/pallas_call | solution.py:308
  9.9 0.0 collective-permute-done.other
  9.9 1.9 %near_pairs.1.near = f32[63,8,128]{2,1,0:T(8,128)S(1)} custom-call(bf16[10,3,2,1408]{3,2,1,0:T(2,128)(2,1)S(1)} %constant_dynamic-slice_fusion.own, bf16[10,3,2,1408]{3,2,1,0:T(2,128)(2,1)S(1)} %collective-permute-done.other), custom_call_target="tpu_custom_call" | custom-call | flops 15000000 | bytes 595968 | tf_op jit(solution)/shard_map/near_pairs/pallas_call | solution.py:308
  11.9 2.7 %collective-permute-start.2 = (f32[63,8,128]{2,1,0:T(8,128)S(1)}, f32[63,8,128]{2,1,0:T(8,128)S(1)}, u32[]{:S(2)}, u32[]{:S(2)}) collective-permute-start(f32[63,8,128]{2,1,0:T(8,128)S(1)} %near_pairs.1.near), channel_id=1, source_target_pairs={{0,1},{1,0},{2,3},{3,2},{4,5},{5,4},{6,7},{7,6},{8,9},{9,8},{10,11... | collective-permute-start | bytes 774152 | tf_op jit(solution)/shard_map/ppermute | solution.py:363
  14.6 3.0 %collective-permute-start.3 = (f32[63,8,128]{2,1,0:T(8,128)S(1)}, f32[63,8,128]{2,1,0:T(8,128)S(1)}, u32[]{:S(2)}, u32[]{:S(2)}) collective-permute-start(f32[63,8,128]{2,1,0:T(8,128)S(1)} %far_pairs.1.far), channel_id=1, source_target_pairs={{1,2},{2,1},{3,4},{4,3},{5,6},{6,5},{7,8},{8,7},{9,10},{10,9},{11,... | collective-permute-start | bytes 774152 | tf_op jit(solution)/shard_map/ppermute | solution.py:361
  17.7 0.0 collective-permute-done.2.near_halo
  17.7 7.3 %collective-permute-done.3.far_halo = f32[63,8,128]{2,1,0:T(8,128)S(1)} collective-permute-done((f32[63,8,128]{2,1,0:T(8,128)S(1)}, f32[63,8,128]{2,1,0:T(8,128)S(1)}, u32[]{:S(2)}, u32[]{:S(2)}) %collective-permute-start.3) | collective-permute-done | bytes 258080 | tf_op jit(solution)/shard_map/ppermute | solution.py:361
  25.0 1.2 %early.1 = (f32[16,8,128]{2,1,0:T(8,128)}, f32[10,8,8,128]{3,2,1,0:T(8,128)S(1)}) custom-call(f32[63,8,128]{2,1,0:T(8,128)S(1)} %near_pairs.1.near, f32[63,8,128]{2,1,0:T(8,128)S(1)} %far_pairs.1.far, f32[63,8,128]{2,1,0:T(8,128)S(1)} %collective-permute-done.2.near_halo, f32[63,8,128]{2,1,0:T(8,128)S(1)} %collective-permute-done.3.far_halo, ...), custom_call_target="tpu_custom_call" | custom-call | flops 15000000 | bytes 1769472 | tf_op jit(solution)/shard_map/early/pallas_call | solution.py:308
  26.2 0.0 collective-permute-done.4.mid
  26.2 1.8 %cross_mid.1.mids = f32[21,48,128]{2,1,0:T(8,128)S(1)} custom-call(f32[12,2,33,8,128]{4,3,2,1,0:T(8,128)S(1)} %get-tuple-element.22.rep, bf16[10,6,2,1408]{3,2,1,0:T(2,128)(2,1)S(1)} %collective-permute-done.4.mid, f32[21,32,128]{2,1,0:T(8,128)S(1)} %get-tuple-element.23.mids.own), custom_call_target="tpu_custom_call" | custom-call | flops 15000000 | bytes 4442112 | tf_op jit(solution)/shard_map/cross_mid/pallas_call | solution.py:308
  28.0 1.6 %finish.1 = f32[10,20,8,128]{3,2,1,0:T(8,128)} custom-call(f32[63,8,128]{2,1,0:T(8,128)S(1)} %near_pairs.1.near, f32[63,8,128]{2,1,0:T(8,128)S(1)} %far_pairs.1.far, f32[63,8,128]{2,1,0:T(8,128)S(1)} %collective-permute-done.2.near_halo, f32[63,8,128]{2,1,0:T(8,128)S(1)} %collective-permute-done.3.far_halo, f32[21,48,128]{2,1,0:T(8,128)S(1)} %cross_mid.1.mids, ...), custom_call_target="tpu_custom_call" | custom-call | flops 5000000 | bytes 2695168 | tf_op jit(solution)/shard_map/finish/pallas_call | solution.py:308
Async XLA Ops:
  1.0 6.9 %collective-permute-start.1 = (bf16[10,3,2,1408]{3,2,1,0:T(2,128)(2,1)S(1)}, bf16[10,3,2,1408]{3,2,1,0:T(2,128)(2,1)S(1)}, u32[]{:S(2)}, u32[]{:S(2)}) collective-permute-start(bf16[10,3,2,1408]{3,2,1,0:T(2,128)(2,1)S(1)} %dynamic-slice_bitcast_fusion.own), channel_id=1, source_target_pairs={{0,16},{16,0},{1,17},{17,1},{2,18},{18,2},{3,19},{19,3},{4,20},{20... | collective-permute-start | bytes 506888 | tf_op jit(solution)/shard_map/ppermute | solution.py:351
  3.4 6.6 %collective-permute-start = (bf16[10,3,2,1408]{3,2,1,0:T(2,128)(2,1)S(1)}, bf16[10,3,2,1408]{3,2,1,0:T(2,128)(2,1)S(1)}, u32[]{:S(2)}, u32[]{:S(2)}) collective-permute-start(bf16[10,3,2,1408]{3,2,1,0:T(2,128)(2,1)S(1)} %constant_dynamic-slice_fusion.own), channel_id=1, source_target_pairs={{0,16},{16,0},{1,17},{17,1},{2,18},{18,2},{3,19},{19,3},{4,20},{20... | collective-permute-start | bytes 506888 | tf_op jit(solution)/shard_map/ppermute | solution.py:352
  4.9 21.3 %collective-permute-start.4 = (bf16[10,6,2,1408]{3,2,1,0:T(2,128)(2,1)S(1)}, bf16[10,6,2,1408]{3,2,1,0:T(2,128)(2,1)S(1)}, u32[]{:S(2)}, u32[]{:S(2)}) collective-permute-start(bf16[10,6,2,1408]{3,2,1,0:T(2,128)(2,1)S(1)} %slice.3.mid), channel_id=1, source_target_pairs={{0,16},{16,0},{1,17},{17,1},{2,18},{18,2},{3,19},{19,3},{4,20},{20... | collective-permute-start | bytes 1013768 | tf_op jit(solution)/shard_map/ppermute | solution.py:353
  11.9 5.8 %collective-permute-start.2 = (f32[63,8,128]{2,1,0:T(8,128)S(1)}, f32[63,8,128]{2,1,0:T(8,128)S(1)}, u32[]{:S(2)}, u32[]{:S(2)}) collective-permute-start(f32[63,8,128]{2,1,0:T(8,128)S(1)} %near_pairs.1.near), channel_id=1, source_target_pairs={{0,1},{1,0},{2,3},{3,2},{4,5},{5,4},{6,7},{7,6},{8,9},{9,8},{10,11... | collective-permute-start | bytes 774152 | tf_op jit(solution)/shard_map/ppermute | solution.py:363
  14.6 10.4 %collective-permute-start.3 = (f32[63,8,128]{2,1,0:T(8,128)S(1)}, f32[63,8,128]{2,1,0:T(8,128)S(1)}, u32[]{:S(2)}, u32[]{:S(2)}) collective-permute-start(f32[63,8,128]{2,1,0:T(8,128)S(1)} %far_pairs.1.far), channel_id=1, source_target_pairs={{1,2},{2,1},{3,4},{4,3},{5,6},{6,5},{7,8},{8,7},{9,10},{10,9},{11,... | collective-permute-start | bytes 774152 | tf_op jit(solution)/shard_map/ppermute | solution.py:361

commit v7 on v6

--- a/solution.py
+++ b/solution.py
@@ -351,21 +351,21 @@
     fars = [lax.ppermute(far, "date", ring) for ring in rings]
     nears = [lax.ppermute(near, "date", ring) for ring in rings]
     middles = [lax.ppermute(mid, "date", ring) for ring in rings]
-    rep_mid, own_mid = run(own_mid_kernel, "own_mid", (mid,), (rep, mid_sums), work(quads))
-    fars, rep_mid = lax.optimization_barrier((fars, rep_mid))
     edges = []
     for t in range(1, count):
         scratch = (*work(octs), pltpu.VMEM((dates, 2, STEPS, *TILE), F32))
         (far_sums,) = run(edge_kernel, "far_pairs", (far, fars[t - 1]), (edge_sums,), scratch)
-        nears[t - 1], far_sums = lax.optimization_barrier((nears[t - 1], far_sums))
         far_halo = lax.ppermute(far_sums, "strip", chips)
+        if t == 1:
+            own_rows, far_sums = lax.optimization_barrier((mid, far_sums))
+            rep_mid, own_mid = run(own_mid_kernel, "own_mid", (own_rows,), (rep, mid_sums), work(quads))
+            nears, rep_mid = lax.optimization_barrier((nears, rep_mid))
         (near_sums,) = run(edge_kernel, "near_pairs", (near, nears[t - 1]), (edge_sums,), scratch)
         near_halo = lax.ppermute(near_sums, "strip", chip)
         edges.append((near_sums, far_sums, near_halo, far_halo))
     _, out = run(
         early_kernel, "early", (*edges[0], own_mid), (shape((8 * ((dates + 7) // 8), *TILE), F32), pairs), (wide, tall)
     )
-    middles, out = lax.optimization_barrier((middles, out))
     for t in range(1, count):
         (mids,) = run(
             cross_mid_kernel,

time: 29.9 us -> 24.1 us (0.81)
  the two profiles are of different devices: /device:TPU:9 before, /device:TPU:0 now
where the time goes in v7:
time: 24.1 us; the launch traced here: 23.9 us
  Pallas kernels  10.4 us (43%)
  starting transfers between devices  9.34 us (39%)
  local copies, waits for them, and re-layouts  3.28 us (14%)
  waiting for transfers between devices  0.87 us (4%)
    pallas_call x6, Pallas kernels, call(): pl.pallas_call(kernel, out_shape=tuple(outs), in_specs=ins, out_specs=(fa...  10.4 us
    ppermute x1, starting transfers between devices, per_device(): near_halo = lax.ppermute(near_sums, 'strip', chip)  3.5 us
    ppermute x1, starting transfers between devices, per_device(): fars = [lax.ppermute(far, 'date', ring) for ring in rings]  3 us
    ppermute x1, starting transfers between devices, per_device(): middles = [lax.ppermute(mid, 'date', ring) for ring in rings]  2.06 us
    slice x1, local copies, waits for them, and re-layouts, per_device(): mid = x[:, 3:rows - 3]  1.21 us
    dynamic_slice x1, local copies, waits for them, and re-layouts, per_device(): far = lax.dynamic_slice_in_dim(x, odd * (rows - 3), 3, 1)  1.04 us
    dynamic_slice x1, local copies, waits for them, and re-layouts, per_device(): near = lax.dynamic_slice_in_dim(x, (1 - odd) * (rows - 3), 3, 1)  1.04 us
    ppermute x1, waiting for transfers between devices, per_device(): fars = [lax.ppermute(far, 'date', ring) for ring in rings]  0.73 us
  transfers between devices with their start and end apart: 5, of which 2 were waited for; matrix products, arithmetic and copies ran while one was open for 9% of the time, Pallas kernels for 31%

profile of v7, /device:TPU:0, one launch (start us, length us, event | category | flops | bytes accessed | tf_op | source)
XLA Modules:
  0.0 23.9 jit_solution(1499941452721210435)
XLA Ops:
  0.0 1.0 %dynamic-slice_bitcast_fusion.own = bf16[10,3,2,1408]{3,2,1,0:T(2,128)(2,1)S(1)} fusion(bf16[10,2,12,1408]{3,1,2,0:T(2,128)(2,1)} %param.1, s32[]{:T(128)S(6)} %select_n.6), kind=kLoop, calls=%fused_computation | loop fusion | bytes 337924 | tf_op jit(solution)/shard_map/dynamic_slice | solution.py:346
  1.0 3.0 %collective-permute-start.1 = (bf16[10,3,2,1408]{3,2,1,0:T(2,128)(2,1)S(1)}, bf16[10,3,2,1408]{3,2,1,0:T(2,128)(2,1)S(1)}, u32[]{:S(2)}, u32[]{:S(2)}) collective-permute-start(bf16[10,3,2,1408]{3,2,1,0:T(2,128)(2,1)S(1)} %dynamic-slice_bitcast_fusion.own), channel_id=1, source_target_pairs={{0,16},{16,0},{1,17},{17,1},{2,18},{18,2},{3,19},{19,3},{4,20},{20... | collective-permute-start | bytes 506888 | tf_op jit(solution)/shard_map/ppermute | solution.py:351
  4.0 1.0 %constant_dynamic-slice_fusion.own = bf16[10,3,2,1408]{3,2,1,0:T(2,128)(2,1)S(1)} fusion(bf16[10,12,2,1408]{3,2,1,0:T(2,128)(2,1)} %bitcast.4, s32[]{:T(128)S(6)} %select_n.7), kind=kLoop, calls=%fused_computation.1 | loop fusion | bytes 337924 | tf_op jit(solution)/shard_map/dynamic_slice | solution.py:348
  5.1 0.1 collective-permute-start
  5.2 1.2 %slice.3.mid = bf16[10,6,2,1408]{3,2,1,0:T(2,128)(2,1)S(1)} slice(bf16[10,12,2,1408]{3,2,1,0:T(2,128)(2,1)} %bitcast.5), slice={[0:10], [3:9], [0:2], [0:1408]} | slice | bytes 675840 | tf_op jit(solution)/shard_map/slice | solution.py:349
  6.4 2.1 %collective-permute-start.4 = (bf16[10,6,2,1408]{3,2,1,0:T(2,128)(2,1)S(1)}, bf16[10,6,2,1408]{3,2,1,0:T(2,128)(2,1)S(1)}, u32[]{:S(2)}, u32[]{:S(2)}) collective-permute-start(bf16[10,6,2,1408]{3,2,1,0:T(2,128)(2,1)S(1)} %slice.3.mid), channel_id=1, source_target_pairs={{0,16},{16,0},{1,17},{17,1},{2,18},{18,2},{3,19},{19,3},{4,20},{20... | collective-permute-start | bytes 1013768 | tf_op jit(solution)/shard_map/ppermute | solution.py:353
  8.5 0.7 %collective-permute-done.1.other = bf16[10,3,2,1408]{3,2,1,0:T(2,128)(2,1)S(1)} collective-permute-done((bf16[10,3,2,1408]{3,2,1,0:T(2,128)(2,1)S(1)}, bf16[10,3,2,1408]{3,2,1,0:T(2,128)(2,1)S(1)}, u32[]{:S(2)}, u32[]{:S(2)}) %collective-permute-start.1) | collective-permute-done | bytes 168992 | tf_op jit(solution)/shard_map/ppermute | solution.py:351
  9.2 1.9 %far_pairs.1.far = f32[63,8,128]{2,1,0:T(8,128)S(1)} custom-call(bf16[10,3,2,1408]{3,2,1,0:T(2,128)(2,1)S(1)} %dynamic-slice_bitcast_fusion.own, bf16[10,3,2,1408]{3,2,1,0:T(2,128)(2,1)S(1)} %collective-permute-done.1.other), custom_call_target="tpu_custom_call" | custom-call | flops 15000000 | bytes 595968 | tf_op jit(solution)/shard_map/far_pairs/pallas_call | solution.py:308
  11.1 0.7 %collective-permute-start.3 = (f32[63,8,128]{2,1,0:T(8,128)S(1)}, f32[63,8,128]{2,1,0:T(8,128)S(1)}, u32[]{:S(2)}, u32[]{:S(2)}) collective-permute-start(f32[63,8,128]{2,1,0:T(8,128)S(1)} %far_pairs.1.far), channel_id=1, source_target_pairs={{1,2},{2,1},{3,4},{4,3},{5,6},{6,5},{7,8},{8,7},{9,10},{10,9},{11,... | collective-permute-start | bytes 774152 | tf_op jit(solution)/shard_map/ppermute | solution.py:358
  11.8 1.8 %own_mid.1 = (f32[12,2,33,8,128]{4,3,2,1,0:T(8,128)S(1)}, f32[21,32,128]{2,1,0:T(8,128)S(1)}) custom-call(bf16[10,6,2,1408]{3,2,1,0:T(2,128)(2,1)S(1)} %slice.3.mid), custom_call_target="tpu_custom_call" | custom-call | flops 15000000 | bytes 3926016 | tf_op jit(solution)/shard_map/own_mid/pallas_call | solution.py:308
  13.6 0.0 collective-permute-done.other
  13.6 1.9 %near_pairs.1.near = f32[63,8,128]{2,1,0:T(8,128)S(1)} custom-call(bf16[10,3,2,1408]{3,2,1,0:T(2,128)(2,1)S(1)} %constant_dynamic-slice_fusion.own, bf16[10,3,2,1408]{3,2,1,0:T(2,128)(2,1)S(1)} %collective-permute-done.other), custom_call_target="tpu_custom_call" | custom-call | flops 15000000 | bytes 595968 | tf_op jit(solution)/shard_map/near_pairs/pallas_call | solution.py:308
  15.6 3.5 %collective-permute-start.2 = (f32[63,8,128]{2,1,0:T(8,128)S(1)}, f32[63,8,128]{2,1,0:T(8,128)S(1)}, u32[]{:S(2)}, u32[]{:S(2)}) collective-permute-start(f32[63,8,128]{2,1,0:T(8,128)S(1)} %near_pairs.1.near), channel_id=1, source_target_pairs={{0,1},{1,0},{2,3},{3,2},{4,5},{5,4},{6,7},{7,6},{8,9},{9,8},{10,11... | collective-permute-start | bytes 774152 | tf_op jit(solution)/shard_map/ppermute | solution.py:364
  19.1 0.1 collective-permute-done.4.mid
  19.2 1.8 %cross_mid.1.mids = f32[21,48,128]{2,1,0:T(8,128)S(1)} custom-call(f32[12,2,33,8,128]{4,3,2,1,0:T(8,128)S(1)} %get-tuple-element.20.rep, bf16[10,6,2,1408]{3,2,1,0:T(2,128)(2,1)S(1)} %collective-permute-done.4.mid, f32[21,32,128]{2,1,0:T(8,128)S(1)} %get-tuple-element.21.own.mids), custom_call_target="tpu_custom_call" | custom-call | flops 15000000 | bytes 4442112 | tf_op jit(solution)/shard_map/cross_mid/pallas_call | solution.py:308
  21.0 0.0 collective-permute-done.3.far_halo
  21.0 0.0 collective-permute-done.2.near_halo
  21.1 1.2 %early.1 = (f32[16,8,128]{2,1,0:T(8,128)}, f32[10,8,8,128]{3,2,1,0:T(8,128)S(1)}) custom-call(f32[63,8,128]{2,1,0:T(8,128)S(1)} %near_pairs.1.near, f32[63,8,128]{2,1,0:T(8,128)S(1)} %far_pairs.1.far, f32[63,8,128]{2,1,0:T(8,128)S(1)} %collective-permute-done.2.near_halo, f32[63,8,128]{2,1,0:T(8,128)S(1)} %collective-permute-done.3.far_halo, ...), custom_call_target="tpu_custom_call" | custom-call | flops 15000000 | bytes 1769472 | tf_op jit(solution)/shard_map/early/pallas_call | solution.py:308
  22.3 1.6 %finish.1 = f32[10,20,8,128]{3,2,1,0:T(8,128)} custom-call(f32[63,8,128]{2,1,0:T(8,128)S(1)} %near_pairs.1.near, f32[63,8,128]{2,1,0:T(8,128)S(1)} %far_pairs.1.far, f32[63,8,128]{2,1,0:T(8,128)S(1)} %collective-permute-done.2.near_halo, f32[63,8,128]{2,1,0:T(8,128)S(1)} %collective-permute-done.3.far_halo, f32[21,48,128]{2,1,0:T(8,128)S(1)} %cross_mid.1.mids, ...), custom_call_target="tpu_custom_call" | custom-call | flops 5000000 | bytes 2695168 | tf_op jit(solution)/shard_map/finish/pallas_call | solution.py:308
Async XLA Ops:
  1.0 8.1 %collective-permute-start.1 = (bf16[10,3,2,1408]{3,2,1,0:T(2,128)(2,1)S(1)}, bf16[10,3,2,1408]{3,2,1,0:T(2,128)(2,1)S(1)}, u32[]{:S(2)}, u32[]{:S(2)}) collective-permute-start(bf16[10,3,2,1408]{3,2,1,0:T(2,128)(2,1)S(1)} %dynamic-slice_bitcast_fusion.own), channel_id=1, source_target_pairs={{0,16},{16,0},{1,17},{17,1},{2,18},{18,2},{3,19},{19,3},{4,20},{20... | collective-permute-start | bytes 506888 | tf_op jit(solution)/shard_map/ppermute | solution.py:351
  5.1 8.5 %collective-permute-start = (bf16[10,3,2,1408]{3,2,1,0:T(2,128)(2,1)S(1)}, bf16[10,3,2,1408]{3,2,1,0:T(2,128)(2,1)S(1)}, u32[]{:S(2)}, u32[]{:S(2)}) collective-permute-start(bf16[10,3,2,1408]{3,2,1,0:T(2,128)(2,1)S(1)} %constant_dynamic-slice_fusion.own), channel_id=1, source_target_pairs={{0,16},{16,0},{1,17},{17,1},{2,18},{18,2},{3,19},{19,3},{4,20},{20... | collective-permute-start | bytes 506888 | tf_op jit(solution)/shard_map/ppermute | solution.py:352
  6.4 12.8 %collective-permute-start.4 = (bf16[10,6,2,1408]{3,2,1,0:T(2,128)(2,1)S(1)}, bf16[10,6,2,1408]{3,2,1,0:T(2,128)(2,1)S(1)}, u32[]{:S(2)}, u32[]{:S(2)}) collective-permute-start(bf16[10,6,2,1408]{3,2,1,0:T(2,128)(2,1)S(1)} %slice.3.mid), channel_id=1, source_target_pairs={{0,16},{16,0},{1,17},{17,1},{2,18},{18,2},{3,19},{19,3},{4,20},{20... | collective-permute-start | bytes 1013768 | tf_op jit(solution)/shard_map/ppermute | solution.py:353
  11.1 9.9 %collective-permute-start.3 = (f32[63,8,128]{2,1,0:T(8,128)S(1)}, f32[63,8,128]{2,1,0:T(8,128)S(1)}, u32[]{:S(2)}, u32[]{:S(2)}) collective-permute-start(f32[63,8,128]{2,1,0:T(8,128)S(1)} %far_pairs.1.far), channel_id=1, source_target_pairs={{1,2},{2,1},{3,4},{4,3},{5,6},{6,5},{7,8},{8,7},{9,10},{10,9},{11,... | collective-permute-start | bytes 774152 | tf_op jit(solution)/shard_map/ppermute | solution.py:358
  15.6 5.5 %collective-permute-start.2 = (f32[63,8,128]{2,1,0:T(8,128)S(1)}, f32[63,8,128]{2,1,0:T(8,128)S(1)}, u32[]{:S(2)}, u32[]{:S(2)}) collective-permute-start(f32[63,8,128]{2,1,0:T(8,128)S(1)} %near_pairs.1.near), channel_id=1, source_target_pairs={{0,1},{1,0},{2,3},{3,2},{4,5},{5,4},{6,7},{7,6},{8,9},{9,8},{10,11... | collective-permute-start | bytes 774152 | tf_op jit(solution)/shard_map/ppermute | solution.py:364

commit v8 on v7

--- a/solution.py
+++ b/solution.py
@@ -95,22 +95,12 @@
     return spread
 
 
-def spread_edge(dates, cells, rep):
-    def one(s, carry):
-        for i in range(dates):
-            for ri in range(2):
-                rep[i, ri, s] = jnp.broadcast_to(cells[i // 8, ri, s, i % 8 : i % 8 + 1, :], TILE)
-        return carry
-
-    lax.fori_loop(0, STEPS, one, 0, unroll=3)
-
-
-def products(rows, cols, rep, cells):
+def products(rows, cols, load, cells):
     count = len(rows) * len(cols)
 
     def step(s, acc):
-        a = [rep[i, 0, s] for i in rows]
-        b = [rep[i, 1, s] for i in rows]
+        a = [load(i, 0, s) for i in rows]
+        b = [load(i, 1, s) for i in rows]
         ab = [x + y for x, y in zip(a, b)]
         acc = list(acc)
         at = 0
@@ -152,23 +142,22 @@
     return (2 * dates + 7) // 8
 
 
-def edge_kernel(dates, own, other, sums, flat, cells, rep):
+def edge_kernel(dates, own, other, sums, flat, cells):
     octs = octs_of(dates)
     unpack_edge(dates, own, other, flat)
     rotate(octs, flat, cells)
     place(octs, cells)
-    spread_edge(dates, cells, rep)
     for o, pw in enumerate(powers(range(octs), cells)):
         sums[2 * octs * dates + o] = pw
 
-    def one(b, carry):
-        for i, o, re, im in products([2 * b, 2 * b + 1], range(octs), rep, cells):
+    def load(i, ri, s):
+        return cells[i // 8, ri, s, pl.ds(i % 8, 8, stride=0), :]
+
+    for b in range(dates // 2):
+        for i, o, re, im in products([2 * b, 2 * b + 1], range(octs), load, cells):
             at = 2 * octs * (2 * b + i) + o
             sums[at] = re
             sums[at + octs] = im
-        return carry
-
-    lax.fori_loop(0, dates // 2, one, 0)
 
 
 def put_mid(dates, rep, cells, sums):
@@ -177,7 +166,7 @@
         sums[2 * dates, 8 * q : 8 * q + 8, :] = pw
 
     def one(b, carry):
-        for i, q, re, im in products([2 * b, 2 * b + 1], range(quads), rep, cells):
+        for i, q, re, im in products([2 * b, 2 * b + 1], range(quads), lambda i, ri, s: rep[i, ri, s], cells):
             sums[4 * b + 2 * i, 8 * q : 8 * q + 8, :] = re
             sums[4 * b + 2 * i + 1, 8 * q : 8 * q + 8, :] = im
         return carry
@@ -347,20 +336,20 @@
     x, far = lax.optimization_barrier((x, far))
     near = lax.dynamic_slice_in_dim(x, (1 - odd) * (rows - 3), 3, 1)
     mid = x[:, 3 : rows - 3]
+    near, mid = lax.optimization_barrier((near, mid))
     rings = [[(i, (i + t) % count) for i in range(count)] for t in range(1, count)]
     fars = [lax.ppermute(far, "date", ring) for ring in rings]
     nears = [lax.ppermute(near, "date", ring) for ring in rings]
     middles = [lax.ppermute(mid, "date", ring) for ring in rings]
     edges = []
     for t in range(1, count):
-        scratch = (*work(octs), pltpu.VMEM((dates, 2, STEPS, *TILE), F32))
-        (far_sums,) = run(edge_kernel, "far_pairs", (far, fars[t - 1]), (edge_sums,), scratch)
+        (far_sums,) = run(edge_kernel, "far_pairs", (far, fars[t - 1]), (edge_sums,), work(octs))
         far_halo = lax.ppermute(far_sums, "strip", chips)
         if t == 1:
             own_rows, far_sums = lax.optimization_barrier((mid, far_sums))
             rep_mid, own_mid = run(own_mid_kernel, "own_mid", (own_rows,), (rep, mid_sums), work(quads))
             nears, rep_mid = lax.optimization_barrier((nears, rep_mid))
-        (near_sums,) = run(edge_kernel, "near_pairs", (near, nears[t - 1]), (edge_sums,), scratch)
+        (near_sums,) = run(edge_kernel, "near_pairs", (near, nears[t - 1]), (edge_sums,), work(octs))
         near_halo = lax.ppermute(near_sums, "strip", chip)
         edges.append((near_sums, far_sums, near_halo, far_halo))
     _, out = run(

time: 24.1 us -> 24.3 us (level)
  waiting for transfers between devices: 0.87 us -> 2.98 us
  starting transfers between devices: 9.34 us -> 7.92 us
  Pallas kernels: 10.4 us -> 9.84 us
    ppermute x1, waiting for transfers between devices: 0.13 us -> 1.95 us  [per_device(): middles = [lax.ppermute(mid, 'date', ring) for ring in rings]]
    ppermute x1, starting transfers between devices: 3.5 us -> 2.14 us  [per_device(): near_halo = lax.ppermute(near_sums, 'strip', chip)]
    ppermute x1, waiting for transfers between devices: 0.01 us -> 0.66 us  [per_device(): nears = [lax.ppermute(near, 'date', ring) for ring in rings]]
    pallas_call x6, Pallas kernels: 10.4 us -> 9.84 us  [call(): pl.pallas_call(kernel, out_shape=tuple(outs), in_specs=ins, out_specs=(fa...]
    ppermute x1, waiting for transfers between devices: 0.73 us -> 0.36 us  [per_device(): fars = [lax.ppermute(far, 'date', ring) for ring in rings]]
  transfers between devices with their start and end apart: 5 -> 5, of which waited for: 2 -> 3; matrix products, arithmetic and copies ran while one was open for 9% -> 9% of each run, Pallas kernels for 31% -> 29%
where the time goes in v8:
time: 24.3 us; the launch traced here: 24.1 us
  Pallas kernels  9.84 us (40%)
  starting transfers between devices  7.92 us (33%)
  local copies, waits for them, and re-layouts  3.29 us (14%)
  waiting for transfers between devices  2.98 us (12%)
    pallas_call x6, Pallas kernels, call(): pl.pallas_call(kernel, out_shape=tuple(outs), in_specs=ins, out_specs=(fa...  9.84 us
    ppermute x1, starting transfers between devices, per_device(): fars = [lax.ppermute(far, 'date', ring) for ring in rings]  3 us
    ppermute x1, starting transfers between devices, per_device(): near_halo = lax.ppermute(near_sums, 'strip', chip)  2.14 us
    ppermute x1, starting transfers between devices, per_device(): middles = [lax.ppermute(mid, 'date', ring) for ring in rings]  2 us
    ppermute x1, waiting for transfers between devices, per_device(): middles = [lax.ppermute(mid, 'date', ring) for ring in rings]  1.95 us
    slice x1, local copies, waits for them, and re-layouts, per_device(): mid = x[:, 3:rows - 3]  1.22 us
    dynamic_slice x1, local copies, waits for them, and re-layouts, per_device(): far = lax.dynamic_slice_in_dim(x, odd * (rows - 3), 3, 1)  1.04 us
    dynamic_slice x1, local copies, waits for them, and re-layouts, per_device(): near = lax.dynamic_slice_in_dim(x, (1 - odd) * (rows - 3), 3, 1)  1.04 us
  transfers between devices with their start and end apart: 5, of which 3 were waited for; matrix products, arithmetic and copies ran while one was open for 9% of the time, Pallas kernels for 29%

profile of v8, /device:TPU:0, one launch (start us, length us, event | category | flops | bytes accessed | tf_op | source)
XLA Modules:
  0.0 24.1 jit_solution(13371703607814036536)
XLA Ops:
  0.0 1.0 %dynamic-slice_bitcast_fusion.own = bf16[10,3,2,1408]{3,2,1,0:T(2,128)(2,1)S(1)} fusion(bf16[10,2,12,1408]{3,1,2,0:T(2,128)(2,1)} %param.1, s32[]{:T(128)S(6)} %select_n.6), kind=kLoop, calls=%fused_computation | loop fusion | bytes 337924 | tf_op jit(solution)/shard_map/dynamic_slice | solution.py:335
  1.0 3.0 %collective-permute-start.1 = (bf16[10,3,2,1408]{3,2,1,0:T(2,128)(2,1)S(1)}, bf16[10,3,2,1408]{3,2,1,0:T(2,128)(2,1)S(1)}, u32[]{:S(2)}, u32[]{:S(2)}) collective-permute-start(bf16[10,3,2,1408]{3,2,1,0:T(2,128)(2,1)S(1)} %dynamic-slice_bitcast_fusion.own), channel_id=1, source_target_pairs={{0,16},{16,0},{1,17},{17,1},{2,18},{18,2},{3,19},{19,3},{4,20},{20... | collective-permute-start | bytes 506888 | tf_op jit(solution)/shard_map/ppermute | solution.py:341
  4.0 1.0 %constant_dynamic-slice_fusion.own = bf16[10,3,2,1408]{3,2,1,0:T(2,128)(2,1)S(1)} fusion(bf16[10,12,2,1408]{3,2,1,0:T(2,128)(2,1)} %bitcast.4, s32[]{:T(128)S(6)} %select_n.7), kind=kLoop, calls=%fused_computation.1 | loop fusion | bytes 337924 | tf_op jit(solution)/shard_map/dynamic_slice | solution.py:337
  5.1 1.2 %slice.3.mid = bf16[10,6,2,1408]{3,2,1,0:T(2,128)(2,1)S(1)} slice(bf16[10,12,2,1408]{3,2,1,0:T(2,128)(2,1)} %bitcast.5), slice={[0:10], [3:9], [0:2], [0:1408]} | slice | bytes 675840 | tf_op jit(solution)/shard_map/slice | solution.py:338
  6.3 0.1 collective-permute-start
  6.4 2.0 %collective-permute-start.4 = (bf16[10,6,2,1408]{3,2,1,0:T(2,128)(2,1)S(1)}, bf16[10,6,2,1408]{3,2,1,0:T(2,128)(2,1)S(1)}, u32[]{:S(2)}, u32[]{:S(2)}) collective-permute-start(bf16[10,6,2,1408]{3,2,1,0:T(2,128)(2,1)S(1)} %slice.3.mid), channel_id=1, source_target_pairs={{0,16},{16,0},{1,17},{17,1},{2,18},{18,2},{3,19},{19,3},{4,20},{20... | collective-permute-start | bytes 1013768 | tf_op jit(solution)/shard_map/ppermute | solution.py:343
  8.4 0.4 %collective-permute-done.1.other = bf16[10,3,2,1408]{3,2,1,0:T(2,128)(2,1)S(1)} collective-permute-done((bf16[10,3,2,1408]{3,2,1,0:T(2,128)(2,1)S(1)}, bf16[10,3,2,1408]{3,2,1,0:T(2,128)(2,1)S(1)}, u32[]{:S(2)}, u32[]{:S(2)}) %collective-permute-start.1) | collective-permute-done | bytes 168992 | tf_op jit(solution)/shard_map/ppermute | solution.py:341
  8.8 1.7 %far_pairs.1.far = f32[63,8,128]{2,1,0:T(8,128)S(1)} custom-call(bf16[10,3,2,1408]{3,2,1,0:T(2,128)(2,1)S(1)} %dynamic-slice_bitcast_fusion.own, bf16[10,3,2,1408]{3,2,1,0:T(2,128)(2,1)S(1)} %collective-permute-done.1.other), custom_call_target="tpu_custom_call" | custom-call | flops 15000000 | bytes 595968 | tf_op jit(solution)/shard_map/far_pairs/pallas_call | solution.py:297
  10.4 0.7 %collective-permute-start.3 = (f32[63,8,128]{2,1,0:T(8,128)S(1)}, f32[63,8,128]{2,1,0:T(8,128)S(1)}, u32[]{:S(2)}, u32[]{:S(2)}) collective-permute-start(f32[63,8,128]{2,1,0:T(8,128)S(1)} %far_pairs.1.far), channel_id=1, source_target_pairs={{1,2},{2,1},{3,4},{4,3},{5,6},{6,5},{7,8},{8,7},{9,10},{10,9},{11,... | collective-permute-start | bytes 774152 | tf_op jit(solution)/shard_map/ppermute | solution.py:347
  11.1 1.8 %own_mid.1 = (f32[12,2,33,8,128]{4,3,2,1,0:T(8,128)S(1)}, f32[21,32,128]{2,1,0:T(8,128)S(1)}) custom-call(bf16[10,6,2,1408]{3,2,1,0:T(2,128)(2,1)S(1)} %slice.3.mid), custom_call_target="tpu_custom_call" | custom-call | flops 15000000 | bytes 3926016 | tf_op jit(solution)/shard_map/own_mid/pallas_call | solution.py:297
  12.9 0.7 %collective-permute-done.other = bf16[10,3,2,1408]{3,2,1,0:T(2,128)(2,1)S(1)} collective-permute-done((bf16[10,3,2,1408]{3,2,1,0:T(2,128)(2,1)S(1)}, bf16[10,3,2,1408]{3,2,1,0:T(2,128)(2,1)S(1)}, u32[]{:S(2)}, u32[]{:S(2)}) %collective-permute-start) | collective-permute-done | bytes 168992 | tf_op jit(solution)/shard_map/ppermute | solution.py:342
  13.6 1.7 %near_pairs.1.near = f32[63,8,128]{2,1,0:T(8,128)S(1)} custom-call(bf16[10,3,2,1408]{3,2,1,0:T(2,128)(2,1)S(1)} %constant_dynamic-slice_fusion.own, bf16[10,3,2,1408]{3,2,1,0:T(2,128)(2,1)S(1)} %collective-permute-done.other), custom_call_target="tpu_custom_call" | custom-call | flops 15000000 | bytes 595968 | tf_op jit(solution)/shard_map/near_pairs/pallas_call | solution.py:297
  15.3 2.1 %collective-permute-start.2 = (f32[63,8,128]{2,1,0:T(8,128)S(1)}, f32[63,8,128]{2,1,0:T(8,128)S(1)}, u32[]{:S(2)}, u32[]{:S(2)}) collective-permute-start(f32[63,8,128]{2,1,0:T(8,128)S(1)} %near_pairs.1.near), channel_id=1, source_target_pairs={{0,1},{1,0},{2,3},{3,2},{4,5},{5,4},{6,7},{7,6},{8,9},{9,8},{10,11... | collective-permute-start | bytes 774152 | tf_op jit(solution)/shard_map/ppermute | solution.py:353
  17.4 1.9 %collective-permute-done.4.mid = bf16[10,6,2,1408]{3,2,1,0:T(2,128)(2,1)S(1)} collective-permute-done((bf16[10,6,2,1408]{3,2,1,0:T(2,128)(2,1)S(1)}, bf16[10,6,2,1408]{3,2,1,0:T(2,128)(2,1)S(1)}, u32[]{:S(2)}, u32[]{:S(2)}) %collective-permute-start.4) | collective-permute-done | bytes 337952 | tf_op jit(solution)/shard_map/ppermute | solution.py:343
  19.4 1.8 %cross_mid.1.mids = f32[21,48,128]{2,1,0:T(8,128)S(1)} custom-call(f32[12,2,33,8,128]{4,3,2,1,0:T(8,128)S(1)} %get-tuple-element.24.rep, bf16[10,6,2,1408]{3,2,1,0:T(2,128)(2,1)S(1)} %collective-permute-done.4.mid, f32[21,32,128]{2,1,0:T(8,128)S(1)} %get-tuple-element.25.own.mids), custom_call_target="tpu_custom_call" | custom-call | flops 15000000 | bytes 4442112 | tf_op jit(solution)/shard_map/cross_mid/pallas_call | solution.py:297
  21.2 0.0 collective-permute-done.3.far_halo
  21.2 0.0 collective-permute-done.2.near_halo
  21.2 1.2 %early.1 = (f32[16,8,128]{2,1,0:T(8,128)}, f32[10,8,8,128]{3,2,1,0:T(8,128)S(1)}) custom-call(f32[63,8,128]{2,1,0:T(8,128)S(1)} %near_pairs.1.near, f32[63,8,128]{2,1,0:T(8,128)S(1)} %far_pairs.1.far, f32[63,8,128]{2,1,0:T(8,128)S(1)} %collective-permute-done.2.near_halo, f32[63,8,128]{2,1,0:T(8,128)S(1)} %collective-permute-done.3.far_halo, ...), custom_call_target="tpu_custom_call" | custom-call | flops 15000000 | bytes 1769472 | tf_op jit(solution)/shard_map/early/pallas_call | solution.py:297
  22.5 1.6 %finish.1 = f32[10,20,8,128]{3,2,1,0:T(8,128)} custom-call(f32[63,8,128]{2,1,0:T(8,128)S(1)} %near_pairs.1.near, f32[63,8,128]{2,1,0:T(8,128)S(1)} %far_pairs.1.far, f32[63,8,128]{2,1,0:T(8,128)S(1)} %collective-permute-done.2.near_halo, f32[63,8,128]{2,1,0:T(8,128)S(1)} %collective-permute-done.3.far_halo, f32[21,48,128]{2,1,0:T(8,128)S(1)} %cross_mid.1.mids, ...), custom_call_target="tpu_custom_call" | custom-call | flops 5000000 | bytes 2695168 | tf_op jit(solution)/shard_map/finish/pallas_call | solution.py:297
Async XLA Ops:
  1.0 7.7 %collective-permute-start.1 = (bf16[10,3,2,1408]{3,2,1,0:T(2,128)(2,1)S(1)}, bf16[10,3,2,1408]{3,2,1,0:T(2,128)(2,1)S(1)}, u32[]{:S(2)}, u32[]{:S(2)}) collective-permute-start(bf16[10,3,2,1408]{3,2,1,0:T(2,128)(2,1)S(1)} %dynamic-slice_bitcast_fusion.own), channel_id=1, source_target_pairs={{0,16},{16,0},{1,17},{17,1},{2,18},{18,2},{3,19},{19,3},{4,20},{20... | collective-permute-start | bytes 506888 | tf_op jit(solution)/shard_map/ppermute | solution.py:341
  6.3 7.3 %collective-permute-start = (bf16[10,3,2,1408]{3,2,1,0:T(2,128)(2,1)S(1)}, bf16[10,3,2,1408]{3,2,1,0:T(2,128)(2,1)S(1)}, u32[]{:S(2)}, u32[]{:S(2)}) collective-permute-start(bf16[10,3,2,1408]{3,2,1,0:T(2,128)(2,1)S(1)} %constant_dynamic-slice_fusion.own), channel_id=1, source_target_pairs={{0,16},{16,0},{1,17},{17,1},{2,18},{18,2},{3,19},{19,3},{4,20},{20... | collective-permute-start | bytes 506888 | tf_op jit(solution)/shard_map/ppermute | solution.py:342
  6.4 13.0 %collective-permute-start.4 = (bf16[10,6,2,1408]{3,2,1,0:T(2,128)(2,1)S(1)}, bf16[10,6,2,1408]{3,2,1,0:T(2,128)(2,1)S(1)}, u32[]{:S(2)}, u32[]{:S(2)}) collective-permute-start(bf16[10,6,2,1408]{3,2,1,0:T(2,128)(2,1)S(1)} %slice.3.mid), channel_id=1, source_target_pairs={{0,16},{16,0},{1,17},{17,1},{2,18},{18,2},{3,19},{19,3},{4,20},{20... | collective-permute-start | bytes 1013768 | tf_op jit(solution)/shard_map/ppermute | solution.py:343
  10.4 10.8 %collective-permute-start.3 = (f32[63,8,128]{2,1,0:T(8,128)S(1)}, f32[63,8,128]{2,1,0:T(8,128)S(1)}, u32[]{:S(2)}, u32[]{:S(2)}) collective-permute-start(f32[63,8,128]{2,1,0:T(8,128)S(1)} %far_pairs.1.far), channel_id=1, source_target_pairs={{1,2},{2,1},{3,4},{4,3},{5,6},{6,5},{7,8},{8,7},{9,10},{10,9},{11,... | collective-permute-start | bytes 774152 | tf_op jit(solution)/shard_map/ppermute | solution.py:347
  15.3 5.9 %collective-permute-start.2 = (f32[63,8,128]{2,1,0:T(8,128)S(1)}, f32[63,8,128]{2,1,0:T(8,128)S(1)}, u32[]{:S(2)}, u32[]{:S(2)}) collective-permute-start(f32[63,8,128]{2,1,0:T(8,128)S(1)} %near_pairs.1.near), channel_id=1, source_target_pairs={{0,1},{1,0},{2,3},{3,2},{4,5},{5,4},{6,7},{7,6},{8,9},{9,8},{10,11... | collective-permute-start | bytes 774152 | tf_op jit(solution)/shard_map/ppermute | solution.py:353

commit v9 on v8

v9 whole, which is shorter than its diff:
```python
import functools

import jax
import jax.numpy as jnp
from jax import lax
from jax.experimental import pallas as pl
from jax.experimental.pallas import tpu as pltpu
from jax.sharding import PartitionSpec as P

EPS = 1e-06
LANES = 128
CELL = 11
STEPS = 33
TILE = (8, LANES)
F32 = jnp.float32
VMEM = pltpu.MemorySpace.VMEM


def iota(dim):
    return lax.broadcasted_iota(jnp.int32, TILE, dim)


def put_rows(ref, date, row, flat, q, at):
    pair = ref[date, row].astype(F32)
    for m in range(CELL):
        flat[q, m, at : at + 2, :] = pair[:, m * LANES : (m + 1) * LANES]


def unpack_mid(parts, flat):
    first = 0
    for ref in parts:
        dates = ref.shape[0]

        def one(q, carry, ref=ref, dates=dates, first=first):
            for part in range(4):
                date = jnp.minimum(4 * q + part, dates - 1)
                for row in range(6):
                    put_rows(ref, date, row, flat, first + q, part * 12 + row * 2)
            return carry

        lax.fori_loop(0, quads_of(dates), one, 0)
        first += quads_of(dates)
    return first


def unpack_edge(dates, own, other, flat):
    for j in range(2 * dates):
        ref, date = (own, j) if j < dates else (other, j - dates)
        for sub in range(3):
            put_rows(ref, date, sub, flat, j // 8, (j % 8) * 6 + sub * 2)


def rotate(count, flat, cells):
    lane = iota(1)
    turn = lax.rem(lane * 3, CELL)
    bits = [(s, (turn & s) != 0) for s in (1, 2, 4, 8)]

    def one(q, carry):
        for part in range(6):
            v = [flat[q, m, pl.ds(part, 8, stride=6), :] for m in range(CELL)]
            for shift, mask in bits:
                v = [jnp.where(mask, v[(t + shift) % CELL], v[t]) for t in range(CELL)]
            for c in range(CELL):
                cells[q, part % 2, (part // 2) * CELL + c] = v[(8 * c) % CELL]
        return carry

    lax.fori_loop(0, count, one, 0)


def place(count, cells, spread=None):
    lane = iota(1)
    for c in range(CELL):
        pick = (lane * CELL + c) & (LANES - 1)

        def one(q, carry):
            for ri in range(2):
                for sub in range(3):
                    s = sub * CELL + c
                    v = jnp.take_along_axis(cells[q, ri, s], pick, axis=1)
                    cells[q, ri, s] = v
                    if spread is not None:
                        spread(q, ri, s, v)
            return carry

        lax.fori_loop(0, count, one, 0, unroll=count)


def spread_mid(rep):
    low = iota(0) < 4
    even = (iota(0) & 2) == 0

    def spread(q, ri, s, v):
        a = jnp.where(even, v, pltpu.roll(v, 2, 0))
        b = jnp.where(even, pltpu.roll(v, 6, 0), v)
        c, d = pltpu.roll(a, 4, 0), pltpu.roll(b, 4, 0)
        rep[4 * q, ri, s] = jnp.where(low, a, c)
        rep[4 * q + 1, ri, s] = jnp.where(low, b, d)
        rep[4 * q + 2, ri, s] = jnp.where(low, c, a)
        rep[4 * q + 3, ri, s] = jnp.where(low, d, b)

    return spread


def products(rows, cols, load, cells):
    count = len(rows) * len(cols)

    def step(s, acc):
        a = [load(i, 0, s) for i in rows]
        b = [load(i, 1, s) for i in rows]
        ab = [x + y for x, y in zip(a, b)]
        acc = list(acc)
        at = 0
        for q in cols:
            c, d = cells[q, 0, s], cells[q, 1, s]
            cd = c - d
            for i in range(len(rows)):
                acc[at] = acc[at] + a[i] * c
                acc[at + 1] = acc[at + 1] + b[i] * d
                acc[at + 2] = acc[at + 2] + ab[i] * cd
                at += 3
        return tuple(acc)

    acc = lax.fori_loop(0, STEPS, step, (jnp.zeros(TILE, F32),) * (3 * count), unroll=11)
    at = 0
    for j in range(len(cols)):
        for i in range(len(rows)):
            p, q, r = acc[at : at + 3]
            yield i, j, p + q, r - p + q
            at += 3


def powers(qs, cells):
    def step(s, acc):
        out = []
        for n, q in enumerate(qs):
            c, d = cells[q, 0, s], cells[q, 1, s]
            out.append(acc[n] + c * c + d * d)
        return tuple(out)

    return lax.fori_loop(0, STEPS, step, (jnp.zeros(TILE, F32),) * len(qs), unroll=11)


def quads_of(dates):
    return (dates + 3) // 4


def octs_of(dates):
    return (2 * dates + 7) // 8


def edge_kernel(dates, own, other, sums, flat, cells):
    octs = octs_of(dates)
    unpack_edge(dates, own, other, flat)
    rotate(octs, flat, cells)
    place(octs, cells)
    for o, pw in enumerate(powers(range(octs), cells)):
        sums[2 * octs * dates + o] = pw

    def load(i, ri, s):
        return cells[i // 8, ri, s, pl.ds(i % 8, 8, stride=0), :]

    for b in range(dates // 2):
        for i, o, re, im in products([2 * b, 2 * b + 1], range(octs), load, cells):
            at = 2 * octs * (2 * b + i) + o
            sums[at] = re
            sums[at + octs] = im


def near_kernel(dates, own, other, far, mids, sums, rows, flat, cells):
    edge_kernel(dates, own, other, sums, flat, cells)
    middle_rows(dates, 0, sums, far, mids, rows)


def put_mid(dates, quads, rep, cells, sums, first=0, rows=None):
    def store(n, q, v):
        size = 8 if rows is None else min(8, rows - 8 * q)
        sums[n, first + 8 * q : first + 8 * q + size, :] = v[:size]

    for q, pw in enumerate(powers(range(quads), cells)):
        store(2 * dates, q, pw)

    def one(b, carry):
        pairs = products([2 * b, 2 * b + 1], range(quads), lambda i, ri, s: rep[i, ri, s], cells)
        for i, q, re, im in pairs:
            store(4 * b + 2 * i, q, re)
            store(4 * b + 2 * i + 1, q, im)
        return carry

    lax.fori_loop(0, dates // 2, one, 0)


def own_mid_kernel(dates, *refs):
    *parts, rep, sums, flat, cells = refs
    quads = unpack_mid(parts, flat)
    rotate(quads, flat, cells)
    place(quads, cells, spread_mid(rep))
    put_mid(dates, quads, rep, cells, sums)


def cross_mid_kernel(dates, done, ready, rep, mid, before, near, far, sums, *refs):
    rows = refs[: len(ready)]
    flat, cells = refs[len(ready) :]

    def keep(n, carry):
        sums[n, : 2 * (dates + done), :] = before[n, : 2 * (dates + done), :]
        return carry

    quads = unpack_mid([mid], flat)
    rotate(quads, flat, cells)
    place(quads, cells)
    lax.fori_loop(0, 2 * dates + 1, keep, 0, unroll=3)
    put_mid(dates, quads, rep, cells, sums, 2 * (dates + done), 2 * mid.shape[0])
    for o, out in zip(ready, rows):
        middle_rows(dates, o, near, far, sums, out)


def box(v):
    lane = iota(1)
    left = jnp.where(lane > 0, pltpu.roll(v, 1, 1), 0.0)
    right = jnp.where(lane < LANES - 1, pltpu.roll(v, LANES - 1, 1), 0.0)
    return v + left + right


def odd_strip():
    return iota(0) * 0 + lax.rem(lax.axis_index("strip"), 2) == 1


def vreg_of(dates, i, comp, o):
    octs = octs_of(dates)
    if isinstance(i, int) and i == dates:
        return 2 * octs * dates + o
    return 2 * octs * i + octs * comp + o


def mids_of(dates, i, comp, o, mids):
    row = 2 * dates if isinstance(i, int) and i == dates else 2 * i + comp
    return (mids[row, pl.ds(16 * o + e, 8, stride=2), :] for e in range(2))


def each_date(dates, one):
    def step(i, carry):
        one(i)
        return carry

    one(dates)
    lax.fori_loop(0, dates, step, 0, unroll=2)


def middle_rows(dates, o, near, far, mids, out):
    odd = odd_strip()

    def one(i):
        for comp in range(2):
            at = vreg_of(dates, i, comp, o)
            p, q = near[at], far[at]
            b, c = mids_of(dates, i, comp, o, mids)
            a, d = jnp.where(odd, p, q), jnp.where(odd, q, p)
            bc = b + c
            out[i, pl.ds(4 * comp + 1, 8, stride=8), :] = box(a + bc)
            out[i, pl.ds(4 * comp + 2, 8, stride=8), :] = box(bc + d)

    each_date(dates, one)


def outer_row(dates, i, side, sums, halo, mids, out):
    odd = odd_strip()
    for o in range(octs_of(dates)):
        for comp in range(2):
            at = vreg_of(dates, i, comp, o)
            b, c = mids_of(dates, i, comp, o, mids)
            first, second = (b, c) if side == "near" else (c, b)
            v = box(halo[at] + sums[at] + jnp.where(odd, first, second))
            for r in (0, 3):
                out[i, pl.ds(64 * o + 4 * comp + r, 8, stride=8), :] = v


def far_end_kernel(dates, far_halo, far, mids, out):
    each_date(dates, lambda i: outer_row(dates, i, "far", far, far_halo, mids, out))


def last_kernel(dates, count, turn, near_halo, near, mids, far_end, *refs):
    octs = octs_of(dates)
    middle = refs[:octs]
    before, out, ends, scale, mine, other, sem = refs[octs:]
    me = lax.axis_index("date")
    base = lax.rem(me + count - turn, count) * dates
    sub = iota(0) & 3
    odd = odd_strip()
    near_row = sub == jnp.where(odd, 0, 3)
    far_row = sub == jnp.where(odd, 3, 0)

    def tile(i, j):
        o, at = j // 8, 8 * (j % 8)
        rows = slice(8 * j, 8 * j + 8)
        rest = jnp.where(far_row, far_end[i, rows, :], middle[o][i, at : at + 8, :])
        return jnp.where(near_row, ends[i, rows, :], rest)

    outer_row(dates, dates, "near", near, near_halo, mids, ends)
    for j in range(2 * dates):
        scale[j] = lax.rsqrt(tile(dates, j) + EPS)

    def copies(b):
        rows = pl.ds(2 * b, 2)
        yield pltpu.make_async_copy(other.at[rows], out.at[rows, pl.ds(base, dates)], sem.at[b])
        if turn == 1:
            own = out.at[rows, pl.ds(me * dates, dates)]
            yield pltpu.make_async_copy(mine.at[rows], own, sem.at[dates // 2 + b])

    def one(b, carry):
        for i in (2 * b, 2 * b + 1):
            outer_row(dates, i, "near", near, near_halo, mids, ends)
            own = scale[i]
            for j in range(2 * dates):
                v = tile(i, j) * (own * scale[j])
                if j < dates:
                    mine[i, j] = v
                else:
                    other[i, j - dates] = v
        for copy in copies(b):
            copy.start()
        return carry

    lax.fori_loop(0, dates // 2, one, 0)
    for b in range(dates // 2):
        for copy in copies(b):
            copy.wait()


def call(kernel, name, args, outs, scratch=(), flops=0, limit=32, hbm=False, aliases=None):
    vm = pl.BlockSpec(memory_space=VMEM)
    far = pl.BlockSpec(memory_space=pltpu.MemorySpace.HBM)
    ins = [vm] * len(args)
    for n in aliases or {}:
        ins[n] = far
    size = sum(a.size * a.dtype.itemsize for a in (*args, *outs))
    return pl.pallas_call(
        kernel,
        out_shape=tuple(outs),
        in_specs=ins,
        out_specs=(far if hbm else vm,) * len(outs),
        scratch_shapes=list(scratch),
        input_output_aliases=aliases or {},
        compiler_params=pltpu.CompilerParams(vmem_limit_bytes=limit << 20),
        cost_estimate=pl.CostEstimate(flops=flops, bytes_accessed=size, transcendentals=0),
        name=name,
    )(*args)


def per_device(slc):
    dates, _, rows, width = slc.shape
    count = lax.axis_size("date")
    strips = lax.axis_size("strip")
    chip = [(i, i ^ 1) for i in range(strips)]
    chips = [(i, i + 1 if i % 2 else i - 1) for i in range(1, strips - 1)]
    quads, octs = quads_of(dates), octs_of(dates)
    shape = jax.ShapeDtypeStruct
    edge_sums = shape((octs * (2 * dates + 1), *TILE), F32)
    mid_sums = shape((2 * dates + 1, 16 * ((dates + 7) // 8), LANES), F32)
    all_sums = shape((2 * dates + 1, 16 * octs, LANES), F32)
    eight = shape((dates + 1, 64, LANES), F32)
    rep = shape((4 * quads, 2, STEPS, *TILE), F32)

    def work(n):
        return pltpu.VMEM((n, CELL, 48, LANES), F32), pltpu.VMEM((n, 2, STEPS, *TILE), F32)

    def run(kernel, name, args, outs, scratch, fixed=()):
        return call(functools.partial(kernel, dates, *fixed), name, args, outs, scratch, flops=15_000_000)

    x = jnp.transpose(slc, (0, 2, 1, 3))
    odd = lax.rem(lax.axis_index("strip"), 2)
    far = lax.dynamic_slice_in_dim(x, odd * (rows - 3), 3, 1)
    x, far = lax.optimization_barrier((x, far))
    near = lax.dynamic_slice_in_dim(x, (1 - odd) * (rows - 3), 3, 1)
    cuts = [0] + [] + [dates]
    parts = [x[lo:hi, 3 : rows - 3] for lo, hi in zip(cuts, cuts[1:])]
    near, parts = lax.optimization_barrier((near, parts))
    rings = [[(i, (i + t) % count) for i in range(count)] for t in range(1, count)]
    fars = [lax.ppermute(far, "date", ring) for ring in rings]
    nears = [lax.ppermute(near, "date", ring) for ring in rings]
    middles = [[lax.ppermute(part, "date", ring) for part in parts] for ring in rings]
    edges = []
    for t in range(1, count):
        (far_sums,) = run(edge_kernel, "far_pairs", (far, fars[t - 1]), (edge_sums,), work(octs))
        far_halo = lax.ppermute(far_sums, "strip", chips)
        if t == 1:
            own_rows, far_sums = lax.optimization_barrier((parts, far_sums))
            rep_mid, own_mid = run(own_mid_kernel, "own_mid", own_rows, (rep, mid_sums), work(quads))
            nears, rep_mid = lax.optimization_barrier((nears, rep_mid))
        args = (near, nears[t - 1], far_sums, own_mid)
        near_sums, ready = run(near_kernel, "near_pairs", args, (edge_sums, eight), work(octs))
        near_halo = lax.ppermute(near_sums, "strip", chip)
        edges.append((near_sums, far_sums, near_halo, far_halo, ready))
    out = None
    for t in range(1, count):
        near_sums, far_sums, near_halo, far_halo, *ready = edges[t - 1]
        mids = own_mid
        for done, part in zip(cuts, middles[t - 1]):
            known = dates + done + part.shape[0]
            octets = [o for o in range(len(ready), octs) if known >= min(8 * o + 8, 2 * dates)]
            mids, *more = run(
                cross_mid_kernel,
                "cross_mid",
                (rep_mid, part, mids, near_sums, far_sums),
                (all_sums, *[eight] * len(octets)),
                work(quads_of(part.shape[0])),
                (done, octets),
            )
            ready += more
        (far_end,) = run(
            far_end_kernel,
            "far_end",
            (far_halo, far_sums, mids),
            (shape((dates + 1, 64 * octs, LANES), F32),),
            (),
        )
        block = pltpu.VMEM((dates, dates, *TILE), F32)
        (out,) = call(
            functools.partial(last_kernel, dates, count, t),
            "finish",
            (near_halo, near_sums, mids, far_end, *ready, mids if out is None else out),
            (shape((dates, dates * count, *TILE), F32),),
            (
                pltpu.VMEM((dates + 1, 64 * octs, LANES), F32),
                pltpu.VMEM((2 * dates, *TILE), F32),
                block,
                block,
                pltpu.SemaphoreType.DMA((dates,)),
            ),
            flops=5_000_000,
            hbm=True,
            aliases={4 + octs: 0} if t > 1 else None,
        )
    return out.reshape(dates, dates * count, 2, 4, LANES)


def solution(mesh):
    return jax.shard_map(
        per_device,
        mesh=mesh,
        in_specs=(P("date", None, "strip", None),),
        out_specs=P("date", None, None, "strip", None),
        check_vma=False,
    )
```

time: 24.3 us -> 24.6 us (1.012)
  Pallas kernels: 9.84 us -> 10.7 us
  waiting for transfers between devices: 2.98 us -> 2.48 us
    pallas_call x6, Pallas kernels: 9.84 us -> 10.7 us  [call(): pl.pallas_call(kernel, out_shape=tuple(outs), in_specs=ins, out_specs=(fa...]
    ppermute x1, waiting for transfers between devices: 1.95 us -> 1.44 us  [per_device(): lax.ppermute(part, 'date', ring)]
  transfers between devices with their start and end apart: 5 -> 5, of which waited for: 3 -> 3; matrix products, arithmetic and copies ran while one was open for 9% -> 9% of each run, Pallas kernels for 29% -> 37%
where the time goes in v9:
time: 24.6 us; the launch traced here: 24.4 us
  Pallas kernels  10.7 us (43%)
  starting transfers between devices  7.9 us (32%)
  local copies, waits for them, and re-layouts  3.29 us (13%)
  waiting for transfers between devices  2.48 us (10%)
    pallas_call x6, Pallas kernels, call(): pl.pallas_call(kernel, out_shape=tuple(outs), in_specs=ins, out_specs=(fa...  10.7 us
    ppermute x1, starting transfers between devices, per_device(): fars = [lax.ppermute(far, 'date', ring) for ring in rings]  3 us
    ppermute x1, starting transfers between devices, per_device(): near_halo = lax.ppermute(near_sums, 'strip', chip)  2.13 us
    ppermute x1, starting transfers between devices, per_device(): lax.ppermute(part, 'date', ring)  2 us
    ppermute x1, waiting for transfers between devices, per_device(): lax.ppermute(part, 'date', ring)  1.44 us
    slice x1, local copies, waits for them, and re-layouts, per_device(): parts = [x[lo:hi, 3:rows - 3] for lo, hi in zip(cuts, cuts[1:])]  1.22 us
    dynamic_slice x1, local copies, waits for them, and re-layouts, per_device(): far = lax.dynamic_slice_in_dim(x, odd * (rows - 3), 3, 1)  1.04 us
    dynamic_slice x1, local copies, waits for them, and re-layouts, per_device(): near = lax.dynamic_slice_in_dim(x, (1 - odd) * (rows - 3), 3, 1)  1.04 us
  transfers between devices with their start and end apart: 5, of which 3 were waited for; matrix products, arithmetic and copies ran while one was open for 9% of the time, Pallas kernels for 37%

profile of v9, /device:TPU:0, one launch (start us, length us, event | category | flops | bytes accessed | tf_op | source)
XLA Modules:
  0.0 24.4 jit_solution(14100890918293868225)
XLA Ops:
  0.0 1.0 %dynamic-slice_bitcast_fusion.own = bf16[10,3,2,1408]{3,2,1,0:T(2,128)(2,1)S(1)} fusion(bf16[10,2,12,1408]{3,1,2,0:T(2,128)(2,1)} %param.1, s32[]{:T(128)S(6)} %select_n.6), kind=kLoop, calls=%fused_computation | loop fusion | bytes 337924 | tf_op jit(solution)/shard_map/dynamic_slice | solution.py:371
  1.0 3.0 %collective-permute-start.1 = (bf16[10,3,2,1408]{3,2,1,0:T(2,128)(2,1)S(1)}, bf16[10,3,2,1408]{3,2,1,0:T(2,128)(2,1)S(1)}, u32[]{:S(2)}, u32[]{:S(2)}) collective-permute-start(bf16[10,3,2,1408]{3,2,1,0:T(2,128)(2,1)S(1)} %dynamic-slice_bitcast_fusion.own), channel_id=1, source_target_pairs={{0,16},{16,0},{1,17},{17,1},{2,18},{18,2},{3,19},{19,3},{4,20},{20... | collective-permute-start | bytes 506888 | tf_op jit(solution)/shard_map/ppermute | solution.py:378
  4.0 1.0 %constant_dynamic-slice_fusion.own = bf16[10,3,2,1408]{3,2,1,0:T(2,128)(2,1)S(1)} fusion(bf16[10,12,2,1408]{3,2,1,0:T(2,128)(2,1)} %bitcast.4, s32[]{:T(128)S(6)} %select_n.7), kind=kLoop, calls=%fused_computation.1 | loop fusion | bytes 337924 | tf_op jit(solution)/shard_map/dynamic_slice | solution.py:373
  5.1 1.2 %slice.3.refs_0_ = bf16[10,6,2,1408]{3,2,1,0:T(2,128)(2,1)S(1)} slice(bf16[10,12,2,1408]{3,2,1,0:T(2,128)(2,1)} %bitcast.5), slice={[0:10], [3:9], [0:2], [0:1408]} | slice | bytes 675840 | tf_op jit(solution)/shard_map/slice | solution.py:375
  6.3 0.1 collective-permute-start
  6.4 2.0 %collective-permute-start.3 = (bf16[10,6,2,1408]{3,2,1,0:T(2,128)(2,1)S(1)}, bf16[10,6,2,1408]{3,2,1,0:T(2,128)(2,1)S(1)}, u32[]{:S(2)}, u32[]{:S(2)}) collective-permute-start(bf16[10,6,2,1408]{3,2,1,0:T(2,128)(2,1)S(1)} %slice.3.refs_0_), channel_id=1, source_target_pairs={{0,16},{16,0},{1,17},{17,1},{2,18},{18,2},{3,19},{19,3},{4,20},{20... | collective-permute-start | bytes 1013768 | tf_op jit(solution)/shard_map/ppermute | solution.py:380
  8.4 0.4 %collective-permute-done.1.other = bf16[10,3,2,1408]{3,2,1,0:T(2,128)(2,1)S(1)} collective-permute-done((bf16[10,3,2,1408]{3,2,1,0:T(2,128)(2,1)S(1)}, bf16[10,3,2,1408]{3,2,1,0:T(2,128)(2,1)S(1)}, u32[]{:S(2)}, u32[]{:S(2)}) %collective-permute-start.1) | collective-permute-done | bytes 168992 | tf_op jit(solution)/shard_map/ppermute | solution.py:378
  8.8 1.7 %far_pairs.1.far = f32[63,8,128]{2,1,0:T(8,128)S(1)} custom-call(bf16[10,3,2,1408]{3,2,1,0:T(2,128)(2,1)S(1)} %dynamic-slice_bitcast_fusion.own, bf16[10,3,2,1408]{3,2,1,0:T(2,128)(2,1)S(1)} %collective-permute-done.1.other), custom_call_target="tpu_custom_call" | custom-call | flops 15000000 | bytes 595968 | tf_op jit(solution)/shard_map/far_pairs/pallas_call | solution.py:336
  10.4 0.7 %collective-permute-start.4 = (f32[63,8,128]{2,1,0:T(8,128)S(1)}, f32[63,8,128]{2,1,0:T(8,128)S(1)}, u32[]{:S(2)}, u32[]{:S(2)}) collective-permute-start(f32[63,8,128]{2,1,0:T(8,128)S(1)} %far_pairs.1.far), channel_id=1, source_target_pairs={{1,2},{2,1},{3,4},{4,3},{5,6},{6,5},{7,8},{8,7},{9,10},{10,9},{11,... | collective-permute-start | bytes 774152 | tf_op jit(solution)/shard_map/ppermute | solution.py:384
  11.1 1.8 %own_mid.1 = (f32[12,2,33,8,128]{4,3,2,1,0:T(8,128)S(1)}, f32[21,32,128]{2,1,0:T(8,128)S(1)}) custom-call(bf16[10,6,2,1408]{3,2,1,0:T(2,128)(2,1)S(1)} %slice.3.refs_0_), custom_call_target="tpu_custom_call" | custom-call | flops 15000000 | bytes 3926016 | tf_op jit(solution)/shard_map/own_mid/pallas_call | solution.py:336
  12.9 0.7 %collective-permute-done.other = bf16[10,3,2,1408]{3,2,1,0:T(2,128)(2,1)S(1)} collective-permute-done((bf16[10,3,2,1408]{3,2,1,0:T(2,128)(2,1)S(1)}, bf16[10,3,2,1408]{3,2,1,0:T(2,128)(2,1)S(1)}, u32[]{:S(2)}, u32[]{:S(2)}) %collective-permute-start) | collective-permute-done | bytes 168992 | tf_op jit(solution)/shard_map/ppermute | solution.py:379
  13.6 2.2 %near_pairs.1 = (f32[63,8,128]{2,1,0:T(8,128)S(1)}, f32[11,64,128]{2,1,0:T(8,128)S(1)}) custom-call(bf16[10,3,2,1408]{3,2,1,0:T(2,128)(2,1)S(1)} %constant_dynamic-slice_fusion.own, bf16[10,3,2,1408]{3,2,1,0:T(2,128)(2,1)S(1)} %collective-permute-done.other, f32[63,8,128]{2,1,0:T(8,128)S(1)} %far_pairs.1.far, f32[21,32,128]{2,1,0:T(8,128)S(1)} %get-tuple-element.28.mids.before), custom_call_target="tpu_custom_call" | custom-call | flops 15000000 | bytes 1558528 | tf_op jit(solution)/shard_map/near_pairs/pallas_call | solution.py:336
  15.8 2.1 %collective-permute-start.2 = (f32[63,8,128]{2,1,0:T(8,128)S(1)}, f32[63,8,128]{2,1,0:T(8,128)S(1)}, u32[]{:S(2)}, u32[]{:S(2)}) collective-permute-start(f32[63,8,128]{2,1,0:T(8,128)S(1)} %get-tuple-element.29.near), channel_id=1, source_target_pairs={{0,1},{1,0},{2,3},{3,2},{4,5},{5,4},{6,7},{7,6},{8,9},{9,8},{10,11... | collective-permute-start | bytes 774152 | tf_op jit(solution)/shard_map/ppermute | solution.py:391
  17.9 1.4 %collective-permute-done.3.mid = bf16[10,6,2,1408]{3,2,1,0:T(2,128)(2,1)S(1)} collective-permute-done((bf16[10,6,2,1408]{3,2,1,0:T(2,128)(2,1)S(1)}, bf16[10,6,2,1408]{3,2,1,0:T(2,128)(2,1)S(1)}, u32[]{:S(2)}, u32[]{:S(2)}) %collective-permute-start.3) | collective-permute-done | bytes 337952 | tf_op jit(solution)/shard_map/ppermute | solution.py:380
  19.4 2.8 %cross_mid.1 = (f32[21,48,128]{2,1,0:T(8,128)S(1)}, f32[11,64,128]{2,1,0:T(8,128)S(1)}, f32[11,64,128]{2,1,0:T(8,128)S(1)}) custom-call(f32[12,2,33,8,128]{4,3,2,1,0:T(8,128)S(1)} %get-tuple-element.30.rep, bf16[10,6,2,1408]{3,2,1,0:T(2,128)(2,1)S(1)} %collective-permute-done.3.mid, f32[21,32,128]{2,1,0:T(8,128)S(1)} %get-tuple-element.28.mids.before, ...), custom_call_target="tpu_custom_call" | custom-call | flops 15000000 | bytes 5679104 | tf_op jit(solution)/shard_map/cross_mid/pallas_call | solution.py:336
  22.2 0.0 collective-permute-done.4.far_halo
  22.2 0.6 %far_end.1 = f32[11,192,128]{2,1,0:T(8,128)S(1)} custom-call(f32[63,8,128]{2,1,0:T(8,128)S(1)} %collective-permute-done.4.far_halo, f32[63,8,128]{2,1,0:T(8,128)S(1)} %far_pairs.1.far, f32[21,48,128]{2,1,0:T(8,128)S(1)} %get-tuple-element.31.mids.refs_3_), custom_call_target="tpu_custom_call" | custom-call | flops 15000000 | bytes 2113536 | tf_op jit(solution)/shard_map/far_end/pallas_call | solution.py:336
  22.9 0.0 collective-permute-done.2.near_halo
  22.9 1.6 %finish.1 = f32[10,20,8,128]{3,2,1,0:T(8,128)} custom-call(f32[63,8,128]{2,1,0:T(8,128)S(1)} %collective-permute-done.2.near_halo, f32[63,8,128]{2,1,0:T(8,128)S(1)} %get-tuple-element.29.near, f32[21,48,128]{2,1,0:T(8,128)S(1)} %get-tuple-element.31.mids.refs_3_, f32[11,192,128]{2,1,0:T(8,128)S(1)} %far_end.1, ...), custom_call_target="tpu_custom_call" | custom-call | flops 5000000 | bytes 4530176 | tf_op jit(solution)/shard_map/finish/pallas_call | solution.py:336
Async XLA Ops:
  1.0 7.7 %collective-permute-start.1 = (bf16[10,3,2,1408]{3,2,1,0:T(2,128)(2,1)S(1)}, bf16[10,3,2,1408]{3,2,1,0:T(2,128)(2,1)S(1)}, u32[]{:S(2)}, u32[]{:S(2)}) collective-permute-start(bf16[10,3,2,1408]{3,2,1,0:T(2,128)(2,1)S(1)} %dynamic-slice_bitcast_fusion.own), channel_id=1, source_target_pairs={{0,16},{16,0},{1,17},{17,1},{2,18},{18,2},{3,19},{19,3},{4,20},{20... | collective-permute-start | bytes 506888 | tf_op jit(solution)/shard_map/ppermute | solution.py:378
  6.3 7.3 %collective-permute-start = (bf16[10,3,2,1408]{3,2,1,0:T(2,128)(2,1)S(1)}, bf16[10,3,2,1408]{3,2,1,0:T(2,128)(2,1)S(1)}, u32[]{:S(2)}, u32[]{:S(2)}) collective-permute-start(bf16[10,3,2,1408]{3,2,1,0:T(2,128)(2,1)S(1)} %constant_dynamic-slice_fusion.own), channel_id=1, source_target_pairs={{0,16},{16,0},{1,17},{17,1},{2,18},{18,2},{3,19},{19,3},{4,20},{20... | collective-permute-start | bytes 506888 | tf_op jit(solution)/shard_map/ppermute | solution.py:379
  6.4 13.0 %collective-permute-start.3 = (bf16[10,6,2,1408]{3,2,1,0:T(2,128)(2,1)S(1)}, bf16[10,6,2,1408]{3,2,1,0:T(2,128)(2,1)S(1)}, u32[]{:S(2)}, u32[]{:S(2)}) collective-permute-start(bf16[10,6,2,1408]{3,2,1,0:T(2,128)(2,1)S(1)} %slice.3.refs_0_), channel_id=1, source_target_pairs={{0,16},{16,0},{1,17},{17,1},{2,18},{18,2},{3,19},{19,3},{4,20},{20... | collective-permute-start | bytes 1013768 | tf_op jit(solution)/shard_map/ppermute | solution.py:380
  10.4 11.8 %collective-permute-start.4 = (f32[63,8,128]{2,1,0:T(8,128)S(1)}, f32[63,8,128]{2,1,0:T(8,128)S(1)}, u32[]{:S(2)}, u32[]{:S(2)}) collective-permute-start(f32[63,8,128]{2,1,0:T(8,128)S(1)} %far_pairs.1.far), channel_id=1, source_target_pairs={{1,2},{2,1},{3,4},{4,3},{5,6},{6,5},{7,8},{8,7},{9,10},{10,9},{11,... | collective-permute-start | bytes 774152 | tf_op jit(solution)/shard_map/ppermute | solution.py:384
  15.8 7.1 %collective-permute-start.2 = (f32[63,8,128]{2,1,0:T(8,128)S(1)}, f32[63,8,128]{2,1,0:T(8,128)S(1)}, u32[]{:S(2)}, u32[]{:S(2)}) collective-permute-start(f32[63,8,128]{2,1,0:T(8,128)S(1)} %get-tuple-element.29.near), channel_id=1, source_target_pairs={{0,1},{1,0},{2,3},{3,2},{4,5},{5,4},{6,7},{7,6},{8,9},{9,8},{10,11... | collective-permute-start | bytes 774152 | tf_op jit(solution)/shard_map/ppermute | solution.py:391

commit v10 on v9

--- a/solution.py
+++ b/solution.py
@@ -243,7 +243,7 @@
         return carry
 
     one(dates)
-    lax.fori_loop(0, dates, step, 0, unroll=2)
+    lax.fori_loop(0, dates, step, 0, unroll=dates)
 
 
 def middle_rows(dates, o, near, far, mids, out):
@@ -295,7 +295,7 @@
         rest = jnp.where(far_row, far_end[i, rows, :], middle[o][i, at : at + 8, :])
         return jnp.where(near_row, ends[i, rows, :], rest)
 
-    outer_row(dates, dates, "near", near, near_halo, mids, ends)
+    each_date(dates, lambda i: outer_row(dates, i, "near", near, near_halo, mids, ends))
     for j in range(2 * dates):
         scale[j] = lax.rsqrt(tile(dates, j) + EPS)
 
@@ -306,9 +306,8 @@
             own = out.at[rows, pl.ds(me * dates, dates)]
             yield pltpu.make_async_copy(mine.at[rows], own, sem.at[dates // 2 + b])
 
-    def one(b, carry):
+    for b in range(dates // 2):
         for i in (2 * b, 2 * b + 1):
-            outer_row(dates, i, "near", near, near_halo, mids, ends)
             own = scale[i]
             for j in range(2 * dates):
                 v = tile(i, j) * (own * scale[j])
@@ -318,9 +317,6 @@
                     other[i, j - dates] = v
         for copy in copies(b):
             copy.start()
-        return carry
-
-    lax.fori_loop(0, dates // 2, one, 0)
     for b in range(dates // 2):
         for copy in copies(b):
             copy.wait()

time: 24.6 us -> 23.1 us (0.939)
  Pallas kernels: 10.7 us -> 8.8 us
  waiting for transfers between devices: 2.48 us -> 2.84 us
    pallas_call x6, Pallas kernels: 10.7 us -> 8.8 us  [call(): pl.pallas_call(kernel, out_shape=tuple(outs), in_specs=ins, out_specs=(fa...]
    ppermute x1, waiting for transfers between devices: 1.44 us -> 1.79 us  [per_device(): lax.ppermute(part, 'date', ring)]
  transfers between devices with their start and end apart: 5 -> 5, of which waited for: 3 -> 3; matrix products, arithmetic and copies ran while one was open for 9% -> 10% of each run, Pallas kernels for 37% -> 33%
where the time goes in v10:
time: 23.1 us; the launch traced here: 22.9 us
  Pallas kernels  8.8 us (38%)
  starting transfers between devices  7.9 us (34%)
  local copies, waits for them, and re-layouts  3.29 us (14%)
  waiting for transfers between devices  2.84 us (12%)
    pallas_call x6, Pallas kernels, call(): pl.pallas_call(kernel, out_shape=tuple(outs), in_specs=ins, out_specs=(fa...  8.8 us
    ppermute x1, starting transfers between devices, per_device(): fars = [lax.ppermute(far, 'date', ring) for ring in rings]  3 us
    ppermute x1, starting transfers between devices, per_device(): near_halo = lax.ppermute(near_sums, 'strip', chip)  2.13 us
    ppermute x1, starting transfers between devices, per_device(): lax.ppermute(part, 'date', ring)  2 us
    ppermute x1, waiting for transfers between devices, per_device(): lax.ppermute(part, 'date', ring)  1.79 us
    slice x1, local copies, waits for them, and re-layouts, per_device(): parts = [x[lo:hi, 3:rows - 3] for lo, hi in zip(cuts, cuts[1:])]  1.22 us
    dynamic_slice x1, local copies, waits for them, and re-layouts, per_device(): far = lax.dynamic_slice_in_dim(x, odd * (rows - 3), 3, 1)  1.04 us
    dynamic_slice x1, local copies, waits for them, and re-layouts, per_device(): near = lax.dynamic_slice_in_dim(x, (1 - odd) * (rows - 3), 3, 1)  1.04 us
  transfers between devices with their start and end apart: 5, of which 3 were waited for; matrix products, arithmetic and copies ran while one was open for 10% of the time, Pallas kernels for 33%

profile of v10, /device:TPU:0, one launch (start us, length us, event | category | flops | bytes accessed | tf_op | source)
XLA Modules:
  0.0 22.9 jit_solution(13014864798807107445)
XLA Ops:
  0.0 1.0 %dynamic-slice_bitcast_fusion.own = bf16[10,3,2,1408]{3,2,1,0:T(2,128)(2,1)S(1)} fusion(bf16[10,2,12,1408]{3,1,2,0:T(2,128)(2,1)} %param.1, s32[]{:T(128)S(6)} %select_n.6), kind=kLoop, calls=%fused_computation | loop fusion | bytes 337924 | tf_op jit(solution)/shard_map/dynamic_slice | solution.py:367
  1.0 3.0 %collective-permute-start.1 = (bf16[10,3,2,1408]{3,2,1,0:T(2,128)(2,1)S(1)}, bf16[10,3,2,1408]{3,2,1,0:T(2,128)(2,1)S(1)}, u32[]{:S(2)}, u32[]{:S(2)}) collective-permute-start(bf16[10,3,2,1408]{3,2,1,0:T(2,128)(2,1)S(1)} %dynamic-slice_bitcast_fusion.own), channel_id=1, source_target_pairs={{0,16},{16,0},{1,17},{17,1},{2,18},{18,2},{3,19},{19,3},{4,20},{20... | collective-permute-start | bytes 506888 | tf_op jit(solution)/shard_map/ppermute | solution.py:374
  4.0 1.0 %constant_dynamic-slice_fusion.own = bf16[10,3,2,1408]{3,2,1,0:T(2,128)(2,1)S(1)} fusion(bf16[10,12,2,1408]{3,2,1,0:T(2,128)(2,1)} %bitcast.4, s32[]{:T(128)S(6)} %select_n.7), kind=kLoop, calls=%fused_computation.1 | loop fusion | bytes 337924 | tf_op jit(solution)/shard_map/dynamic_slice | solution.py:369
  5.1 1.2 %slice.3.refs_0_ = bf16[10,6,2,1408]{3,2,1,0:T(2,128)(2,1)S(1)} slice(bf16[10,12,2,1408]{3,2,1,0:T(2,128)(2,1)} %bitcast.5), slice={[0:10], [3:9], [0:2], [0:1408]} | slice | bytes 675840 | tf_op jit(solution)/shard_map/slice | solution.py:371
  6.3 0.1 collective-permute-start
  6.4 2.0 %collective-permute-start.3 = (bf16[10,6,2,1408]{3,2,1,0:T(2,128)(2,1)S(1)}, bf16[10,6,2,1408]{3,2,1,0:T(2,128)(2,1)S(1)}, u32[]{:S(2)}, u32[]{:S(2)}) collective-permute-start(bf16[10,6,2,1408]{3,2,1,0:T(2,128)(2,1)S(1)} %slice.3.refs_0_), channel_id=1, source_target_pairs={{0,16},{16,0},{1,17},{17,1},{2,18},{18,2},{3,19},{19,3},{4,20},{20... | collective-permute-start | bytes 1013768 | tf_op jit(solution)/shard_map/ppermute | solution.py:376
  8.4 0.4 %collective-permute-done.1.other = bf16[10,3,2,1408]{3,2,1,0:T(2,128)(2,1)S(1)} collective-permute-done((bf16[10,3,2,1408]{3,2,1,0:T(2,128)(2,1)S(1)}, bf16[10,3,2,1408]{3,2,1,0:T(2,128)(2,1)S(1)}, u32[]{:S(2)}, u32[]{:S(2)}) %collective-permute-start.1) | collective-permute-done | bytes 168992 | tf_op jit(solution)/shard_map/ppermute | solution.py:374
  8.8 1.7 %far_pairs.1.far = f32[63,8,128]{2,1,0:T(8,128)S(1)} custom-call(bf16[10,3,2,1408]{3,2,1,0:T(2,128)(2,1)S(1)} %dynamic-slice_bitcast_fusion.own, bf16[10,3,2,1408]{3,2,1,0:T(2,128)(2,1)S(1)} %collective-permute-done.1.other), custom_call_target="tpu_custom_call" | custom-call | flops 15000000 | bytes 595968 | tf_op jit(solution)/shard_map/far_pairs/pallas_call | solution.py:332
  10.4 0.7 %collective-permute-start.4 = (f32[63,8,128]{2,1,0:T(8,128)S(1)}, f32[63,8,128]{2,1,0:T(8,128)S(1)}, u32[]{:S(2)}, u32[]{:S(2)}) collective-permute-start(f32[63,8,128]{2,1,0:T(8,128)S(1)} %far_pairs.1.far), channel_id=1, source_target_pairs={{1,2},{2,1},{3,4},{4,3},{5,6},{6,5},{7,8},{8,7},{9,10},{10,9},{11,... | collective-permute-start | bytes 774152 | tf_op jit(solution)/shard_map/ppermute | solution.py:380
  11.1 1.8 %own_mid.1 = (f32[12,2,33,8,128]{4,3,2,1,0:T(8,128)S(1)}, f32[21,32,128]{2,1,0:T(8,128)S(1)}) custom-call(bf16[10,6,2,1408]{3,2,1,0:T(2,128)(2,1)S(1)} %slice.3.refs_0_), custom_call_target="tpu_custom_call" | custom-call | flops 15000000 | bytes 3926016 | tf_op jit(solution)/shard_map/own_mid/pallas_call | solution.py:332
  12.9 0.7 %collective-permute-done.other = bf16[10,3,2,1408]{3,2,1,0:T(2,128)(2,1)S(1)} collective-permute-done((bf16[10,3,2,1408]{3,2,1,0:T(2,128)(2,1)S(1)}, bf16[10,3,2,1408]{3,2,1,0:T(2,128)(2,1)S(1)}, u32[]{:S(2)}, u32[]{:S(2)}) %collective-permute-start) | collective-permute-done | bytes 168992 | tf_op jit(solution)/shard_map/ppermute | solution.py:375
  13.6 1.8 %near_pairs.1 = (f32[63,8,128]{2,1,0:T(8,128)S(1)}, f32[11,64,128]{2,1,0:T(8,128)S(1)}) custom-call(bf16[10,3,2,1408]{3,2,1,0:T(2,128)(2,1)S(1)} %constant_dynamic-slice_fusion.own, bf16[10,3,2,1408]{3,2,1,0:T(2,128)(2,1)S(1)} %collective-permute-done.other, f32[63,8,128]{2,1,0:T(8,128)S(1)} %far_pairs.1.far, f32[21,32,128]{2,1,0:T(8,128)S(1)} %get-tuple-element.28.mids.before), custom_call_target="tpu_custom_call" | custom-call | flops 15000000 | bytes 1558528 | tf_op jit(solution)/shard_map/near_pairs/pallas_call | solution.py:332
  15.5 2.1 %collective-permute-start.2 = (f32[63,8,128]{2,1,0:T(8,128)S(1)}, f32[63,8,128]{2,1,0:T(8,128)S(1)}, u32[]{:S(2)}, u32[]{:S(2)}) collective-permute-start(f32[63,8,128]{2,1,0:T(8,128)S(1)} %get-tuple-element.29.near), channel_id=1, source_target_pairs={{0,1},{1,0},{2,3},{3,2},{4,5},{5,4},{6,7},{7,6},{8,9},{9,8},{10,11... | collective-permute-start | bytes 774152 | tf_op jit(solution)/shard_map/ppermute | solution.py:387
  17.6 1.8 %collective-permute-done.3.mid = bf16[10,6,2,1408]{3,2,1,0:T(2,128)(2,1)S(1)} collective-permute-done((bf16[10,6,2,1408]{3,2,1,0:T(2,128)(2,1)S(1)}, bf16[10,6,2,1408]{3,2,1,0:T(2,128)(2,1)S(1)}, u32[]{:S(2)}, u32[]{:S(2)}) %collective-permute-start.3) | collective-permute-done | bytes 337952 | tf_op jit(solution)/shard_map/ppermute | solution.py:376
  19.4 2.1 %cross_mid.1 = (f32[21,48,128]{2,1,0:T(8,128)S(1)}, f32[11,64,128]{2,1,0:T(8,128)S(1)}, f32[11,64,128]{2,1,0:T(8,128)S(1)}) custom-call(f32[12,2,33,8,128]{4,3,2,1,0:T(8,128)S(1)} %get-tuple-element.30.rep, bf16[10,6,2,1408]{3,2,1,0:T(2,128)(2,1)S(1)} %collective-permute-done.3.mid, f32[21,32,128]{2,1,0:T(8,128)S(1)} %get-tuple-element.28.mids.before, ...), custom_call_target="tpu_custom_call" | custom-call | flops 15000000 | bytes 5679104 | tf_op jit(solution)/shard_map/cross_mid/pallas_call | solution.py:332
  21.4 0.0 collective-permute-done.4.far_halo
  21.5 0.2 %far_end.1 = f32[11,192,128]{2,1,0:T(8,128)S(1)} custom-call(f32[63,8,128]{2,1,0:T(8,128)S(1)} %collective-permute-done.4.far_halo, f32[63,8,128]{2,1,0:T(8,128)S(1)} %far_pairs.1.far, f32[21,48,128]{2,1,0:T(8,128)S(1)} %get-tuple-element.31.mids.refs_3_), custom_call_target="tpu_custom_call" | custom-call | flops 15000000 | bytes 2113536 | tf_op jit(solution)/shard_map/far_end/pallas_call | solution.py:332
  21.7 0.0 collective-permute-done.2.near_halo
  21.7 1.2 %finish.1 = f32[10,20,8,128]{3,2,1,0:T(8,128)} custom-call(f32[63,8,128]{2,1,0:T(8,128)S(1)} %collective-permute-done.2.near_halo, f32[63,8,128]{2,1,0:T(8,128)S(1)} %get-tuple-element.29.near, f32[21,48,128]{2,1,0:T(8,128)S(1)} %get-tuple-element.31.mids.refs_3_, f32[11,192,128]{2,1,0:T(8,128)S(1)} %far_end.1, ...), custom_call_target="tpu_custom_call" | custom-call | flops 5000000 | bytes 4530176 | tf_op jit(solution)/shard_map/finish/pallas_call | solution.py:332
Async XLA Ops:
  1.0 7.7 %collective-permute-start.1 = (bf16[10,3,2,1408]{3,2,1,0:T(2,128)(2,1)S(1)}, bf16[10,3,2,1408]{3,2,1,0:T(2,128)(2,1)S(1)}, u32[]{:S(2)}, u32[]{:S(2)}) collective-permute-start(bf16[10,3,2,1408]{3,2,1,0:T(2,128)(2,1)S(1)} %dynamic-slice_bitcast_fusion.own), channel_id=1, source_target_pairs={{0,16},{16,0},{1,17},{17,1},{2,18},{18,2},{3,19},{19,3},{4,20},{20... | collective-permute-start | bytes 506888 | tf_op jit(solution)/shard_map/ppermute | solution.py:374
  6.3 7.3 %collective-permute-start = (bf16[10,3,2,1408]{3,2,1,0:T(2,128)(2,1)S(1)}, bf16[10,3,2,1408]{3,2,1,0:T(2,128)(2,1)S(1)}, u32[]{:S(2)}, u32[]{:S(2)}) collective-permute-start(bf16[10,3,2,1408]{3,2,1,0:T(2,128)(2,1)S(1)} %constant_dynamic-slice_fusion.own), channel_id=1, source_target_pairs={{0,16},{16,0},{1,17},{17,1},{2,18},{18,2},{3,19},{19,3},{4,20},{20... | collective-permute-start | bytes 506888 | tf_op jit(solution)/shard_map/ppermute | solution.py:375
  6.4 13.0 %collective-permute-start.3 = (bf16[10,6,2,1408]{3,2,1,0:T(2,128)(2,1)S(1)}, bf16[10,6,2,1408]{3,2,1,0:T(2,128)(2,1)S(1)}, u32[]{:S(2)}, u32[]{:S(2)}) collective-permute-start(bf16[10,6,2,1408]{3,2,1,0:T(2,128)(2,1)S(1)} %slice.3.refs_0_), channel_id=1, source_target_pairs={{0,16},{16,0},{1,17},{17,1},{2,18},{18,2},{3,19},{19,3},{4,20},{20... | collective-permute-start | bytes 1013768 | tf_op jit(solution)/shard_map/ppermute | solution.py:376
  10.4 11.0 %collective-permute-start.4 = (f32[63,8,128]{2,1,0:T(8,128)S(1)}, f32[63,8,128]{2,1,0:T(8,128)S(1)}, u32[]{:S(2)}, u32[]{:S(2)}) collective-permute-start(f32[63,8,128]{2,1,0:T(8,128)S(1)} %far_pairs.1.far), channel_id=1, source_target_pairs={{1,2},{2,1},{3,4},{4,3},{5,6},{6,5},{7,8},{8,7},{9,10},{10,9},{11,... | collective-permute-start | bytes 774152 | tf_op jit(solution)/shard_map/ppermute | solution.py:380
  15.5 6.3 %collective-permute-start.2 = (f32[63,8,128]{2,1,0:T(8,128)S(1)}, f32[63,8,128]{2,1,0:T(8,128)S(1)}, u32[]{:S(2)}, u32[]{:S(2)}) collective-permute-start(f32[63,8,128]{2,1,0:T(8,128)S(1)} %get-tuple-element.29.near), channel_id=1, source_target_pairs={{0,1},{1,0},{2,3},{3,2},{4,5},{5,4},{6,7},{7,6},{8,9},{9,8},{10,11... | collective-permute-start | bytes 774152 | tf_op jit(solution)/shard_map/ppermute | solution.py:387

commit v11 on v10

--- a/solution.py
+++ b/solution.py
@@ -197,19 +197,19 @@
     put_mid(dates, quads, rep, cells, sums)
 
 
-def cross_mid_kernel(dates, done, ready, rep, mid, before, near, far, sums, *refs):
+def cross_mid_kernel(dates, first, kept, ready, rep, mid, before, near, far, sums, *refs):
     rows = refs[: len(ready)]
     flat, cells = refs[len(ready) :]
 
     def keep(n, carry):
-        sums[n, : 2 * (dates + done), :] = before[n, : 2 * (dates + done), :]
+        sums[n, :kept, :] = before[n, :kept, :]
         return carry
 
     quads = unpack_mid([mid], flat)
     rotate(quads, flat, cells)
     place(quads, cells)
     lax.fori_loop(0, 2 * dates + 1, keep, 0, unroll=3)
-    put_mid(dates, quads, rep, cells, sums, 2 * (dates + done), 2 * mid.shape[0])
+    put_mid(dates, quads, rep, cells, sums, 2 * (dates + first), 2 * mid.shape[0])
     for o, out in zip(ready, rows):
         middle_rows(dates, o, near, far, sums, out)
 
@@ -367,8 +367,8 @@
     far = lax.dynamic_slice_in_dim(x, odd * (rows - 3), 3, 1)
     x, far = lax.optimization_barrier((x, far))
     near = lax.dynamic_slice_in_dim(x, (1 - odd) * (rows - 3), 3, 1)
-    cuts = [0] + [] + [dates]
-    parts = [x[lo:hi, 3 : rows - 3] for lo, hi in zip(cuts, cuts[1:])]
+    spans = [(0, 8), (8, dates)]
+    parts = [x[lo:hi, 3 : rows - 3] for lo, hi in spans]
     near, parts = lax.optimization_barrier((near, parts))
     rings = [[(i, (i + t) % count) for i in range(count)] for t in range(1, count)]
     fars = [lax.ppermute(far, "date", ring) for ring in rings]
@@ -381,27 +381,33 @@
         if t == 1:
             own_rows, far_sums = lax.optimization_barrier((parts, far_sums))
             rep_mid, own_mid = run(own_mid_kernel, "own_mid", own_rows, (rep, mid_sums), work(quads))
-            nears, rep_mid = lax.optimization_barrier((nears, rep_mid))
+            early = [part[1] for part in middles]
+            nears, early, rep_mid = lax.optimization_barrier((nears, early, rep_mid))
         args = (near, nears[t - 1], far_sums, own_mid)
         near_sums, ready = run(near_kernel, "near_pairs", args, (edge_sums, eight), work(octs))
         near_halo = lax.ppermute(near_sums, "strip", chip)
         edges.append((near_sums, far_sums, near_halo, far_halo, ready))
     out = None
     for t in range(1, count):
-        near_sums, far_sums, near_halo, far_halo, *ready = edges[t - 1]
-        mids = own_mid
-        for done, part in zip(cuts, middles[t - 1]):
-            known = dates + done + part.shape[0]
-            octets = [o for o in range(len(ready), octs) if known >= min(8 * o + 8, 2 * dates)]
+        near_sums, far_sums, near_halo, far_halo, ready = edges[t - 1]
+        middle = {0: ready}
+        known = set(range(dates))
+        mids, kept = own_mid, 2 * dates
+        for (lo, hi), part in ((spans[1], early[t - 1]), (spans[0], middles[t - 1][0])):
+            known |= set(range(dates + lo, dates + hi))
+            slots = {o: range(8 * o, min(8 * o + 8, 2 * dates)) for o in range(octs)}
+            octets = [o for o in slots if o not in middle and known.issuperset(slots[o])]
             mids, *more = run(
                 cross_mid_kernel,
                 "cross_mid",
                 (rep_mid, part, mids, near_sums, far_sums),
                 (all_sums, *[eight] * len(octets)),
-                work(quads_of(part.shape[0])),
-                (done, octets),
+                work(quads_of(hi - lo)),
+                (lo, kept, octets),
             )
-            ready += more
+            middle.update(zip(octets, more))
+            kept = 4 * dates
+        ready = [middle[o] for o in range(octs)]
         (far_end,) = run(
             far_end_kernel,
             "far_end",

time: 23.1 us -> 23.5 us (1.017)
  starting transfers between devices: 7.9 us -> 6.84 us
  local copies, waits for them, and re-layouts: 3.29 us -> 4.16 us
  waiting for transfers between devices: 2.84 us -> 3.14 us
  Pallas kernels: 8.8 us -> 9.04 us
    ppermute x1 -> x2, waiting for transfers between devices: 1.79 us -> 3.13 us  [per_device(): lax.ppermute(part, 'date', ring)]
    ppermute x1, starting transfers between devices: 2.13 us -> 0.99 us  [per_device(): near_halo = lax.ppermute(near_sums, 'strip', chip)]
    slice x1 -> x2, local copies, waits for them, and re-layouts: 1.22 us -> 2.09 us  [per_device(): parts = [x[lo:hi, 3:rows - 3] for lo, hi in spans]]
    ppermute x1, waiting for transfers between devices: 0.67 us -> 0.01 us  [per_device(): nears = [lax.ppermute(near, 'date', ring) for ring in rings]]
    ppermute x1, waiting for transfers between devices: 0.36 us -> 0.01 us  [per_device(): fars = [lax.ppermute(far, 'date', ring) for ring in rings]]
    pallas_call x6 -> x7, Pallas kernels: 8.8 us -> 9.04 us  [call(): pl.pallas_call(kernel, out_shape=tuple(outs), in_specs=ins, out_specs=(fa...]
    ppermute x1 -> x2, starting transfers between devices: 2 us -> 2.08 us  [per_device(): lax.ppermute(part, 'date', ring)]
  transfers between devices with their start and end apart: 5 -> 6, of which waited for: 3 -> 2; matrix products, arithmetic and copies ran while one was open for 10% -> 13% of each run, Pallas kernels for 33% -> 34%
where the time goes in v11:
time: 23.5 us; the launch traced here: 23.3 us
  Pallas kernels  9.04 us (38%)
  starting transfers between devices  6.84 us (29%)
  local copies, waits for them, and re-layouts  4.16 us (18%)
  waiting for transfers between devices  3.14 us (13%)
    pallas_call x7, Pallas kernels, call(): pl.pallas_call(kernel, out_shape=tuple(outs), in_specs=ins, out_specs=(fa...  9.04 us
    ppermute x2, waiting for transfers between devices, per_device(): lax.ppermute(part, 'date', ring)  3.13 us
    ppermute x1, starting transfers between devices, per_device(): fars = [lax.ppermute(far, 'date', ring) for ring in rings]  3 us
    slice x2, local copies, waits for them, and re-layouts, per_device(): parts = [x[lo:hi, 3:rows - 3] for lo, hi in spans]  2.09 us
    ppermute x2, starting transfers between devices, per_device(): lax.ppermute(part, 'date', ring)  2.08 us
    dynamic_slice x1, local copies, waits for them, and re-layouts, per_device(): far = lax.dynamic_slice_in_dim(x, odd * (rows - 3), 3, 1)  1.04 us
    dynamic_slice x1, local copies, waits for them, and re-layouts, per_device(): near = lax.dynamic_slice_in_dim(x, (1 - odd) * (rows - 3), 3, 1)  1.04 us
    ppermute x1, starting transfers between devices, per_device(): near_halo = lax.ppermute(near_sums, 'strip', chip)  0.99 us
  transfers between devices with their start and end apart: 6, of which 2 were waited for; matrix products, arithmetic and copies ran while one was open for 13% of the time, Pallas kernels for 34%

profile of v11, /device:TPU:0, one launch (start us, length us, event | category | flops | bytes accessed | tf_op | source)
XLA Modules:
  0.0 23.3 jit_solution(7305450714324288714)
XLA Ops:
  0.0 1.0 %dynamic-slice_bitcast_fusion.own = bf16[10,3,2,1408]{3,2,1,0:T(2,128)(2,1)S(1)} fusion(bf16[10,2,12,1408]{3,1,2,0:T(2,128)(2,1)} %param.1, s32[]{:T(128)S(6)} %select_n.6), kind=kLoop, calls=%fused_computation | loop fusion | bytes 337924 | tf_op jit(solution)/shard_map/dynamic_slice | solution.py:367
  1.0 3.0 %collective-permute-start.2 = (bf16[10,3,2,1408]{3,2,1,0:T(2,128)(2,1)S(1)}, bf16[10,3,2,1408]{3,2,1,0:T(2,128)(2,1)S(1)}, u32[]{:S(2)}, u32[]{:S(2)}) collective-permute-start(bf16[10,3,2,1408]{3,2,1,0:T(2,128)(2,1)S(1)} %dynamic-slice_bitcast_fusion.own), channel_id=1, source_target_pairs={{0,16},{16,0},{1,17},{17,1},{2,18},{18,2},{3,19},{19,3},{4,20},{20... | collective-permute-start | bytes 506888 | tf_op jit(solution)/shard_map/ppermute | solution.py:374
  4.0 1.0 %constant_dynamic-slice_fusion.own = bf16[10,3,2,1408]{3,2,1,0:T(2,128)(2,1)S(1)} fusion(bf16[10,12,2,1408]{3,2,1,0:T(2,128)(2,1)} %bitcast.4, s32[]{:T(128)S(6)} %select_n.7), kind=kLoop, calls=%fused_computation.1 | loop fusion | bytes 337924 | tf_op jit(solution)/shard_map/dynamic_slice | solution.py:369
  5.1 1.1 %slice.6.refs_0_ = bf16[8,6,2,1408]{3,2,1,0:T(2,128)(2,1)S(1)} slice(bf16[10,12,2,1408]{3,2,1,0:T(2,128)(2,1)} %bitcast.5), slice={[0:8], [3:9], [0:2], [0:1408]} | slice | bytes 540672 | tf_op jit(solution)/shard_map/slice | solution.py:371
  6.2 0.9 %slice.7.refs_1_ = bf16[2,6,2,1408]{3,2,1,0:T(2,128)(2,1)S(1)} slice(bf16[10,12,2,1408]{3,2,1,0:T(2,128)(2,1)} %bitcast.6), slice={[8:10], [3:9], [0:2], [0:1408]} | slice | bytes 135168 | tf_op jit(solution)/shard_map/slice | solution.py:371
  7.2 0.1 collective-permute-start
  7.3 2.0 %collective-permute-start.1 = (bf16[2,6,2,1408]{3,2,1,0:T(2,128)(2,1)S(1)}, bf16[2,6,2,1408]{3,2,1,0:T(2,128)(2,1)S(1)}, u32[]{:S(2)}, u32[]{:S(2)}) collective-permute-start(bf16[2,6,2,1408]{3,2,1,0:T(2,128)(2,1)S(1)} %slice.7.refs_1_), channel_id=1, source_target_pairs={{0,16},{16,0},{1,17},{17,1},{2,18},{18,2},{3,19},{19,3},{4,20},{20... | collective-permute-start | bytes 202760 | tf_op jit(solution)/shard_map/ppermute | solution.py:376
  9.3 0.1 collective-permute-start.4
  9.3 0.0 collective-permute-done.2.other
  9.3 1.7 %far_pairs.1.far = f32[63,8,128]{2,1,0:T(8,128)S(1)} custom-call(bf16[10,3,2,1408]{3,2,1,0:T(2,128)(2,1)S(1)} %dynamic-slice_bitcast_fusion.own, bf16[10,3,2,1408]{3,2,1,0:T(2,128)(2,1)S(1)} %collective-permute-done.2.other), custom_call_target="tpu_custom_call" | custom-call | flops 15000000 | bytes 595968 | tf_op jit(solution)/shard_map/far_pairs/pallas_call | solution.py:332
  11.0 0.7 %collective-permute-start.5 = (f32[63,8,128]{2,1,0:T(8,128)S(1)}, f32[63,8,128]{2,1,0:T(8,128)S(1)}, u32[]{:S(2)}, u32[]{:S(2)}) collective-permute-start(f32[63,8,128]{2,1,0:T(8,128)S(1)} %far_pairs.1.far), channel_id=1, source_target_pairs={{1,2},{2,1},{3,4},{4,3},{5,6},{6,5},{7,8},{8,7},{9,10},{10,9},{11,... | collective-permute-start | bytes 774152 | tf_op jit(solution)/shard_map/ppermute | solution.py:380
  11.7 1.8 %own_mid.1 = (f32[12,2,33,8,128]{4,3,2,1,0:T(8,128)S(1)}, f32[21,32,128]{2,1,0:T(8,128)S(1)}) custom-call(bf16[8,6,2,1408]{3,2,1,0:T(2,128)(2,1)S(1)} %slice.6.refs_0_, bf16[2,6,2,1408]{3,2,1,0:T(2,128)(2,1)S(1)} %slice.7.refs_1_), custom_call_target="tpu_custom_call" | custom-call | flops 15000000 | bytes 3926016 | tf_op jit(solution)/shard_map/own_mid/pallas_call | solution.py:332
  13.5 2.4 %collective-permute-done.1.mid = bf16[2,6,2,1408]{3,2,1,0:T(2,128)(2,1)S(1)} collective-permute-done((bf16[2,6,2,1408]{3,2,1,0:T(2,128)(2,1)S(1)}, bf16[2,6,2,1408]{3,2,1,0:T(2,128)(2,1)S(1)}, u32[]{:S(2)}, u32[]{:S(2)}) %collective-permute-start.1) | collective-permute-done | bytes 67616 | tf_op jit(solution)/shard_map/ppermute | solution.py:376
  15.9 0.0 collective-permute-done.other
  15.9 1.8 %near_pairs.1 = (f32[63,8,128]{2,1,0:T(8,128)S(1)}, f32[11,64,128]{2,1,0:T(8,128)S(1)}) custom-call(bf16[10,3,2,1408]{3,2,1,0:T(2,128)(2,1)S(1)} %constant_dynamic-slice_fusion.own, bf16[10,3,2,1408]{3,2,1,0:T(2,128)(2,1)S(1)} %collective-permute-done.other, f32[63,8,128]{2,1,0:T(8,128)S(1)} %far_pairs.1.far, f32[21,32,128]{2,1,0:T(8,128)S(1)} %get-tuple-element.33.mids.before), custom_call_target="tpu_custom_call" | custom-call | flops 15000000 | bytes 1558528 | tf_op jit(solution)/shard_map/near_pairs/pallas_call | solution.py:332
  17.8 1.0 %collective-permute-start.3 = (f32[63,8,128]{2,1,0:T(8,128)S(1)}, f32[63,8,128]{2,1,0:T(8,128)S(1)}, u32[]{:S(2)}, u32[]{:S(2)}) collective-permute-start(f32[63,8,128]{2,1,0:T(8,128)S(1)} %get-tuple-element.34.near), channel_id=1, source_target_pairs={{0,1},{1,0},{2,3},{3,2},{4,5},{5,4},{6,7},{7,6},{8,9},{9,8},{10,11... | collective-permute-start | bytes 774152 | tf_op jit(solution)/shard_map/ppermute | solution.py:388
  18.8 0.8 %cross_mid.2.before = f32[21,48,128]{2,1,0:T(8,128)S(1)} custom-call(f32[12,2,33,8,128]{4,3,2,1,0:T(8,128)S(1)} %get-tuple-element.35.rep, bf16[2,6,2,1408]{3,2,1,0:T(2,128)(2,1)S(1)} %collective-permute-done.1.mid, f32[21,32,128]{2,1,0:T(8,128)S(1)} %get-tuple-element.33.mids.before, f32[63,8,128]{2,1,0:T(8,128)S(1)} %get-tuple-element.34.near, ...), custom_call_target="tpu_custom_call" | custom-call | flops 15000000 | bytes 4687872 | tf_op jit(solution)/shard_map/cross_mid/pallas_call | solution.py:332
  19.5 0.7 %collective-permute-done.4.mid = bf16[8,6,2,1408]{3,2,1,0:T(2,128)(2,1)S(1)} collective-permute-done((bf16[8,6,2,1408]{3,2,1,0:T(2,128)(2,1)S(1)}, bf16[8,6,2,1408]{3,2,1,0:T(2,128)(2,1)S(1)}, u32[]{:S(2)}, u32[]{:S(2)}) %collective-permute-start.4) | collective-permute-done | bytes 270368 | tf_op jit(solution)/shard_map/ppermute | solution.py:376
  20.3 1.6 %cross_mid.3 = (f32[21,48,128]{2,1,0:T(8,128)S(1)}, f32[11,64,128]{2,1,0:T(8,128)S(1)}, f32[11,64,128]{2,1,0:T(8,128)S(1)}) custom-call(f32[12,2,33,8,128]{4,3,2,1,0:T(8,128)S(1)} %get-tuple-element.35.rep, bf16[8,6,2,1408]{3,2,1,0:T(2,128)(2,1)S(1)} %collective-permute-done.4.mid, f32[21,48,128]{2,1,0:T(8,128)S(1)} %cross_mid.2.before, ...), custom_call_target="tpu_custom_call" | custom-call | flops 15000000 | bytes 5783552 | tf_op jit(solution)/shard_map/cross_mid/pallas_call | solution.py:332
  21.8 0.0 collective-permute-done.5.far_halo
  21.8 0.2 %far_end.1 = f32[11,192,128]{2,1,0:T(8,128)S(1)} custom-call(f32[63,8,128]{2,1,0:T(8,128)S(1)} %collective-permute-done.5.far_halo, f32[63,8,128]{2,1,0:T(8,128)S(1)} %far_pairs.1.far, f32[21,48,128]{2,1,0:T(8,128)S(1)} %get-tuple-element.37.mids.refs_3_), custom_call_target="tpu_custom_call" | custom-call | flops 15000000 | bytes 2113536 | tf_op jit(solution)/shard_map/far_end/pallas_call | solution.py:332
  22.1 0.0 collective-permute-done.3.near_halo
  22.1 1.2 %finish.1 = f32[10,20,8,128]{3,2,1,0:T(8,128)} custom-call(f32[63,8,128]{2,1,0:T(8,128)S(1)} %collective-permute-done.3.near_halo, f32[63,8,128]{2,1,0:T(8,128)S(1)} %get-tuple-element.34.near, f32[21,48,128]{2,1,0:T(8,128)S(1)} %get-tuple-element.37.mids.refs_3_, f32[11,192,128]{2,1,0:T(8,128)S(1)} %far_end.1, ...), custom_call_target="tpu_custom_call" | custom-call | flops 5000000 | bytes 4530176 | tf_op jit(solution)/shard_map/finish/pallas_call | solution.py:332
Async XLA Ops:
  1.0 8.3 %collective-permute-start.2 = (bf16[10,3,2,1408]{3,2,1,0:T(2,128)(2,1)S(1)}, bf16[10,3,2,1408]{3,2,1,0:T(2,128)(2,1)S(1)}, u32[]{:S(2)}, u32[]{:S(2)}) collective-permute-start(bf16[10,3,2,1408]{3,2,1,0:T(2,128)(2,1)S(1)} %dynamic-slice_bitcast_fusion.own), channel_id=1, source_target_pairs={{0,16},{16,0},{1,17},{17,1},{2,18},{18,2},{3,19},{19,3},{4,20},{20... | collective-permute-start | bytes 506888 | tf_op jit(solution)/shard_map/ppermute | solution.py:374
  7.2 8.8 %collective-permute-start = (bf16[10,3,2,1408]{3,2,1,0:T(2,128)(2,1)S(1)}, bf16[10,3,2,1408]{3,2,1,0:T(2,128)(2,1)S(1)}, u32[]{:S(2)}, u32[]{:S(2)}) collective-permute-start(bf16[10,3,2,1408]{3,2,1,0:T(2,128)(2,1)S(1)} %constant_dynamic-slice_fusion.own), channel_id=1, source_target_pairs={{0,16},{16,0},{1,17},{17,1},{2,18},{18,2},{3,19},{19,3},{4,20},{20... | collective-permute-start | bytes 506888 | tf_op jit(solution)/shard_map/ppermute | solution.py:375
  7.3 8.7 %collective-permute-start.1 = (bf16[2,6,2,1408]{3,2,1,0:T(2,128)(2,1)S(1)}, bf16[2,6,2,1408]{3,2,1,0:T(2,128)(2,1)S(1)}, u32[]{:S(2)}, u32[]{:S(2)}) collective-permute-start(bf16[2,6,2,1408]{3,2,1,0:T(2,128)(2,1)S(1)} %slice.7.refs_1_), channel_id=1, source_target_pairs={{0,16},{16,0},{1,17},{17,1},{2,18},{18,2},{3,19},{19,3},{4,20},{20... | collective-permute-start | bytes 202760 | tf_op jit(solution)/shard_map/ppermute | solution.py:376
  9.3 11.0 %collective-permute-start.4 = (bf16[8,6,2,1408]{3,2,1,0:T(2,128)(2,1)S(1)}, bf16[8,6,2,1408]{3,2,1,0:T(2,128)(2,1)S(1)}, u32[]{:S(2)}, u32[]{:S(2)}) collective-permute-start(bf16[8,6,2,1408]{3,2,1,0:T(2,128)(2,1)S(1)} %slice.6.refs_0_), channel_id=1, source_target_pairs={{0,16},{16,0},{1,17},{17,1},{2,18},{18,2},{3,19},{19,3},{4,20},{20... | collective-permute-start | bytes 811016 | tf_op jit(solution)/shard_map/ppermute | solution.py:376
  11.0 10.8 %collective-permute-start.5 = (f32[63,8,128]{2,1,0:T(8,128)S(1)}, f32[63,8,128]{2,1,0:T(8,128)S(1)}, u32[]{:S(2)}, u32[]{:S(2)}) collective-permute-start(f32[63,8,128]{2,1,0:T(8,128)S(1)} %far_pairs.1.far), channel_id=1, source_target_pairs={{1,2},{2,1},{3,4},{4,3},{5,6},{6,5},{7,8},{8,7},{9,10},{10,9},{11,... | collective-permute-start | bytes 774152 | tf_op jit(solution)/shard_map/ppermute | solution.py:380
  17.8 4.3 %collective-permute-start.3 = (f32[63,8,128]{2,1,0:T(8,128)S(1)}, f32[63,8,128]{2,1,0:T(8,128)S(1)}, u32[]{:S(2)}, u32[]{:S(2)}) collective-permute-start(f32[63,8,128]{2,1,0:T(8,128)S(1)} %get-tuple-element.34.near), channel_id=1, source_target_pairs={{0,1},{1,0},{2,3},{3,2},{4,5},{5,4},{6,7},{7,6},{8,9},{9,8},{10,11... | collective-permute-start | bytes 774152 | tf_op jit(solution)/shard_map/ppermute | solution.py:388

commit v12 on v10

--- a/solution.py
+++ b/solution.py
@@ -320,6 +320,26 @@
     for b in range(dates // 2):
         for copy in copies(b):
             copy.wait()
+
+
+def far_rows_kernel(x, far, sem):
+    odd = lax.rem(lax.axis_index("strip"), 2)
+    copy = pltpu.make_async_copy(x.at[:, pl.ds(odd * (x.shape[1] - 3), 3)], far, sem)
+    copy.start()
+    copy.wait()
+
+
+def other_rows_kernel(x, far, near, mid, sem):
+    rows = x.shape[1]
+    odd = lax.rem(lax.axis_index("strip"), 2)
+    copies = [
+        pltpu.make_async_copy(x.at[:, pl.ds((1 - odd) * (rows - 3), 3)], near, sem.at[0]),
+        pltpu.make_async_copy(x.at[:, 3 : rows - 3], mid, sem.at[1]),
+    ]
+    for copy in copies:
+        copy.start()
+    for copy in copies:
+        copy.wait()
 
 
 def call(kernel, name, args, outs, scratch=(), flops=0, limit=32, hbm=False, aliases=None):
@@ -363,13 +383,30 @@
         return call(functools.partial(kernel, dates, *fixed), name, args, outs, scratch, flops=15_000_000)
 
     x = jnp.transpose(slc, (0, 2, 1, 3))
-    odd = lax.rem(lax.axis_index("strip"), 2)
-    far = lax.dynamic_slice_in_dim(x, odd * (rows - 3), 3, 1)
-    x, far = lax.optimization_barrier((x, far))
-    near = lax.dynamic_slice_in_dim(x, (1 - odd) * (rows - 3), 3, 1)
-    cuts = [0] + [] + [dates]
-    parts = [x[lo:hi, 3 : rows - 3] for lo, hi in zip(cuts, cuts[1:])]
-    near, parts = lax.optimization_barrier((near, parts))
+    edge = shape((dates, 3, 2, width), slc.dtype)
+    vm = pl.BlockSpec(memory_space=VMEM)
+    hbm = pl.BlockSpec(memory_space=pltpu.MemorySpace.HBM)
+    params = pltpu.CompilerParams(vmem_limit_bytes=2 << 20)
+    far = pl.pallas_call(
+        far_rows_kernel,
+        out_shape=edge,
+        in_specs=[hbm],
+        out_specs=vm,
+        scratch_shapes=[pltpu.SemaphoreType.DMA],
+        compiler_params=params,
+        name="far_rows",
+    )(x)
+    near, mid = pl.pallas_call(
+        other_rows_kernel,
+        out_shape=(edge, shape((dates, rows - 6, 2, width), slc.dtype)),
+        in_specs=[hbm, vm],
+        out_specs=(vm, vm),
+        scratch_shapes=[pltpu.SemaphoreType.DMA((2,))],
+        compiler_params=params,
+        name="other_rows",
+    )(x, far)
+    parts = [mid]
+    cuts = [0, dates]
     rings = [[(i, (i + t) % count) for i in range(count)] for t in range(1, count)]
     fars = [lax.ppermute(far, "date", ring) for ring in rings]
     nears = [lax.ppermute(near, "date", ring) for ring in rings]

time: 23.1 us -> 23 us (level)
  local copies, waits for them, and re-layouts: 3.29 us -> 1.09 us
  starting transfers between devices: 7.9 us -> 9.27 us
  waiting for transfers between devices: 2.84 us -> 3.48 us
    ppermute x1, waiting for transfers between devices: 0.36 us -> 2.97 us  [per_device(): fars = [lax.ppermute(far, 'date', ring) for ring in rings]]
    dynamic_slice x2 -> x0, local copies, waits for them, and re-layouts: 2.07 us -> none  [the longest x1 1.04 us: per_device(): far = lax.dynamic_slice_in_dim(x, odd * (rows - 3), 3, 1)]
    ppermute x1, starting transfers between devices: 2.13 us -> 3.5 us  [per_device(): near_halo = lax.ppermute(near_sums, 'strip', chip)]
    ppermute x1, waiting for transfers between devices: 1.79 us -> 0.5 us  [per_device(): lax.ppermute(part, 'date', ring)]
    slice x1 -> x0, local copies, waits for them, and re-layouts: 1.22 us -> none  [per_device(): parts = [x[lo:hi, 3:rows - 3] for lo, hi in zip(cuts, cuts[1:])]]
    unnamed x0 -> x2, local copies, waits for them, and re-layouts: none -> 1.09 us
    ppermute x1, waiting for transfers between devices: 0.67 us -> 0.01 us  [per_device(): nears = [lax.ppermute(near, 'date', ring) for ring in rings]]
  transfers between devices with their start and end apart: 5 -> 5, of which waited for: 3 -> 2; matrix products, arithmetic and copies ran while one was open for 10% -> 0% of each run, Pallas kernels for 33% -> 34%
where the time goes in v12:
time: 23 us; the launch traced here: 22.8 us
  starting transfers between devices  9.27 us (40%)
  Pallas kernels  8.9 us (39%)
  waiting for transfers between devices  3.48 us (15%)
  local copies, waits for them, and re-layouts  1.09 us (5%)
    pallas_call x6, Pallas kernels, call(): pl.pallas_call(kernel, out_shape=tuple(outs), in_specs=ins, out_specs=(fa...  8.8 us
    ppermute x1, starting transfers between devices, per_device(): near_halo = lax.ppermute(near_sums, 'strip', chip)  3.5 us
    ppermute x1, starting transfers between devices, per_device(): fars = [lax.ppermute(far, 'date', ring) for ring in rings]  3 us
    ppermute x1, waiting for transfers between devices, per_device(): fars = [lax.ppermute(far, 'date', ring) for ring in rings]  2.97 us
    ppermute x1, starting transfers between devices, per_device(): lax.ppermute(part, 'date', ring)  2 us
    unnamed x2, local copies, waits for them, and re-layouts  1.09 us
    ppermute x1, starting transfers between devices, per_device(): far_halo = lax.ppermute(far_sums, 'strip', chips)  0.68 us
    ppermute x1, waiting for transfers between devices, per_device(): lax.ppermute(part, 'date', ring)  0.5 us
  transfers between devices with their start and end apart: 5, of which 2 were waited for; matrix products, arithmetic and copies ran while one was open for 0% of the time, Pallas kernels for 34%

profile of v12, /device:TPU:0, one launch (start us, length us, event | category | flops | bytes accessed | tf_op | source)
XLA Modules:
  0.0 22.8 jit_solution(1675201058392043840)
XLA Ops:
  0.0 0.0 copy-start
  0.0 1.1 %copy-done = bf16[10,2,12,1408]{3,1,2,0:T(2,128)(2,1)S(1)} copy-done((bf16[10,2,12,1408]{3,1,2,0:T(2,128)(2,1)S(1)}, bf16[10,2,12,1408]{3,1,2,0:T(2,128)(2,1)}, u32[]{:S(2)}) %copy-start) | copy-done | bytes 675864
  1.1 3.0 %collective-permute-start.1 = (bf16[10,3,2,1408]{3,2,1,0:T(2,128)(2,1)S(1)}, bf16[10,3,2,1408]{3,2,1,0:T(2,128)(2,1)S(1)}, u32[]{:S(2)}, u32[]{:S(2)}) collective-permute-start(bf16[10,3,2,1408]{3,2,1,0:T(2,128)(2,1)S(1)} %far_rows.1.far.own), channel_id=1, source_target_pairs={{0,16},{16,0},{1,17},{17,1},{2,18},{18,2},{3,19},{19,3},{4,20},{20... | collective-permute-start | bytes 506888 | tf_op jit(solution)/shard_map/ppermute | solution.py:411
  4.1 0.1 other_rows.1
  4.2 0.1 collective-permute-start
  4.3 2.0 %collective-permute-start.3 = (bf16[10,6,2,1408]{3,2,1,0:T(2,128)(2,1)S(1)}, bf16[10,6,2,1408]{3,2,1,0:T(2,128)(2,1)S(1)}, u32[]{:S(2)}, u32[]{:S(2)}) collective-permute-start(bf16[10,6,2,1408]{3,2,1,0:T(2,128)(2,1)S(1)} %get-tuple-element.20.refs_0_), channel_id=1, source_target_pairs={{0,16},{16,0},{1,17},{17,1},{2,18},{18,2},{3,19},{19,3},{4,20},{20... | collective-permute-start | bytes 1013768 | tf_op jit(solution)/shard_map/ppermute | solution.py:413
  6.3 3.0 %collective-permute-done.1.other = bf16[10,3,2,1408]{3,2,1,0:T(2,128)(2,1)S(1)} collective-permute-done((bf16[10,3,2,1408]{3,2,1,0:T(2,128)(2,1)S(1)}, bf16[10,3,2,1408]{3,2,1,0:T(2,128)(2,1)S(1)}, u32[]{:S(2)}, u32[]{:S(2)}) %collective-permute-start.1) | collective-permute-done | bytes 168992 | tf_op jit(solution)/shard_map/ppermute | solution.py:411
  9.3 1.7 %far_pairs.1.far = f32[63,8,128]{2,1,0:T(8,128)S(1)} custom-call(bf16[10,3,2,1408]{3,2,1,0:T(2,128)(2,1)S(1)} %far_rows.1.far.own, bf16[10,3,2,1408]{3,2,1,0:T(2,128)(2,1)S(1)} %collective-permute-done.1.other), custom_call_target="tpu_custom_call" | custom-call | flops 15000000 | bytes 595968 | tf_op jit(solution)/shard_map/far_pairs/pallas_call | solution.py:352
  11.0 0.7 %collective-permute-start.4 = (f32[63,8,128]{2,1,0:T(8,128)S(1)}, f32[63,8,128]{2,1,0:T(8,128)S(1)}, u32[]{:S(2)}, u32[]{:S(2)}) collective-permute-start(f32[63,8,128]{2,1,0:T(8,128)S(1)} %far_pairs.1.far), channel_id=1, source_target_pairs={{1,2},{2,1},{3,4},{4,3},{5,6},{6,5},{7,8},{8,7},{9,10},{10,9},{11,... | collective-permute-start | bytes 774152 | tf_op jit(solution)/shard_map/ppermute | solution.py:417
  11.6 1.8 %own_mid.1 = (f32[12,2,33,8,128]{4,3,2,1,0:T(8,128)S(1)}, f32[21,32,128]{2,1,0:T(8,128)S(1)}) custom-call(bf16[10,6,2,1408]{3,2,1,0:T(2,128)(2,1)S(1)} %get-tuple-element.20.refs_0_), custom_call_target="tpu_custom_call" | custom-call | flops 15000000 | bytes 3926016 | tf_op jit(solution)/shard_map/own_mid/pallas_call | solution.py:352
  13.4 0.0 collective-permute-done.other
  13.5 1.8 %near_pairs.1 = (f32[63,8,128]{2,1,0:T(8,128)S(1)}, f32[11,64,128]{2,1,0:T(8,128)S(1)}) custom-call(bf16[10,3,2,1408]{3,2,1,0:T(2,128)(2,1)S(1)} %get-tuple-element.18.own, bf16[10,3,2,1408]{3,2,1,0:T(2,128)(2,1)S(1)} %collective-permute-done.other, f32[63,8,128]{2,1,0:T(8,128)S(1)} %far_pairs.1.far, f32[21,32,128]{2,1,0:T(8,128)S(1)} %get-tuple-element.24.mids.before), custom_call_target="tpu_custom_call" | custom-call | flops 15000000 | bytes 1558528 | tf_op jit(solution)/shard_map/near_pairs/pallas_call | solution.py:352
  15.3 3.5 %collective-permute-start.2 = (f32[63,8,128]{2,1,0:T(8,128)S(1)}, f32[63,8,128]{2,1,0:T(8,128)S(1)}, u32[]{:S(2)}, u32[]{:S(2)}) collective-permute-start(f32[63,8,128]{2,1,0:T(8,128)S(1)} %get-tuple-element.25.near), channel_id=1, source_target_pairs={{0,1},{1,0},{2,3},{3,2},{4,5},{5,4},{6,7},{7,6},{8,9},{9,8},{10,11... | collective-permute-start | bytes 774152 | tf_op jit(solution)/shard_map/ppermute | solution.py:424
  18.8 0.5 %collective-permute-done.3.mid = bf16[10,6,2,1408]{3,2,1,0:T(2,128)(2,1)S(1)} collective-permute-done((bf16[10,6,2,1408]{3,2,1,0:T(2,128)(2,1)S(1)}, bf16[10,6,2,1408]{3,2,1,0:T(2,128)(2,1)S(1)}, u32[]{:S(2)}, u32[]{:S(2)}) %collective-permute-start.3) | collective-permute-done | bytes 337952 | tf_op jit(solution)/shard_map/ppermute | solution.py:413
  19.3 2.1 %cross_mid.1 = (f32[21,48,128]{2,1,0:T(8,128)S(1)}, f32[11,64,128]{2,1,0:T(8,128)S(1)}, f32[11,64,128]{2,1,0:T(8,128)S(1)}) custom-call(f32[12,2,33,8,128]{4,3,2,1,0:T(8,128)S(1)} %get-tuple-element.26.rep, bf16[10,6,2,1408]{3,2,1,0:T(2,128)(2,1)S(1)} %collective-permute-done.3.mid, f32[21,32,128]{2,1,0:T(8,128)S(1)} %get-tuple-element.24.mids.before, ...), custom_call_target="tpu_custom_call" | custom-call | flops 15000000 | bytes 5679104 | tf_op jit(solution)/shard_map/cross_mid/pallas_call | solution.py:352
  21.4 0.0 collective-permute-done.4.far_halo
  21.4 0.2 %far_end.1 = f32[11,192,128]{2,1,0:T(8,128)S(1)} custom-call(f32[63,8,128]{2,1,0:T(8,128)S(1)} %collective-permute-done.4.far_halo, f32[63,8,128]{2,1,0:T(8,128)S(1)} %far_pairs.1.far, f32[21,48,128]{2,1,0:T(8,128)S(1)} %get-tuple-element.27.mids.refs_3_), custom_call_target="tpu_custom_call" | custom-call | flops 15000000 | bytes 2113536 | tf_op jit(solution)/shard_map/far_end/pallas_call | solution.py:352
  21.6 0.0 collective-permute-done.2.near_halo
  21.6 1.2 %finish.1 = f32[10,20,8,128]{3,2,1,0:T(8,128)} custom-call(f32[63,8,128]{2,1,0:T(8,128)S(1)} %collective-permute-done.2.near_halo, f32[63,8,128]{2,1,0:T(8,128)S(1)} %get-tuple-element.25.near, f32[21,48,128]{2,1,0:T(8,128)S(1)} %get-tuple-element.27.mids.refs_3_, f32[11,192,128]{2,1,0:T(8,128)S(1)} %far_end.1, ...), custom_call_target="tpu_custom_call" | custom-call | flops 5000000 | bytes 4530176 | tf_op jit(solution)/shard_map/finish/pallas_call | solution.py:352
  (1 shorter events, 0.0 us)
Async XLA Ops:
  0.0 1.1 %copy-start = (bf16[10,2,12,1408]{3,1,2,0:T(2,128)(2,1)S(1)}, bf16[10,2,12,1408]{3,1,2,0:T(2,128)(2,1)}, u32[]{:S(2)}) copy-start(bf16[10,2,12,1408]{3,1,2,0:T(2,128)(2,1)} %param.1) | copy-start | bytes 2027524
  1.1 8.1 %collective-permute-start.1 = (bf16[10,3,2,1408]{3,2,1,0:T(2,128)(2,1)S(1)}, bf16[10,3,2,1408]{3,2,1,0:T(2,128)(2,1)S(1)}, u32[]{:S(2)}, u32[]{:S(2)}) collective-permute-start(bf16[10,3,2,1408]{3,2,1,0:T(2,128)(2,1)S(1)} %far_rows.1.far.own), channel_id=1, source_target_pairs={{0,16},{16,0},{1,17},{17,1},{2,18},{18,2},{3,19},{19,3},{4,20},{20... | collective-permute-start | bytes 506888 | tf_op jit(solution)/shard_map/ppermute | solution.py:411
  4.2 9.2 %collective-permute-start = (bf16[10,3,2,1408]{3,2,1,0:T(2,128)(2,1)S(1)}, bf16[10,3,2,1408]{3,2,1,0:T(2,128)(2,1)S(1)}, u32[]{:S(2)}, u32[]{:S(2)}) collective-permute-start(bf16[10,3,2,1408]{3,2,1,0:T(2,128)(2,1)S(1)} %get-tuple-element.18.own), channel_id=1, source_target_pairs={{0,16},{16,0},{1,17},{17,1},{2,18},{18,2},{3,19},{19,3},{4,20},{20... | collective-permute-start | bytes 506888 | tf_op jit(solution)/shard_map/ppermute | solution.py:412
  4.3 15.0 %collective-permute-start.3 = (bf16[10,6,2,1408]{3,2,1,0:T(2,128)(2,1)S(1)}, bf16[10,6,2,1408]{3,2,1,0:T(2,128)(2,1)S(1)}, u32[]{:S(2)}, u32[]{:S(2)}) collective-permute-start(bf16[10,6,2,1408]{3,2,1,0:T(2,128)(2,1)S(1)} %get-tuple-element.20.refs_0_), channel_id=1, source_target_pairs={{0,16},{16,0},{1,17},{17,1},{2,18},{18,2},{3,19},{19,3},{4,20},{20... | collective-permute-start | bytes 1013768 | tf_op jit(solution)/shard_map/ppermute | solution.py:413
  11.0 10.4 %collective-permute-start.4 = (f32[63,8,128]{2,1,0:T(8,128)S(1)}, f32[63,8,128]{2,1,0:T(8,128)S(1)}, u32[]{:S(2)}, u32[]{:S(2)}) collective-permute-start(f32[63,8,128]{2,1,0:T(8,128)S(1)} %far_pairs.1.far), channel_id=1, source_target_pairs={{1,2},{2,1},{3,4},{4,3},{5,6},{6,5},{7,8},{8,7},{9,10},{10,9},{11,... | collective-permute-start | bytes 774152 | tf_op jit(solution)/shard_map/ppermute | solution.py:417
  15.3 6.3 %collective-permute-start.2 = (f32[63,8,128]{2,1,0:T(8,128)S(1)}, f32[63,8,128]{2,1,0:T(8,128)S(1)}, u32[]{:S(2)}, u32[]{:S(2)}) collective-permute-start(f32[63,8,128]{2,1,0:T(8,128)S(1)} %get-tuple-element.25.near), channel_id=1, source_target_pairs={{0,1},{1,0},{2,3},{3,2},{4,5},{5,4},{6,7},{7,6},{8,9},{9,8},{10,11... | collective-permute-start | bytes 774152 | tf_op jit(solution)/shard_map/ppermute | solution.py:424
